TPU v7x, 128 devices: a whole 4x4x4 slice. The times are simulated.
128 devices in a mesh: gx: 16 (over y, x), gy: 8 (over z, core).
Axes of the slice: x: 4, y: 4, z: 4, core: 2. Of those that a mesh axis runs over, the one named last changes fastest.
Arguments:
- prior_member_matrix: float32 [8, 256, 256, 128], P(None, 'gx', 'gy'), may hold values from -6 to 6
- east_speed: float32 [4, 256, 256], P(None, 'gx', 'gy'), may hold values from -0.3 to 0.3
- north_speed: float32 [4, 256, 256], P(None, 'gx', 'gy'), may hold values from -0.3 to 0.3
- diffusion: float32 [4, 256, 256], P(None, 'gx', 'gy'), may hold values from 0.1 to 0.22
- obs_column: int32 [1024, 2], replicated, may hold values from 0 to 255, as said below
- obs_comp: int32 [1024], replicated, may hold values from 0 to 7
- observation_reach: int32 [1024], replicated, may hold values from 0 to 3
- obs_owner: int32 [1024], replicated, may hold values from 0 to 15, as said below
- obs_order: int32 [1024], replicated, may hold values from 0 to 1023, each once
- obs_value: float32 [16, 8, 32], P('gx', 'gy'), may hold values from -6 to 6
- obs_error: float32 [16, 8, 32], P('gx', 'gy'), may hold values from 0.3 to 3
Outputs:
- analysis: float32 [8, 256, 256, 128], P(None, 'gx', 'gy')
Inputs may be any that keep to these rules, and one draw needn't show every extreme that they name: `obs_column`: tile t = (8 tx + ty) holds observations 8 t to 8 (t + 1) - 1; each entry is a (longitude, latitude) column inside that tile. `obs_owner`: the owner lies in the observation's latitude tile; one tile's observations reach one owner at most 2 times, and exactly 2 times for some owner of every tile.
All inputs are finite; a program needn't handle non-finite values.
Results may differ from a plain program's by a relative error of at most 0.0001.
Values sent between devices are 32-bit elements; how exact they have to be, the bound alone decides.
No kernel may reach another device: no remote copies, remote signals or barrier semaphores. Data moves between devices by JAX's collectives and lax.ppermute only.
A program may use at most 64 MiB of HBM per device.

v0:
```python
import jax
import jax.numpy as jnp
from jax import lax
from jax.sharding import PartitionSpec as P

FSTEPS = 2
PANEL = 256


PRECISE = lax.Precision.HIGHEST


def with_halo(cells, sides, width, closed):
    for axis, dim in sides:
        count = lax.axis_size(axis)
        ends = count if closed else count - 1
        head = lax.slice_in_dim(cells, 0, width, axis=dim)
        tail = lax.slice_in_dim(cells, cells.shape[dim] - width, cells.shape[dim], axis=dim)
        cells = jnp.concatenate(
            [
                lax.ppermute(tail, axis, [(i, (i + 1) % count) for i in range(ends)]),
                cells,
                lax.ppermute(head, axis, [((i + 1) % count, i) for i in range(ends)]),
            ],
            axis=dim,
        )
    return cells


def slot_rank(tile_x, tile_y, owner, tiles_x, tiles_y):
    total_obs = owner.shape[0]
    keyed = (tile_x * tiles_y + tile_y) * tiles_x + owner
    sort_order = jnp.argsort(keyed, stable=True)
    sorted_keys = keyed[sort_order]
    places = jnp.arange(total_obs, dtype=jnp.int32)
    segment_beginning = jnp.concatenate(
        [jnp.ones((1,), dtype=bool), sorted_keys[1:] != sorted_keys[:-1]]
    )
    starts = lax.cummax(jnp.where(segment_beginning, places, 0), axis=0)
    ranked = places - starts
    inverse_order = jnp.argsort(sort_order)
    return ranked[inverse_order]


def horizontal(first_x, first_y, second_x, second_y, span_x, span_y, total_x):
    wrapped = (first_x - second_x) % total_x
    dist_x = jnp.minimum(wrapped, total_x - wrapped).astype(jnp.float32)
    dist_y = (first_y - second_y).astype(jnp.float32)
    radius_sq = (dist_x / span_x) ** 2 + (dist_y / span_y) ** 2
    return jnp.maximum(0.0, 1.0 - radius_sq) ** 2


def vertical(first_level, second_level, reach):
    level_gap = jnp.abs(first_level - second_level).astype(jnp.float32)
    return jnp.maximum(0.0, 1.0 - level_gap / (reach.astype(jnp.float32) + 1.0))


def panel_terms(priors, values, errors):
    members = priors.shape[1]
    centre = jnp.mean(priors, axis=1)
    spread = priors - centre[:, None]
    variance = jnp.sum(spread * spread, axis=1) / (members - 1)
    inverse = 1.0 / (variance + errors)
    damping = 1.0 / (1.0 + jnp.sqrt(errors * inverse))
    return (spread, (values - centre) * inverse, damping * inverse)


def regress(row_block, weight, spread, mean_gain, shrink):
    members = row_block.shape[1]
    centre = jnp.mean(row_block, axis=1, keepdims=True)
    anomaly = row_block - centre
    covariance = jnp.dot(
        anomaly, spread.T, precision=PRECISE, preferred_element_type=jnp.float32
    ) / (members - 1)
    weighted = weight * covariance
    centre = centre + jnp.dot(
        weighted, mean_gain[:, None], precision=PRECISE, preferred_element_type=jnp.float32
    )
    anomaly = anomaly - jnp.dot(
        weighted * shrink[None, :], spread, precision=PRECISE, preferred_element_type=jnp.float32
    )
    return centre + anomaly


def shards(
    prior_member_matrix,
    east_speed,
    north_speed,
    diffusion,
    obs_column,
    obs_comp,
    observation_reach,
    obs_owner,
    obs_order,
    obs_value,
    obs_error,
):
    comps, zonal_extent, width_y, members = prior_member_matrix.shape
    per_level = comps // east_speed.shape[0]
    tiles_x = lax.axis_size("gx")
    tiles_y = lax.axis_size("gy")
    here_x = lax.axis_index("gx")
    here_y = lax.axis_index("gy")
    east_vel = jnp.repeat(east_speed, per_level, axis=0)[..., None]
    north_vel = jnp.repeat(north_speed, per_level, axis=0)[..., None]
    diff_coef = jnp.repeat(diffusion, per_level, axis=0)[..., None]
    model_mesh_values = prior_member_matrix
    for substep in range(FSTEPS):
        rim_wide = with_halo(model_mesh_values, (("gx", 1),), 1, True)
        rim_tall = with_halo(model_mesh_values, (("gy", 2),), 1, False)
        east_side = rim_wide[:, 2:]
        west_side = rim_wide[:, :-2]
        north_side = rim_tall[:, :, 2:]
        south_side = rim_tall[:, :, :-2]
        spread_term = diff_coef * (
            east_side + west_side + north_side + south_side - 4.0 * model_mesh_values
        )
        carry_term = 0.5 * (
            east_vel * (east_side - west_side) + north_vel * (north_side - south_side)
        )
        model_mesh_values = model_mesh_values + spread_term - carry_term
    row_state = model_mesh_values.reshape(comps * zonal_extent * width_y, members)
    obs_total = obs_comp.shape[0]
    slot_count = obs_value.shape[2]
    capacity = slot_count // tiles_x
    panel_count = obs_total // PANEL
    col_x = obs_column[:, 0]
    col_y = obs_column[:, 1]
    tile_x = col_x // zonal_extent
    tile_y = col_y // width_y
    ranked_slot = slot_rank(tile_x, tile_y, obs_owner, tiles_x, tiles_y)
    obs_level = obs_comp // per_level
    in_tile = (tile_x == here_x) & (tile_y == here_y)
    held_here = (obs_owner == here_x) & (tile_y == here_y)
    own_place = tile_x * capacity + ranked_slot
    element = (
        (obs_comp * zonal_extent + col_x - tile_x * zonal_extent) * width_y
        + col_y
        - tile_y * width_y
    )
    total_x = zonal_extent * tiles_x
    grid_x = jnp.repeat(here_x * zonal_extent + jnp.arange(zonal_extent, dtype=jnp.int32), width_y)
    grid_y = jnp.tile(here_y * width_y + jnp.arange(width_y, dtype=jnp.int32), zonal_extent)
    comp_level = jnp.arange(comps, dtype=jnp.int32) // per_level
    local_vals = obs_value.reshape(slot_count)
    local_errs = obs_error.reshape(slot_count)

    def state_weight(panel_index_list):
        flat_weight = horizontal(
            grid_x[:, None],
            grid_y[:, None],
            col_x[panel_index_list][None, :],
            col_y[panel_index_list][None, :],
            3.0 * zonal_extent,
            3.0 * width_y,
            total_x,
        )
        level_weight = vertical(
            comp_level[:, None],
            obs_level[panel_index_list][None, :],
            observation_reach[panel_index_list][None, :],
        )
        return (level_weight[:, None, :] * flat_weight[None, :, :]).reshape(
            -1, panel_index_list.shape[0]
        )

    slot_ids = jnp.arange(slot_count, dtype=jnp.int32)
    measurement_labels = jnp.arange(obs_total, dtype=jnp.int32)
    send_place = obs_owner * capacity + ranked_slot
    send_match = in_tile[None, :] & (send_place[None, :] == slot_ids[:, None])
    filled = jnp.any(send_match, axis=1)
    source_elem = jnp.sum(jnp.where(send_match, element[None, :], 0), axis=1)
    outgoing = jnp.where(filled[:, None], row_state[source_elem], 0.0).reshape(
        tiles_x, capacity, members
    )
    arrived = lax.all_to_all(outgoing, "gx", split_axis=0, concat_axis=0, tiled=True).reshape(
        slot_count, members
    )
    hold_match = held_here[None, :] & (own_place[None, :] == slot_ids[:, None])
    held_obs = jnp.sum(jnp.where(hold_match, measurement_labels[None, :], 0), axis=1)
    slot_east_coord = col_x[held_obs]
    slot_y = col_y[held_obs]
    slot_level = obs_level[held_obs]
    all_vals, all_errs = (
        lax.all_gather(local_vals, ("gx", "gy"), axis=0, tiled=True),
        lax.all_gather(local_errs, ("gx", "gy"), axis=0, tiled=True),
    )
    global_place = (obs_owner * tiles_y + tile_y) * slot_count + own_place
    obs_vals = all_vals[global_place]
    obs_errs = all_errs[global_place]

    def one_panel(panel_num, carried):
        row_state, owner_rows = carried
        panel_index_list = lax.dynamic_slice_in_dim(obs_order, panel_num * PANEL, PANEL)
        every_slot = lax.all_gather(owner_rows, ("gx", "gy"), axis=0, tiled=True)
        priors = every_slot[global_place[panel_index_list]]
        spread, mean_gain, shrink = panel_terms(
            priors, obs_vals[panel_index_list], obs_errs[panel_index_list]
        )
        owner_weight = horizontal(
            slot_east_coord[:, None],
            slot_y[:, None],
            col_x[panel_index_list][None, :],
            col_y[panel_index_list][None, :],
            3.0 * zonal_extent,
            3.0 * width_y,
            total_x,
        )
        owner_weight = owner_weight * vertical(
            slot_level[:, None],
            obs_level[panel_index_list][None, :],
            observation_reach[panel_index_list][None, :],
        )
        new_state = regress(row_state, state_weight(panel_index_list), spread, mean_gain, shrink)
        new_owner = regress(owner_rows, owner_weight, spread, mean_gain, shrink)
        return (new_state, new_owner)

    row_state, owner_rows = lax.fori_loop(0, panel_count, one_panel, (row_state, arrived))
    return row_state.reshape(comps, zonal_extent, width_y, members)


def solution(mesh):
    return jax.shard_map(
        shards,
        mesh=mesh,
        in_specs=(
            P(None, "gx", "gy", None),
            P(None, "gx", "gy"),
            P(None, "gx", "gy"),
            P(None, "gx", "gy"),
            P(),
            P(),
            P(),
            P(),
            P(),
            P("gx", "gy", None),
            P("gx", "gy", None),
        ),
        out_specs=P(None, "gx", "gy", None),
        check_vma=False,
    )
```

profile of v0, /device:TPU:1, one launch (start us, length us, event | category | flops | bytes accessed | tf_op | source)
XLA Modules:
  0.0 494.7 jit_solution(18060016406997314425)
XLA Ops:
  7.8 3.3 collective-permute-start.2
  11.2 3.5 collective-permute-start.3
  17.0 3.8 collective-permute-start
  23.0 4.4 sort.34
  27.4 4.5 gather_fusion.8
  32.0 4.4 sort.35
  37.0 4.5 gather_fusion.9
  43.7 64.4 %all-reduce.2 = (f32[4096]{0:T(1024)S(1)}, f32[4096]{0:T(1024)S(1)}) all-reduce(f32[4096]{0:T(1024)S(1)} %bitcast_dynamic-update-slice_fusion.1, f32[4096]{0:T(1024)S(1)} %bitcast_dynamic-update-slice_fusion), channel_id=2, replica_groups=mesh['gx'=16,'gy'=8] {'gx','gy'}, use_global_device_ids=true, to_apply=%add | all-reduce | flops 8192 | bytes 65536 | tf_op jit(solution)/shard_map/all_gather | solution.py:185
  108.0 6.1 %gather_fusion.12 = f32[1024]{0:T(1024)S(1)} fusion(f32[4096]{0:T(1024)S(1)} %get-tuple-element.561, s32[1024]{0:T(1024)S(1)} %get-tuple-element.564), kind=kCustom, calls=%fused_computation.12 | custom fusion | bytes 12288 | tf_op jit(solution)/shard_map/gather | solution.py:190
  114.2 6.2 %gather_fusion.11 = f32[1024]{0:T(1024)S(1)} fusion(f32[4096]{0:T(1024)S(1)} %get-tuple-element.560, s32[1024]{0:T(1024)S(1)} %get-tuple-element.564), kind=kCustom, calls=%fused_computation.11 | custom fusion | bytes 12288 | tf_op jit(solution)/shard_map/gather | solution.py:189
  123.9 4.5 collective-permute-start.4
  128.5 3.1 collective-permute-start.6
  131.6 2.5 collective-permute-start.7
  138.8 3.5 all-to-all-start
  142.9 5.8 %all-to-all-done = f32[16,2,128]{2,1,0:T(2,128)S(1)} async-done(((f32[16,2,128]{2,1,0:T(2,128)}), f32[16,2,128]{2,1,0:T(2,128)S(1)}, u32[]{:S(2)}, u32[]{:S(2)}) %all-to-all-start) | async-done | bytes 16416 | tf_op jit(solution)/shard_map/all_to_all | solution.py:176
  148.7 338.1 %while.18 = (s32[]{:T(128)}, f32[4096,128]{1,0:T(8,128)S(1)}, f32[32,128]{1,0:T(8,128)S(1)}, s32[1024]{0:T(1024)}, s32[1024]{0:T(1024)S(1)}, /*index=5*/s32[1024...) while((s32[]{:T(128)}, f32[4096,128]{1,0:T(8,128)S(1)}, ...), condition=%wide.region_12.13_spmd.clone, body=%wide.region_7.12_spmd.clone.sunk | while | flops 3269761536 | bytes 36260832 | solution.py:218
  163.8 54.0 %all-gather.4.cloned.1.call-done = f32[4096,128]{1,0:T(8,128)} async-done(((f32[32,128]{1,0:T(8,128)}), f32[4096,128]{1,0:T(8,128)}) %all-gather.4.cloned.1.call-update) | async-done | bytes 2097168 | tf_op jit(solution)/shard_map/while/body/eval_jaxpr/all_gather | solution.py:195
  220.9 5.6 %fusion.99 = f32[4096,256]{1,0:T(8,128)S(1)} fusion(f32[4096,256]{1,0:T(8,128)} %bitcast.72, f32[4096,128]{1,0:T(8,128)S(1)} %get-tuple-element.720, f32[4096]{0:T(1024)S(1)} %broadcast_multiply_fusion.10, f32[256,128]{1,0:T(8,128)S(1)} %gather_fusion.1, f32[256]{0:T(256)S(1)} %broadcast_multiply_fusion.8), kind=kOutput, calls=%fused_computation.20.clone.1 | convolution fusion | flops 1613266944 | bytes 10634240 | tf_op jit(solution)/shard_map/while/body/eval_jaxpr/dot_general | solution.py:72
  226.5 3.6 fusion.100
  230.4 4.6 fusion.102
  250.3 51.6 %all-gather.4.cloned.1.call-done = f32[4096,128]{1,0:T(8,128)} async-done(((f32[32,128]{1,0:T(8,128)}), f32[4096,128]{1,0:T(8,128)}) %all-gather.4.cloned.1.call-update) | async-done | bytes 2097168 | tf_op jit(solution)/shard_map/while/body/eval_jaxpr/all_gather | solution.py:195
  305.0 5.6 %fusion.99 = f32[4096,256]{1,0:T(8,128)S(1)} fusion(f32[4096,256]{1,0:T(8,128)} %bitcast.72, f32[4096,128]{1,0:T(8,128)S(1)} %get-tuple-element.720, f32[4096]{0:T(1024)S(1)} %broadcast_multiply_fusion.10, f32[256,128]{1,0:T(8,128)S(1)} %gather_fusion.1, f32[256]{0:T(256)S(1)} %broadcast_multiply_fusion.8), kind=kOutput, calls=%fused_computation.20.clone.1 | convolution fusion | flops 1613266944 | bytes 10634240 | tf_op jit(solution)/shard_map/while/body/eval_jaxpr/dot_general | solution.py:72
  310.6 3.6 fusion.100
  314.5 4.6 fusion.102
  334.3 51.6 %all-gather.4.cloned.1.call-done = f32[4096,128]{1,0:T(8,128)} async-done(((f32[32,128]{1,0:T(8,128)}), f32[4096,128]{1,0:T(8,128)}) %all-gather.4.cloned.1.call-update) | async-done | bytes 2097168 | tf_op jit(solution)/shard_map/while/body/eval_jaxpr/all_gather | solution.py:195
  389.0 5.6 %fusion.99 = f32[4096,256]{1,0:T(8,128)S(1)} fusion(f32[4096,256]{1,0:T(8,128)} %bitcast.72, f32[4096,128]{1,0:T(8,128)S(1)} %get-tuple-element.720, f32[4096]{0:T(1024)S(1)} %broadcast_multiply_fusion.10, f32[256,128]{1,0:T(8,128)S(1)} %gather_fusion.1, f32[256]{0:T(256)S(1)} %broadcast_multiply_fusion.8), kind=kOutput, calls=%fused_computation.20.clone.1 | convolution fusion | flops 1613266944 | bytes 10634240 | tf_op jit(solution)/shard_map/while/body/eval_jaxpr/dot_general | solution.py:72
  394.6 3.6 fusion.100
  398.5 4.6 fusion.102
  418.2 51.4 %all-gather.4.cloned.1.call-done = f32[4096,128]{1,0:T(8,128)} async-done(((f32[32,128]{1,0:T(8,128)}), f32[4096,128]{1,0:T(8,128)}) %all-gather.4.cloned.1.call-update) | async-done | bytes 2097168 | tf_op jit(solution)/shard_map/while/body/eval_jaxpr/all_gather | solution.py:195
  472.7 5.6 %fusion.99 = f32[4096,256]{1,0:T(8,128)S(1)} fusion(f32[4096,256]{1,0:T(8,128)} %bitcast.72, f32[4096,128]{1,0:T(8,128)S(1)} %get-tuple-element.720, f32[4096]{0:T(1024)S(1)} %broadcast_multiply_fusion.10, f32[256,128]{1,0:T(8,128)S(1)} %gather_fusion.1, f32[256]{0:T(256)S(1)} %broadcast_multiply_fusion.8), kind=kOutput, calls=%fused_computation.20.clone.1 | convolution fusion | flops 1613266944 | bytes 10634240 | tf_op jit(solution)/shard_map/while/body/eval_jaxpr/dot_general | solution.py:72
  478.3 3.6 fusion.100
  482.2 4.6 fusion.102
  (226 shorter events, 92.2 us)
Async XLA Ops:
  7.8 113.3 %collective-permute-start.2 = (f32[8,16,1,128]{3,2,1,0:T(1,128)S(1)}, f32[8,16,1,128]{3,2,1,0:T(1,128)S(1)}, u32[]{:S(2)}, u32[]{:S(2)}) collective-permute-start(f32[8,16,1,128]{3,2,1,0:T(1,128)S(1)} %get-tuple-element.577), channel_id=1, source_target_pairs={{1,0},{2,1},{3,2},{4,3},{5,4},{6,5},{7,6},{9,8},{10,9},{11,10},{12... | collective-permute-start | bytes 196616 | tf_op jit(solution)/shard_map/ppermute | solution.py:23
  11.2 110.0 %collective-permute-start.3 = (f32[8,16,1,128]{3,2,1,0:T(1,128)S(1)}, f32[8,16,1,128]{3,2,1,0:T(1,128)S(1)}, u32[]{:S(2)}, u32[]{:S(2)}) collective-permute-start(f32[8,16,1,128]{3,2,1,0:T(1,128)S(1)} %get-tuple-element.578), channel_id=1, source_target_pairs={{0,1},{1,2},{2,3},{3,4},{4,5},{5,6},{6,7},{8,9},{9,10},{10,11},{11... | collective-permute-start | bytes 196616 | tf_op jit(solution)/shard_map/ppermute | solution.py:21
  15.7 105.5 %collective-permute-start.1 = (f32[8,1,32,128]{3,2,1,0:T(8,128)S(1)}, f32[8,1,32,128]{3,2,1,0:T(8,128)S(1)}, u32[]{:S(2)}, u32[]{:S(2)}) collective-permute-start(f32[8,1,32,128]{3,2,1,0:T(8,128)S(1)} %get-tuple-element.575), channel_id=1, source_target_pairs={{0,8},{8,16},{16,24},{24,32},{32,40},{40,48},{48,56},{56,64},{64,7... | collective-permute-start | bytes 393224 | tf_op jit(solution)/shard_map/ppermute | solution.py:21
  17.0 104.2 %collective-permute-start = (f32[8,1,32,128]{3,2,1,0:T(8,128)S(1)}, f32[8,1,32,128]{3,2,1,0:T(8,128)S(1)}, u32[]{:S(2)}, u32[]{:S(2)}) collective-permute-start(f32[8,1,32,128]{3,2,1,0:T(8,128)S(1)} %get-tuple-element.576), channel_id=1, source_target_pairs={{8,0},{16,8},{24,16},{32,24},{40,32},{48,40},{56,48},{64,56},{72,6... | collective-permute-start | bytes 393224 | tf_op jit(solution)/shard_map/ppermute | solution.py:23
  37.0 4.6 copy-start.5
  37.0 4.6 copy-start.9
  37.0 5.0 %copy-start.10 = (f32[1,1,32]{2,1,0:T(1,128)S(1)}, f32[1,1,32]{2,1,0:T(1,128)}, u32[]{:S(2)}) copy-start(f32[1,1,32]{2,1,0:T(1,128)} %param.22) | copy-start | bytes 388
  37.0 5.2 %copy-start.11 = (f32[1,1,32]{2,1,0:T(1,128)S(1)}, f32[1,1,32]{2,1,0:T(1,128)}, u32[]{:S(2)}) copy-start(f32[1,1,32]{2,1,0:T(1,128)} %param.23) | copy-start | bytes 388
  114.2 7.0 %copy-start.6 = (f32[4,16,32]{2,1,0:T(8,128)S(1)}, f32[4,16,32]{2,1,0:T(8,128)}, u32[]{:S(2)}) copy-start(f32[4,16,32]{2,1,0:T(8,128)} %param.14) | copy-start | bytes 24580
  114.2 7.0 %copy-start.7 = (f32[4,16,32]{2,1,0:T(8,128)S(1)}, f32[4,16,32]{2,1,0:T(8,128)}, u32[]{:S(2)}) copy-start(f32[4,16,32]{2,1,0:T(8,128)} %param.15) | copy-start | bytes 24580
  114.2 7.1 %copy-start.8 = (f32[4,16,32]{2,1,0:T(8,128)S(1)}, f32[4,16,32]{2,1,0:T(8,128)}, u32[]{:S(2)}) copy-start(f32[4,16,32]{2,1,0:T(8,128)} %param.16) | copy-start | bytes 24580
  114.2 7.1 %copy-start.4 = (f32[8,16,32,128]{3,2,1,0:T(8,128)S(1)}, f32[8,16,32,128]{3,2,1,0:T(8,128)}, u32[]{:S(2)}) copy-start(f32[8,16,32,128]{3,2,1,0:T(8,128)} %param.13) | copy-start | bytes 6291460
  123.6 11.8 %collective-permute-start.5 = (f32[8,1,32,128]{3,2,1,0:T(8,128)S(1)}, f32[8,1,32,128]{3,2,1,0:T(8,128)S(1)}, u32[]{:S(2)}, u32[]{:S(2)}) collective-permute-start(f32[8,1,32,128]{3,2,1,0:T(8,128)S(1)} %get-tuple-element.571), channel_id=1, source_target_pairs={{0,8},{8,16},{16,24},{24,32},{32,40},{40,48},{48,56},{56,64},{64,7... | collective-permute-start | bytes 393224 | tf_op jit(solution)/shard_map/ppermute | solution.py:21
  123.9 11.5 %collective-permute-start.4 = (f32[8,1,32,128]{3,2,1,0:T(8,128)S(1)}, f32[8,1,32,128]{3,2,1,0:T(8,128)S(1)}, u32[]{:S(2)}, u32[]{:S(2)}) collective-permute-start(f32[8,1,32,128]{3,2,1,0:T(8,128)S(1)} %get-tuple-element.572), channel_id=1, source_target_pairs={{8,0},{16,8},{24,16},{32,24},{40,32},{48,40},{56,48},{64,56},{72,6... | collective-permute-start | bytes 393224 | tf_op jit(solution)/shard_map/ppermute | solution.py:23
  128.5 5.6 %collective-permute-start.6 = (f32[8,16,1,128]{3,2,1,0:T(1,128)S(1)}, f32[8,16,1,128]{3,2,1,0:T(1,128)S(1)}, u32[]{:S(2)}, u32[]{:S(2)}) collective-permute-start(f32[8,16,1,128]{3,2,1,0:T(1,128)S(1)} %get-tuple-element.573), channel_id=1, source_target_pairs={{1,0},{2,1},{3,2},{4,3},{5,4},{6,5},{7,6},{9,8},{10,9},{11,10},{12... | collective-permute-start | bytes 196616 | tf_op jit(solution)/shard_map/ppermute | solution.py:23
  131.6 3.8 collective-permute-start.7
  137.6 11.2 %copy-start = (s32[1024]{0:T(1024)S(1)}, s32[1024]{0:T(1024)}, u32[]{:S(2)}) copy-start(s32[1024]{0:T(1024)} %param.19) | copy-start | bytes 12292
  138.8 9.9 %all-to-all-start = ((f32[16,2,128]{2,1,0:T(2,128)}), f32[16,2,128]{2,1,0:T(2,128)S(1)}, u32[]{:S(2)}, u32[]{:S(2)}) async-start(f32[16,2,128]{2,1,0:T(2,128)} %broadcast_select_fusion), calls=%async_computation | async-start | bytes 32768 | tf_op jit(solution)/shard_map/all_to_all | solution.py:176
  148.7 0.6 copy-start.2
  148.7 69.1 %all-gather.4.cloned.1.call-start = ((), (), s32[]{:S(2)}) async-start(), calls=%async_computation.1 | async-start | bytes 2113536 | tf_op jit(solution)/shard_map/while/body/eval_jaxpr/all_gather | solution.py:195
  161.5 58.9 %copy-start.3 = (f32[32,128]{1,0:T(8,128)S(1)}, f32[32,128]{1,0:T(8,128)}, u32[]{:S(2)}) copy-start(f32[32,128]{1,0:T(8,128)} %copy-done.2) | copy-start | bytes 49156 | tf_op jit(solution)/shard_map/while
  235.1 0.6 copy-start.2
  235.1 66.8 %all-gather.4.cloned.1.call-start = ((), (), s32[]{:S(2)}) async-start(), calls=%async_computation.1 | async-start | bytes 2113536 | tf_op jit(solution)/shard_map/while/body/eval_jaxpr/all_gather | solution.py:195
  247.9 56.6 %copy-start.3 = (f32[32,128]{1,0:T(8,128)S(1)}, f32[32,128]{1,0:T(8,128)}, u32[]{:S(2)}) copy-start(f32[32,128]{1,0:T(8,128)} %copy-done.2) | copy-start | bytes 49156 | tf_op jit(solution)/shard_map/while
  319.1 0.6 copy-start.2
  319.1 66.8 %all-gather.4.cloned.1.call-start = ((), (), s32[]{:S(2)}) async-start(), calls=%async_computation.1 | async-start | bytes 2113536 | tf_op jit(solution)/shard_map/while/body/eval_jaxpr/all_gather | solution.py:195
  332.0 56.6 %copy-start.3 = (f32[32,128]{1,0:T(8,128)S(1)}, f32[32,128]{1,0:T(8,128)}, u32[]{:S(2)}) copy-start(f32[32,128]{1,0:T(8,128)} %copy-done.2) | copy-start | bytes 49156 | tf_op jit(solution)/shard_map/while
  403.1 0.6 copy-start.2
  403.2 66.4 %all-gather.4.cloned.1.call-start = ((), (), s32[]{:S(2)}) async-start(), calls=%async_computation.1 | async-start | bytes 2113536 | tf_op jit(solution)/shard_map/while/body/eval_jaxpr/all_gather | solution.py:195
  415.9 56.4 %copy-start.3 = (f32[32,128]{1,0:T(8,128)S(1)}, f32[32,128]{1,0:T(8,128)}, u32[]{:S(2)}) copy-start(f32[32,128]{1,0:T(8,128)} %copy-done.2) | copy-start | bytes 49156 | tf_op jit(solution)/shard_map/while
  486.8 1.3 copy-start.1
Sparse Core Ops, SparseCore 0:
  152.7 65.1 all-gather.3
  239.1 62.7 all-gather.3
  323.1 62.7 all-gather.3
  406.8 62.7 all-gather.3
where the time goes:
time: 496 us; the launch traced here: 495 us
  waiting for transfers between devices  216 us (44%)
  local copies, waits for them, and re-layouts  79.7 us (16%)
  blocking collectives  64.4 us (13%)
  matrix products  58.2 us (12%)
  other arithmetic  36.2 us (7%)
  starting transfers between devices  26 us (5%)
  between operations  13.4 us (3%)
    all_gather x4, waiting for transfers between devices, one_panel(): every_slot = lax.all_gather(owner_rows, ('gx', 'gy'), axis=0, tiled=True)  209 us
    all_gather x1, blocking collectives, shards(): lax.all_gather(local_vals, ('gx', 'gy'), axis=0, tiled=True)  64.4 us
    dot_general x8, matrix products, regress(): jnp.dot(anomaly, spread.T, precision=PRECISE, preferred_element_type=jnp....  23.6 us
    dot_general x8, matrix products, regress(): jnp.dot(weighted * shrink[None, :], spread, precision=PRECISE, preferred_...  19.7 us
    dot_general x8, matrix products, regress(): jnp.dot(weighted, mean_gain[:, None], precision=PRECISE, preferred_elemen...  15 us
    gather x8, local copies, waits for them, and re-layouts, one_panel(): priors = every_slot[global_place[panel_index_list]]  14.7 us
    ppermute x4, starting transfers between devices, with_halo(): lax.ppermute(head, axis, [((i + 1) % count, i) for i in range(ends)])  14.7 us
  transfers between devices with their start and end apart: 13, of which 6 were waited for; matrix products, arithmetic and copies ran while one was open for 19% of the time, Pallas kernels for 0%

commit v1 on v0

v1 whole, which is shorter than its diff:
```python
import jax
import jax.numpy as jnp
from jax import lax
from jax.experimental import pallas as pl
from jax.experimental.pallas import tpu as pltpu
from jax.sharding import PartitionSpec as P

FSTEPS = 2
PANEL = 256
PANELS = 4
NOBS = 1024
COMP = 8
CX = 16
CY = 32
MEM = 128
BLOCK = CX * CY
F32 = jnp.float32
BF16 = jnp.bfloat16
NT = (((1,), (1,)), ((), ()))
NN = (((1,), (0,)), ((), ()))


def with_halo(cells, sides, width, closed):
    for axis, dim in sides:
        count = lax.axis_size(axis)
        ends = count if closed else count - 1
        head = lax.slice_in_dim(cells, 0, width, axis=dim)
        tail = lax.slice_in_dim(cells, cells.shape[dim] - width, cells.shape[dim], axis=dim)
        cells = jnp.concatenate(
            [
                lax.ppermute(tail, axis, [(i, (i + 1) % count) for i in range(ends)]),
                cells,
                lax.ppermute(head, axis, [((i + 1) % count, i) for i in range(ends)]),
            ],
            axis=dim,
        )
    return cells


def dot(left, right, dims=NN):
    return lax.dot_general(left, right, dims, preferred_element_type=F32)


def halves(full):
    high = full.astype(BF16)
    low = (full - high.astype(F32)).astype(BF16)
    return high, low


def as_columns(row):
    return jnp.transpose(jnp.broadcast_to(row, (128, row.shape[1])))


def plan_kernel(pos, table, perm, obs_weight, select, slots, source, place, counts):
    here_x = pos[0]
    here_y = pos[1]
    owner = table[4:5, :]
    lane = lax.broadcasted_iota(jnp.int32, (1, NOBS), 1)
    within = lane & 7
    rank = jnp.zeros((1, NOBS), jnp.int32)
    for gap in range(1, 8):
        same = (within >= gap) & (pltpu.roll(owner, gap, 1) == owner)
        rank = rank + same.astype(jnp.int32)
    place_row = (lane >> 6) * 2 + rank
    source_row = owner * 8 + ((lane >> 3) & 7)
    facts = jnp.concatenate(
        [table[0:4, :], place_row, source_row, jnp.zeros((2, NOBS), jnp.int32)], axis=0
    ).astype(F32)
    order = as_columns(table[5:6, :].astype(F32))
    lanes = lax.broadcasted_iota(jnp.int32, (NOBS, 128), 1).astype(F32)
    for part in range(NOBS // 128):
        hit = order == lanes + float(128 * part)
        perm[:, part * 128 : (part + 1) * 128] = jnp.where(hit, 1.0, 0.0).astype(BF16)
    ordered = dot(facts.astype(BF16), perm[...], NT)

    col_x = as_columns(ordered[0:1])
    col_y = as_columns(ordered[1:2])
    col_l = as_columns(ordered[2:3])
    place[...] = as_columns(ordered[4:5])
    col_s = as_columns(ordered[5:6])
    source[...] = jnp.where(col_s == lanes, 1.0, 0.0).astype(BF16)
    inverse = 1.0 / (ordered[3:4] + 1.0)
    first = 0
    for panel in range(PANELS - 1):
        begin = (panel + 1) * PANEL
        rows = NOBS - begin
        for part in range(PANEL // 128):
            cols = slice(panel * PANEL + part * 128, panel * PANEL + (part + 1) * 128)
            gap_x = jnp.abs(col_x[begin:] - ordered[0:1, cols])
            gap_x = jnp.minimum(gap_x, 256.0 - gap_x)
            gap_y = col_y[begin:] - ordered[1:2, cols]
            near = jnp.maximum(0.0, 1.0 - (gap_x * gap_x * (1.0 / 2304.0) + gap_y * gap_y * (1.0 / 9216.0)))
            gap_l = jnp.abs(col_l[begin:] - ordered[2:3, cols])
            level = jnp.maximum(0.0, 1.0 - gap_l * inverse[:, cols])
            obs_weight[first : first + rows, part * 128 : (part + 1) * 128] = (
                near * near * level * (1.0 / (MEM - 1))
            )
        first += rows

    whole = ordered.astype(jnp.int32)
    off_x = (whole[0:1] - here_x * CX) & 255
    far_x = jnp.where(off_x < CX, 0, jnp.minimum(off_x - (CX - 1), 256 - off_x))
    off_y = whole[1:2] - here_y * CY
    far_y = jnp.maximum(0, jnp.maximum(-off_y, off_y - (CY - 1)))
    reached = jnp.where(4 * far_x * far_x + far_y * far_y < 9216, 1.0, 0.0)
    before = lax.broadcasted_iota(jnp.int32, (PANEL, PANEL), 0) < lax.broadcasted_iota(
        jnp.int32, (PANEL, PANEL), 1
    )
    before = jnp.where(before, 1.0, 0.0).astype(BF16)
    slot = lax.broadcasted_iota(jnp.int32, (PANEL, PANEL), 0).astype(F32)
    for panel in range(PANELS):
        cols = slice(panel * PANEL, (panel + 1) * PANEL)
        mask = reached[:, cols]
        ranks = dot(jnp.broadcast_to(mask, (8, PANEL)).astype(BF16), before)[0:1]
        chosen = jnp.where((slot == ranks) & (mask > 0.0), 1.0, 0.0).astype(BF16)
        select[panel] = chosen
        packed = dot(ordered[:, cols].astype(BF16), chosen, NT)
        slots[panel] = jnp.concatenate(
            [packed[0:3], 1.0 / (packed[3:4] + 1.0), packed[4:8]], axis=0
        )
        counts[panel] = jnp.sum(mask).astype(jnp.int32)


def analysis_kernel(
    pos, counts, priors, given, state, perm, obs_weight, select, slots, source, place,
    out, rows, near, left, right,
):
    here_x = pos[0]
    here_y = pos[1]
    high, low = halves(priors[...])
    both = jnp.concatenate([high, low], axis=1)
    for panel in range(PANELS):
        span = slice(panel * PANEL, (panel + 1) * PANEL)
        moved = dot(perm[span, :], both)
        rows[span, :] = moved[:, :MEM] + moved[:, MEM:]
    v_high = given[...].astype(BF16)
    rest = given[...] - v_high.astype(F32)
    v_mid = rest.astype(BF16)
    v_low = (rest - v_mid.astype(F32)).astype(BF16)
    v_all = jnp.concatenate([v_high, v_mid, v_low], axis=1)
    lanes = lax.broadcasted_iota(jnp.int32, (PANEL, 128), 1).astype(F32)

    first = 0
    for panel in range(PANELS):
        span = slice(panel * PANEL, (panel + 1) * PANEL)
        held = dot(source[span, :], v_all)
        held = held[:, :128] + held[:, 128:256] + held[:, 256:]
        here = place[span, :]
        value = jnp.sum(jnp.where(lanes == here, held, 0.0), axis=1, keepdims=True)
        error = jnp.sum(jnp.where(lanes == here + 32.0, held, 0.0), axis=1, keepdims=True)
        prior = rows[span, :]
        centre = jnp.sum(prior, axis=1, keepdims=True) * (1.0 / MEM)
        spread = prior - centre
        variance = jnp.sum(spread * spread, axis=1, keepdims=True) / (MEM - 1)
        inverse = 1.0 / (variance + error)
        gain = (value - centre) * inverse
        shrink = inverse / (1.0 + jnp.sqrt(error * inverse))
        change = gain - shrink * spread
        q_high, q_low = halves(spread)
        h_high, h_low = halves(change)
        if panel < PANELS - 1:
            begin = (panel + 1) * PANEL
            count = NOBS - begin
            later = rows[begin:, :]
            l_high, l_low = halves(later - jnp.sum(later, axis=1, keepdims=True) * (1.0 / MEM))
            q_both = jnp.concatenate(
                [jnp.concatenate([q_high, q_high], axis=1), jnp.concatenate([q_low, q_low], axis=1)], axis=0
            )
            cov = dot(jnp.concatenate([l_high, l_low], axis=1), q_both, NT)
            local = (cov[:, :PANEL] + cov[:, PANEL:]) * obs_weight[first : first + count, :]
            g_high, g_low = halves(local)
            h_both = jnp.concatenate([h_high, h_low], axis=1)
            step = dot(g_high, h_both) + dot(g_low, h_both)
            rows[begin:, :] = later + (step[:, :MEM] + step[:, MEM:])
            first += count
        packed = dot(select[panel], jnp.concatenate([q_high, q_low, h_high, h_low], axis=1)).astype(BF16)
        for part in range(2):
            half = packed[part * 128 : (part + 1) * 128]
            q_h, q_l, h_h, h_l = (half[:, i * MEM : (i + 1) * MEM] for i in range(4))
            left[panel, part] = jnp.concatenate(
                [jnp.concatenate([q_h, q_h], axis=1), jnp.concatenate([q_l, q_l], axis=1)], axis=0
            )
            h_row = jnp.concatenate([h_h, h_l], axis=1)
            right[panel, part] = jnp.concatenate([h_row, h_row], axis=0)
        fact = slots[panel]
        step_x = lax.broadcasted_iota(jnp.int32, (CX, PANEL), 0) + here_x * CX
        gap_x = jnp.abs(step_x.astype(F32) - fact[0:1])
        gap_x = jnp.minimum(gap_x, 256.0 - gap_x)
        part_x = 1.0 - gap_x * gap_x * (1.0 / 2304.0)
        step_y = lax.broadcasted_iota(jnp.int32, (CY, PANEL), 0) + here_y * CY
        gap_y = step_y.astype(F32) - fact[1:2]
        part_y = gap_y * gap_y * (1.0 / 9216.0)
        for col in range(CX):
            close = jnp.maximum(0.0, part_x[col : col + 1] - part_y)
            near[panel, col * CY : (col + 1) * CY, :] = close * close * (1.0 / (MEM - 1))

    @pl.loop(0, COMP)
    def _(comp):
        level = (comp // 2).astype(F32)
        at = pl.ds(pl.multiple_of(comp * BLOCK, BLOCK), BLOCK)
        block = state[at, :]
        mean = jnp.sum(block, axis=1, keepdims=True) * (1.0 / MEM)
        out[at, :] = block - mean
        for panel in range(PANELS):
            fact = slots[panel]
            level_weight = jnp.maximum(0.0, 1.0 - jnp.abs(fact[2:3] - level) * fact[3:4])

            def local_step(both, part):
                cov = dot(both, left[panel, part], NT)
                cols = slice(part * 128, (part + 1) * 128)
                local = (cov[:, :128] + cov[:, 128:]) * (near[panel, :, cols] * level_weight[:, cols])
                g_high, g_low = halves(local)
                step = dot(jnp.concatenate([g_high, g_low], axis=1), right[panel, part])
                return step[:, :MEM] + step[:, MEM:]

            old = out[at, :]
            old_high, old_low = halves(old)
            old_both = jnp.concatenate([old_high, old_low], axis=1)
            out[at, :] = old + local_step(old_both, 0)

            @pl.when(counts[panel] > 128)
            def _():
                out[at, :] = out[at, :] + local_step(old_both, 1)
        out[at, :] = out[at, :] + mean


def vmem():
    return pl.BlockSpec(memory_space=pltpu.VMEM)


def smem():
    return pl.BlockSpec(memory_space=pltpu.SMEM)


def plan(pos, table):
    shapes = (
        jax.ShapeDtypeStruct((NOBS, NOBS), BF16),
        jax.ShapeDtypeStruct((6 * PANEL, PANEL), F32),
        jax.ShapeDtypeStruct((PANELS, PANEL, PANEL), BF16),
        jax.ShapeDtypeStruct((PANELS, 8, PANEL), F32),
        jax.ShapeDtypeStruct((NOBS, 128), BF16),
        jax.ShapeDtypeStruct((NOBS, 128), F32),
        jax.ShapeDtypeStruct((PANELS,), jnp.int32),
    )
    return pl.pallas_call(
        plan_kernel,
        out_shape=shapes,
        in_specs=[smem(), vmem()],
        out_specs=[vmem()] * 6 + [smem()],
        name="plan",
    )(pos, table)


def analyse(pos, counts, priors, given, state, *planned):
    return pl.pallas_call(
        analysis_kernel,
        out_shape=jax.ShapeDtypeStruct(state.shape, F32),
        in_specs=[smem(), smem()] + [vmem()] * (3 + len(planned)),
        out_specs=vmem(),
        scratch_shapes=[
            pltpu.VMEM((NOBS, MEM), F32),
            pltpu.VMEM((PANELS, BLOCK, PANEL), F32),
            pltpu.VMEM((PANELS, 2, PANEL, PANEL), BF16),
            pltpu.VMEM((PANELS, 2, PANEL, PANEL), BF16),
        ],
        compiler_params=pltpu.CompilerParams(vmem_limit_bytes=48 << 20),
        name="analyse",
    )(pos, counts, priors, given, state, *planned)


def shards(
    prior_member_matrix,
    east_speed,
    north_speed,
    diffusion,
    obs_column,
    obs_comp,
    observation_reach,
    obs_owner,
    obs_order,
    obs_value,
    obs_error,
):
    comps, zonal_extent, width_y, members = prior_member_matrix.shape
    per_level = comps // east_speed.shape[0]
    here_x = lax.axis_index("gx")
    here_y = lax.axis_index("gy")
    pos = jnp.stack([here_x, here_y]).astype(jnp.int32)
    zero = jnp.zeros_like(obs_comp)
    table = jnp.stack(
        [
            obs_column[:, 0],
            obs_column[:, 1],
            obs_comp // per_level,
            observation_reach,
            obs_owner,
            obs_order,
            zero,
            zero,
        ]
    )
    perm, obs_weight, select, slots, source, place, counts = plan(pos, table)

    east_vel = jnp.repeat(east_speed, per_level, axis=0)[..., None]
    north_vel = jnp.repeat(north_speed, per_level, axis=0)[..., None]
    diff_coef = jnp.repeat(diffusion, per_level, axis=0)[..., None]
    cells = prior_member_matrix
    for substep in range(FSTEPS):
        rim_wide = with_halo(cells, (("gx", 1),), 1, True)
        rim_tall = with_halo(cells, (("gy", 2),), 1, False)
        east_side = rim_wide[:, 2:]
        west_side = rim_wide[:, :-2]
        north_side = rim_tall[:, :, 2:]
        south_side = rim_tall[:, :, :-2]
        spread_term = diff_coef * (east_side + west_side + north_side + south_side - 4.0 * cells)
        carry_term = 0.5 * (
            east_vel * (east_side - west_side) + north_vel * (north_side - south_side)
        )
        cells = cells + spread_term - carry_term
    state = cells.reshape(comps * zonal_extent * width_y, members)

    begin = (here_x * lax.axis_size("gy") + here_y) * 8
    mine = lax.dynamic_slice(obs_column, (begin, 0), (8, 2))
    mine_comp = lax.dynamic_slice(obs_comp, (begin,), (8,))
    element = (mine_comp * zonal_extent + mine[:, 0] - here_x * zonal_extent) * width_y + (
        mine[:, 1] - here_y * width_y
    )
    held = jnp.concatenate([obs_value.reshape(1, -1), obs_error.reshape(1, -1)], axis=1)
    held = jnp.pad(held, ((0, 0), (0, members - held.shape[1])))
    bundle = jnp.concatenate([state[element], held], axis=0)
    bundle = jnp.broadcast_to(bundle.reshape(1, 9, 1, members), (128, 9, 1, members))
    arrived = lax.all_to_all(bundle, ("gx", "gy"), 0, 0, tiled=True)
    priors = arrived[:, :8].reshape(NOBS, members)
    given = arrived[:, 8].reshape(128, members)
    result = analyse(
        pos, counts, priors, given, state, perm, obs_weight, select, slots, source, place
    )
    return result.reshape(comps, zonal_extent, width_y, members)


def solution(mesh):
    return jax.shard_map(
        shards,
        mesh=mesh,
        in_specs=(
            P(None, "gx", "gy", None),
            P(None, "gx", "gy"),
            P(None, "gx", "gy"),
            P(None, "gx", "gy"),
            P(),
            P(),
            P(),
            P(),
            P(),
            P("gx", "gy", None),
            P("gx", "gy", None),
        ),
        out_specs=P(None, "gx", "gy", None),
        check_vma=False,
    )
```

time: 496 us -> 93.7 us (0.19)
  waiting for transfers between devices: 216 us -> 10.2 us
  local copies, waits for them, and re-layouts: 79.7 us -> 14.4 us
  blocking collectives: 64.4 us -> 0 us
  matrix products: 58.2 us -> 0 us
  Pallas kernels: 0 us -> 26.2 us
  other arithmetic: 36.2 us -> 11.2 us
  between operations: 13.4 us -> 0.25 us
    all_gather x4 -> x0, waiting for transfers between devices: 209 us -> none  [one_panel(): every_slot = lax.all_gather(owner_rows, ('gx', 'gy'), axis=0, tiled=True)]
    gather x40 -> x1, local copies, waits for them, and re-layouts: 71.4 us -> 0.56 us  [shards(): bundle = jnp.concatenate([state[element], held], axis=0)]
    all_gather x1 -> x0, blocking collectives: 64.4 us -> none  [shards(): lax.all_gather(local_vals, ('gx', 'gy'), axis=0, tiled=True)]
    dot_general x24 -> x0, matrix products: 58.2 us -> none  [the longest x8 23.6 us: regress(): jnp.dot(anomaly, spread.T, precision=PRECISE, preferred_element_type=jnp....]
    pallas_call x0 -> x2, Pallas kernels: none -> 26.2 us  [the longest x1 21.1 us: analyse(): pl.pallas_call(analysis_kernel, out_shape=jax.ShapeDtypeStruct(state.shap...]
    mul x8 -> x0, other arithmetic: 9.28 us -> none  [the longest x4 9.22 us: state_weight(): level_weight[:, None, :] * flat_weight[None, :, :]]
    sort x2 -> x0, other arithmetic: 8.73 us -> none  [the longest x1 4.37 us: slot_rank(): inverse_order = jnp.argsort(sort_order)]
    reduce_sum x15 -> x0, other arithmetic: 5.36 us -> none  [the longest x5 3.93 us: regress(): centre = jnp.mean(row_block, axis=1, keepdims=True)]
  transfers between devices with their start and end apart: 13 -> 9, of which waited for: 6 -> 3; matrix products, arithmetic and copies ran while one was open for 19% -> 4% of each run, Pallas kernels for 0% -> 6%
where the time goes in v1:
time: 93.7 us; the launch traced here: 92.9 us
  starting transfers between devices  30.5 us (33%)
  Pallas kernels  26.2 us (28%)
  local copies, waits for them, and re-layouts  14.4 us (15%)
  other arithmetic  11.2 us (12%)
  waiting for transfers between devices  10.2 us (11%)
    pallas_call x1, Pallas kernels, analyse(): pl.pallas_call(analysis_kernel, out_shape=jax.ShapeDtypeStruct(state.shap...  21.1 us
    ppermute x4, starting transfers between devices, with_halo(): lax.ppermute(head, axis, [((i + 1) % count, i) for i in range(ends)])  14.7 us
    sub x2, other arithmetic, shards(): cells = cells + spread_term - carry_term  9.67 us
    ppermute x4, starting transfers between devices, with_halo(): lax.ppermute(tail, axis, [(i, (i + 1) % count) for i in range(ends)])  8.45 us
    all_to_all x1, waiting for transfers between devices, shards(): arrived = lax.all_to_all(bundle, ('gx', 'gy'), 0, 0, tiled=True)  7.71 us
    all_to_all x1, starting transfers between devices, shards(): arrived = lax.all_to_all(bundle, ('gx', 'gy'), 0, 0, tiled=True)  7.43 us
    unnamed x28, local copies, waits for them, and re-layouts  6.57 us
    pallas_call x1, Pallas kernels, plan(): pl.pallas_call(plan_kernel, out_shape=shapes, in_specs=[smem(), vmem()],...  5.15 us
  transfers between devices with their start and end apart: 9, of which 3 were waited for; matrix products, arithmetic and copies ran while one was open for 4% of the time, Pallas kernels for 6%

profile of v1, /device:TPU:1, one launch (start us, length us, event | category | flops | bytes accessed | tf_op | source)
XLA Modules:
  0.0 92.9 jit_solution(1883670219815975382)
XLA Ops:
  0.0 1.3 %fusion.8 = (f32[8,16,1,128]{3,2,1,0:T(1,128)S(1)}, f32[8,16,1,128]{3,2,1,0:T(1,128)S(1)}) fusion(f32[8,16,32,128]{3,2,1,0:T(8,128)} %param.11), kind=kLoop, calls=%fused_computation.35 | loop fusion | bytes 262144 | tf_op jit(solution)/shard_map/slice | solution.py:27
  1.3 3.3 %collective-permute-start.2 = (f32[8,16,1,128]{3,2,1,0:T(1,128)S(1)}, f32[8,16,1,128]{3,2,1,0:T(1,128)S(1)}, u32[]{:S(2)}, u32[]{:S(2)}) collective-permute-start(f32[8,16,1,128]{3,2,1,0:T(1,128)S(1)} %get-tuple-element.25), channel_id=1, source_target_pairs={{1,0},{2,1},{3,2},{4,3},{5,4},{6,5},{7,6},{9,8},{10,9},{11,10},{12... | collective-permute-start | bytes 196616 | tf_op jit(solution)/shard_map/ppermute | solution.py:33
  4.6 3.5 %collective-permute-start.3 = (f32[8,16,1,128]{3,2,1,0:T(1,128)S(1)}, f32[8,16,1,128]{3,2,1,0:T(1,128)S(1)}, u32[]{:S(2)}, u32[]{:S(2)}) collective-permute-start(f32[8,16,1,128]{3,2,1,0:T(1,128)S(1)} %get-tuple-element.26), channel_id=1, source_target_pairs={{0,1},{1,2},{2,3},{3,4},{4,5},{5,6},{6,7},{8,9},{9,10},{10,11},{11... | collective-permute-start | bytes 196616 | tf_op jit(solution)/shard_map/ppermute | solution.py:31
  8.2 1.0 %fusion.7 = (f32[8,1,32,128]{3,2,1,0:T(8,128)S(1)}, f32[8,1,32,128]{3,2,1,0:T(8,128)S(1)}) fusion(f32[8,16,32,128]{3,2,1,0:T(8,128)} %param.11), kind=kLoop, calls=%fused_computation.34 | loop fusion | bytes 524288 | tf_op jit(solution)/shard_map/slice | solution.py:28
  9.2 1.3 %collective-permute-start.1 = (f32[8,1,32,128]{3,2,1,0:T(8,128)S(1)}, f32[8,1,32,128]{3,2,1,0:T(8,128)S(1)}, u32[]{:S(2)}, u32[]{:S(2)}) collective-permute-start(f32[8,1,32,128]{3,2,1,0:T(8,128)S(1)} %get-tuple-element.23), channel_id=1, source_target_pairs={{0,8},{8,16},{16,24},{24,32},{32,40},{40,48},{48,56},{56,64},{64,7... | collective-permute-start | bytes 393224 | tf_op jit(solution)/shard_map/ppermute | solution.py:31
  10.5 3.8 %collective-permute-start = (f32[8,1,32,128]{3,2,1,0:T(8,128)S(1)}, f32[8,1,32,128]{3,2,1,0:T(8,128)S(1)}, u32[]{:S(2)}, u32[]{:S(2)}) collective-permute-start(f32[8,1,32,128]{3,2,1,0:T(8,128)S(1)} %get-tuple-element.24), channel_id=1, source_target_pairs={{8,0},{16,8},{24,16},{32,24},{40,32},{48,40},{56,48},{64,56},{72,6... | collective-permute-start | bytes 393224 | tf_op jit(solution)/shard_map/ppermute | solution.py:33
  14.3 0.7 constant_dynamic-slice_fusion
  15.0 0.8 compare_select_fusion
  15.8 1.3 %collective-permute-done.1 = f32[8,1,32,128]{3,2,1,0:T(8,128)S(1)} collective-permute-done((f32[8,1,32,128]{3,2,1,0:T(8,128)S(1)}, f32[8,1,32,128]{3,2,1,0:T(8,128)S(1)}, u32[]{:S(2)}, u32[]{:S(2)}) %collective-permute-start.1) | collective-permute-done | bytes 131104 | tf_op jit(solution)/shard_map/ppermute | solution.py:31
  17.1 0.8 broadcast_in_dim.18
  17.9 0.8 broadcast_in_dim.19
  18.7 0.8 broadcast_in_dim.17
  19.4 7.5 %multiply_subtract_fusion.1 = f32[8,16,32,128]{3,2,1,0:T(8,128)S(1)} fusion(f32[8,16,32,128]{3,2,1,0:T(8,128)} %param.11, f32[8,16,1,128]{3,2,1,0:T(1,128)S(1)} %collective-permute-done.3, f32[8,16,1,128]{3,2,1,0:T(1,128)S(1)} %collective-permute-done.2, f32[8,1,32,128]{3,2,1,0:T(8,128)S(1)} %collective-permute-done, ...), kind=kLoop, calls=%fused_computation.10 | loop fusion | flops 9437184 | bytes 4636672 | tf_op jit(solution)/shard_map/sub | solution.py:319
  27.1 5.2 %collective-permute-start.4 = (f32[8,1,32,128]{3,2,1,0:T(8,128)S(1)}, f32[8,1,32,128]{3,2,1,0:T(8,128)S(1)}, u32[]{:S(2)}, u32[]{:S(2)}) collective-permute-start(f32[8,1,32,128]{3,2,1,0:T(8,128)S(1)} %get-tuple-element.20), channel_id=1, source_target_pairs={{8,0},{16,8},{24,16},{32,24},{40,32},{48,40},{56,48},{64,56},{72,6... | collective-permute-start | bytes 393224 | tf_op jit(solution)/shard_map/ppermute | solution.py:33
  32.3 2.4 %collective-permute-start.6 = (f32[8,16,1,128]{3,2,1,0:T(1,128)S(1)}, f32[8,16,1,128]{3,2,1,0:T(1,128)S(1)}, u32[]{:S(2)}, u32[]{:S(2)}) collective-permute-start(f32[8,16,1,128]{3,2,1,0:T(1,128)S(1)} %get-tuple-element.21), channel_id=1, source_target_pairs={{1,0},{2,1},{3,2},{4,3},{5,4},{6,5},{7,6},{9,8},{10,9},{11,10},{12... | collective-permute-start | bytes 196616 | tf_op jit(solution)/shard_map/ppermute | solution.py:33
  34.7 3.6 %collective-permute-start.7 = (f32[8,16,1,128]{3,2,1,0:T(1,128)S(1)}, f32[8,16,1,128]{3,2,1,0:T(1,128)S(1)}, u32[]{:S(2)}, u32[]{:S(2)}) collective-permute-start(f32[8,16,1,128]{3,2,1,0:T(1,128)S(1)} %get-tuple-element.22), channel_id=1, source_target_pairs={{0,1},{1,2},{2,3},{3,4},{4,5},{5,6},{6,7},{8,9},{9,10},{10,11},{11... | collective-permute-start | bytes 196616 | tf_op jit(solution)/shard_map/ppermute | solution.py:31
  38.4 1.2 %collective-permute-done.7 = f32[8,16,1,128]{3,2,1,0:T(1,128)S(1)} collective-permute-done((f32[8,16,1,128]{3,2,1,0:T(1,128)S(1)}, f32[8,16,1,128]{3,2,1,0:T(1,128)S(1)}, u32[]{:S(2)}, u32[]{:S(2)}) %collective-permute-start.7) | collective-permute-done | bytes 65568 | tf_op jit(solution)/shard_map/ppermute | solution.py:31
  39.6 2.1 %multiply_subtract_fusion = f32[8,16,32,128]{3,2,1,0:T(8,128)S(1)} fusion(f32[8,16,32,128]{3,2,1,0:T(8,128)S(1)} %multiply_subtract_fusion.1, f32[8,16,1,128]{3,2,1,0:T(1,128)S(1)} %collective-permute-done.7, f32[8,16,1,128]{3,2,1,0:T(1,128)S(1)} %collective-permute-done.6, f32[8,1,32,128]{3,2,1,0:T(8,128)S(1)} %collective-permute-done.4, ...), kind=kLoop, calls=%fused_computation.9 | loop fusion | flops 9437184 | bytes 4636672 | tf_op jit(solution)/shard_map/sub | solution.py:319
  42.3 1.1 %broadcast_in_dim.21 = f32[128,9,1,128]{3,2,1,0:T(1,128)} broadcast(f32[9,128]{1,0:T(8,128)S(1)} %pad_maximum_fusion.8), dimensions={1,3} | broadcast | bytes 594432 | tf_op jit(solution)/shard_map/broadcast_in_dim | solution.py:331
  43.5 7.4 %all-to-all-start = ((f32[128,9,1,128]{3,2,1,0:T(1,128)}), f32[128,9,1,128]{3,2,1,0:T(1,128)S(1)}, u32[]{:S(2)}, u32[]{:S(2)}) async-start(f32[128,9,1,128]{3,2,1,0:T(1,128)} %broadcast_in_dim.21), calls=%async_computation | async-start | bytes 1179648 | tf_op jit(solution)/shard_map/all_to_all | solution.py:332
  51.0 0.7 stack.35.table
  51.6 0.6 pad_add_fusion.pos
  52.3 5.1 %plan.1 = (bf16[1024,1024]{1,0:T(8,128)(2,1)}, f32[1536,256]{1,0:T(8,128)}, bf16[4,256,256]{2,1,0:T(8,128)(2,1)}, f32[4,8,256]{2,1,0:T(8,128)}, bf16[1024,128]{1...) custom-call(s32[2]{0:T(128)} %pad_add_fusion.pos, s32[8,1024]{1,0:T(8,128)} %stack.35.table), custom_call_target="tpu_custom_call" | custom-call | tf_op jit(solution)/shard_map/plan/pallas_call | solution.py:245
  57.4 7.7 %all-to-all-done = f32[128,9,1,128]{3,2,1,0:T(1,128)S(1)} async-done(((f32[128,9,1,128]{3,2,1,0:T(1,128)}), f32[128,9,1,128]{3,2,1,0:T(1,128)S(1)}, u32[]{:S(2)}, u32[]{:S(2)}) %all-to-all-start) | async-done | bytes 589856 | tf_op jit(solution)/shard_map/all_to_all | solution.py:332
  65.3 1.4 %copy-done = f32[1536,256]{1,0:T(8,128)S(1)} copy-done((f32[1536,256]{1,0:T(8,128)S(1)}, f32[1536,256]{1,0:T(8,128)}, u32[]{:S(2)}) %copy-start) | copy-done | bytes 1572888
  66.7 1.0 %copy-done.1 = bf16[4,256,256]{2,1,0:T(8,128)(2,1)S(1)} copy-done((bf16[4,256,256]{2,1,0:T(8,128)(2,1)S(1)}, bf16[4,256,256]{2,1,0:T(8,128)(2,1)}, u32[]{:S(2)}) %copy-start.1) | copy-done | bytes 524312
  67.7 1.0 %copy-done.2 = f32[1024,128]{1,0:T(8,128)S(1)} copy-done((f32[1024,128]{1,0:T(8,128)S(1)}, f32[1024,128]{1,0:T(8,128)}, u32[]{:S(2)}) %copy-start.2) | copy-done | bytes 524312
  68.7 0.9 %copy-done.3 = bf16[1024,128]{1,0:T(8,128)(2,1)S(1)} copy-done((bf16[1024,128]{1,0:T(8,128)(2,1)S(1)}, bf16[1024,128]{1,0:T(8,128)(2,1)}, u32[]{:S(2)}) %copy-start.3) | copy-done | bytes 262168
  69.7 0.8 copy-done.4
  70.5 0.7 copy-done.5
  71.1 0.7 copy-done.6
  71.8 21.1 %analyse.1 = f32[4096,128]{1,0:T(8,128)} custom-call(s32[2]{0:T(128)S(1)} %copy-done.5, s32[4]{0:T(128)S(1)} %copy-done.6, f32[1024,128]{1,0:T(8,128)S(1)} %bitcast.37, f32[128,128]{1,0:T(8,128)S(1)} %bitcast.38, f32[4096,128]{1,0:T(8,128)S(1)} %bitcast.36, bf16[1024,1024]{1,0:T(8,128)(2,1)} %get-tuple-element.13.perm, f32[1536,256]{1,0:T(8,128)S(1)} %copy-done, ...), custom_call_target="tpu_custom_call" | custom-call | tf_op jit(solution)/shard_map/analyse/pallas_call | solution.py:255
  (39 shorter events, 1.0 us)
Async XLA Ops:
  1.3 14.5 %collective-permute-start.2 = (f32[8,16,1,128]{3,2,1,0:T(1,128)S(1)}, f32[8,16,1,128]{3,2,1,0:T(1,128)S(1)}, u32[]{:S(2)}, u32[]{:S(2)}) collective-permute-start(f32[8,16,1,128]{3,2,1,0:T(1,128)S(1)} %get-tuple-element.25), channel_id=1, source_target_pairs={{1,0},{2,1},{3,2},{4,3},{5,4},{6,5},{7,6},{9,8},{10,9},{11,10},{12... | collective-permute-start | bytes 196616 | tf_op jit(solution)/shard_map/ppermute | solution.py:33
  4.6 11.1 %collective-permute-start.3 = (f32[8,16,1,128]{3,2,1,0:T(1,128)S(1)}, f32[8,16,1,128]{3,2,1,0:T(1,128)S(1)}, u32[]{:S(2)}, u32[]{:S(2)}) collective-permute-start(f32[8,16,1,128]{3,2,1,0:T(1,128)S(1)} %get-tuple-element.26), channel_id=1, source_target_pairs={{0,1},{1,2},{2,3},{3,4},{4,5},{5,6},{6,7},{8,9},{9,10},{10,11},{11... | collective-permute-start | bytes 196616 | tf_op jit(solution)/shard_map/ppermute | solution.py:31
  9.2 8.0 %collective-permute-start.1 = (f32[8,1,32,128]{3,2,1,0:T(8,128)S(1)}, f32[8,1,32,128]{3,2,1,0:T(8,128)S(1)}, u32[]{:S(2)}, u32[]{:S(2)}) collective-permute-start(f32[8,1,32,128]{3,2,1,0:T(8,128)S(1)} %get-tuple-element.23), channel_id=1, source_target_pairs={{0,8},{8,16},{16,24},{24,32},{32,40},{40,48},{48,56},{56,64},{64,7... | collective-permute-start | bytes 393224 | tf_op jit(solution)/shard_map/ppermute | solution.py:31
  10.5 6.7 %collective-permute-start = (f32[8,1,32,128]{3,2,1,0:T(8,128)S(1)}, f32[8,1,32,128]{3,2,1,0:T(8,128)S(1)}, u32[]{:S(2)}, u32[]{:S(2)}) collective-permute-start(f32[8,1,32,128]{3,2,1,0:T(8,128)S(1)} %get-tuple-element.24), channel_id=1, source_target_pairs={{8,0},{16,8},{24,16},{32,24},{40,32},{48,40},{56,48},{64,56},{72,6... | collective-permute-start | bytes 393224 | tf_op jit(solution)/shard_map/ppermute | solution.py:33
  19.4 18.9 %copy-start.12 = (f32[1,1,32]{2,1,0:T(1,128)S(1)}, f32[1,1,32]{2,1,0:T(1,128)}, u32[]{:S(2)}) copy-start(f32[1,1,32]{2,1,0:T(1,128)} %param.21) | copy-start | bytes 388
  19.4 18.9 %copy-start.13 = (f32[1,1,32]{2,1,0:T(1,128)S(1)}, f32[1,1,32]{2,1,0:T(1,128)}, u32[]{:S(2)}) copy-start(f32[1,1,32]{2,1,0:T(1,128)} %param.20) | copy-start | bytes 388
  27.0 12.6 %collective-permute-start.5 = (f32[8,1,32,128]{3,2,1,0:T(8,128)S(1)}, f32[8,1,32,128]{3,2,1,0:T(8,128)S(1)}, u32[]{:S(2)}, u32[]{:S(2)}) collective-permute-start(f32[8,1,32,128]{3,2,1,0:T(8,128)S(1)} %get-tuple-element.19), channel_id=1, source_target_pairs={{0,8},{8,16},{16,24},{24,32},{32,40},{40,48},{48,56},{56,64},{64,7... | collective-permute-start | bytes 393224 | tf_op jit(solution)/shard_map/ppermute | solution.py:31
  27.1 12.5 %collective-permute-start.4 = (f32[8,1,32,128]{3,2,1,0:T(8,128)S(1)}, f32[8,1,32,128]{3,2,1,0:T(8,128)S(1)}, u32[]{:S(2)}, u32[]{:S(2)}) collective-permute-start(f32[8,1,32,128]{3,2,1,0:T(8,128)S(1)} %get-tuple-element.20), channel_id=1, source_target_pairs={{8,0},{16,8},{24,16},{32,24},{40,32},{48,40},{56,48},{64,56},{72,6... | collective-permute-start | bytes 393224 | tf_op jit(solution)/shard_map/ppermute | solution.py:33
  32.3 6.1 %collective-permute-start.6 = (f32[8,16,1,128]{3,2,1,0:T(1,128)S(1)}, f32[8,16,1,128]{3,2,1,0:T(1,128)S(1)}, u32[]{:S(2)}, u32[]{:S(2)}) collective-permute-start(f32[8,16,1,128]{3,2,1,0:T(1,128)S(1)} %get-tuple-element.21), channel_id=1, source_target_pairs={{1,0},{2,1},{3,2},{4,3},{5,4},{6,5},{7,6},{9,8},{10,9},{11,10},{12... | collective-permute-start | bytes 196616 | tf_op jit(solution)/shard_map/ppermute | solution.py:33
  34.7 4.9 %collective-permute-start.7 = (f32[8,16,1,128]{3,2,1,0:T(1,128)S(1)}, f32[8,16,1,128]{3,2,1,0:T(1,128)S(1)}, u32[]{:S(2)}, u32[]{:S(2)}) collective-permute-start(f32[8,16,1,128]{3,2,1,0:T(1,128)S(1)} %get-tuple-element.22), channel_id=1, source_target_pairs={{0,1},{1,2},{2,3},{3,4},{4,5},{5,6},{6,7},{8,9},{9,10},{10,11},{11... | collective-permute-start | bytes 196616 | tf_op jit(solution)/shard_map/ppermute | solution.py:31
  38.4 12.5 %copy-start.8 = (s32[1024]{0:T(1024)S(1)}, s32[1024]{0:T(1024)}, u32[]{:S(2)}) copy-start(s32[1024]{0:T(1024)} %param.16) | copy-start | bytes 12292
  38.4 12.5 %copy-start.7 = (s32[1024,2]{0,1:T(2,128)S(1)}, s32[1024,2]{0,1:T(2,128)}, u32[]{:S(2)}) copy-start(s32[1024,2]{0,1:T(2,128)} %param.15) | copy-start | bytes 24580
  38.4 12.6 %copy-start.9 = (s32[1024]{0:T(1024)S(1)}, s32[1024]{0:T(1024)}, u32[]{:S(2)}) copy-start(s32[1024]{0:T(1024)} %param.17) | copy-start | bytes 12292
  38.4 12.6 %copy-start.10 = (s32[1024]{0:T(1024)S(1)}, s32[1024]{0:T(1024)}, u32[]{:S(2)}) copy-start(s32[1024]{0:T(1024)} %param.18) | copy-start | bytes 12292
  38.4 12.6 %copy-start.11 = (s32[1024]{0:T(1024)S(1)}, s32[1024]{0:T(1024)}, u32[]{:S(2)}) copy-start(s32[1024]{0:T(1024)} %param.19) | copy-start | bytes 12292
  43.5 21.7 %all-to-all-start = ((f32[128,9,1,128]{3,2,1,0:T(1,128)}), f32[128,9,1,128]{3,2,1,0:T(1,128)S(1)}, u32[]{:S(2)}, u32[]{:S(2)}) async-start(f32[128,9,1,128]{3,2,1,0:T(1,128)} %broadcast_in_dim.21), calls=%async_computation | async-start | bytes 1179648 | tf_op jit(solution)/shard_map/all_to_all | solution.py:332
  65.3 1.4 %copy-start = (f32[1536,256]{1,0:T(8,128)S(1)}, f32[1536,256]{1,0:T(8,128)}, u32[]{:S(2)}) copy-start(f32[1536,256]{1,0:T(8,128)} %get-tuple-element.14.obs_weight) | copy-start | bytes 4718596
  66.7 1.0 %copy-start.1 = (bf16[4,256,256]{2,1,0:T(8,128)(2,1)S(1)}, bf16[4,256,256]{2,1,0:T(8,128)(2,1)}, u32[]{:S(2)}) copy-start(bf16[4,256,256]{2,1,0:T(8,128)(2,1)} %get-tuple-element.15.select) | copy-start | bytes 1572868
  67.7 1.0 %copy-start.2 = (f32[1024,128]{1,0:T(8,128)S(1)}, f32[1024,128]{1,0:T(8,128)}, u32[]{:S(2)}) copy-start(f32[1024,128]{1,0:T(8,128)} %get-tuple-element.18.place) | copy-start | bytes 1572868
  68.7 0.9 %copy-start.3 = (bf16[1024,128]{1,0:T(8,128)(2,1)S(1)}, bf16[1024,128]{1,0:T(8,128)(2,1)}, u32[]{:S(2)}) copy-start(bf16[1024,128]{1,0:T(8,128)(2,1)} %get-tuple-element.17.source) | copy-start | bytes 786436
  69.7 0.8 copy-start.4
  70.5 0.7 copy-start.5
  71.1 0.7 copy-start.6

commit v2 on v1

--- a/solution.py
+++ b/solution.py
@@ -18,23 +18,6 @@
 BF16 = jnp.bfloat16
 NT = (((1,), (1,)), ((), ()))
 NN = (((1,), (0,)), ((), ()))
-
-
-def with_halo(cells, sides, width, closed):
-    for axis, dim in sides:
-        count = lax.axis_size(axis)
-        ends = count if closed else count - 1
-        head = lax.slice_in_dim(cells, 0, width, axis=dim)
-        tail = lax.slice_in_dim(cells, cells.shape[dim] - width, cells.shape[dim], axis=dim)
-        cells = jnp.concatenate(
-            [
-                lax.ppermute(tail, axis, [(i, (i + 1) % count) for i in range(ends)]),
-                cells,
-                lax.ppermute(head, axis, [((i + 1) % count, i) for i in range(ends)]),
-            ],
-            axis=dim,
-        )
-    return cells
 
 
 def dot(left, right, dims=NN):
@@ -224,6 +207,254 @@
         out[at, :] = out[at, :] + mean
 
 
+OFFSETS = (
+    (0, 0), (-1, 0), (1, 0), (0, -1), (0, 1),
+    (-1, -1), (-1, 1), (1, -1), (1, 1),
+    (-2, 0), (2, 0), (0, -2), (0, 2),
+)
+
+
+def edge_kernel(pos, code, cells, east, north, diff, own, own_coef, to_east, to_west, to_north, to_south):
+    here_x = pos[0]
+    here_y = pos[1]
+    coefs = (east, north, diff)
+
+    def look(shift_x, shift_y, k):
+        tile_x = (here_x + shift_x) & 15
+        tile_y = jnp.clip(here_y + shift_y, 0, 7)
+        word = code[(tile_x * 8 + tile_y) * 8 + k]
+        return word & 15, (word >> 8) & 31, word >> 16
+
+    def cell(comp, x, y):
+        return cells[pl.ds((comp * CX + x) * CY + y, 1), :]
+
+    def clip_x(x):
+        return jnp.clip(x, 0, CX - 1)
+
+    def clip_y(y):
+        return jnp.clip(y, 0, CY - 1)
+
+    for k in range(8):
+        x, y, comp = look(0, 0, k)
+        for index, (step_x, step_y) in enumerate(OFFSETS):
+            at = index * 8 + k
+            own[at : at + 1, :] = cell(comp, clip_x(x + step_x), clip_y(y + step_y))
+        for step_x in (-1, 0, 1):
+            for c in range(3):
+                at = (c * 3 + step_x + 1) * 8 + k
+                own_coef[at : at + 1, 0:CY] = coefs[c][pl.ds((comp >> 1) * CX + clip_x(x + step_x), 1), :]
+        for shift, target, edge in ((1, to_east, CX - 1), (-1, to_west, 0)):
+            x, y, comp = look(shift, 0, k)
+            for index, step_y in enumerate((-1, 0, 1)):
+                at = index * 8 + k
+                target[at : at + 1, :] = cell(comp, edge, clip_y(y + step_y))
+            target[24 + k : 25 + k, :] = cell(comp, clip_x(x + shift * (CX - 2)), y)
+            _, _, comp = look(shift, 1, k)
+            target[32 + k : 33 + k, :] = cell(comp, edge, CY - 1)
+            _, _, comp = look(shift, -1, k)
+            target[40 + k : 41 + k, :] = cell(comp, edge, 0)
+        for shift, target, edge in ((1, to_north, CY - 1), (-1, to_south, 0)):
+            x, y, comp = look(0, shift, k)
+            for index, step_x in enumerate((-1, 0, 1)):
+                at = index * 8 + k
+                target[at : at + 1, :] = cell(comp, clip_x(x + step_x), edge)
+            target[24 + k : 25 + k, :] = cell(comp, x, clip_y(y + shift * (CY - 2)))
+    for target, edge in ((to_east, CX - 1), (to_west, 0)):
+        target[48:64, :] = jnp.zeros((16, MEM), F32)
+        for c in range(3):
+            for level in range(4):
+                at = 48 + c * 4 + level
+                target[at : at + 1, 0:CY] = coefs[c][level * CX + edge : level * CX + edge + 1, :]
+    lanes = lax.broadcasted_iota(jnp.int32, (CX, MEM), 1)
+    for target, edge in ((to_north, CY - 1), (to_south, 0)):
+        table = jnp.zeros((CX, MEM), F32)
+        for c in range(3):
+            for level in range(4):
+                line = coefs[c][level * CX : (level + 1) * CX, edge : edge + 1]
+                table = jnp.where(lanes == c * 4 + level, line, table)
+        target[32:48, :] = table
+
+
+def obs_columns(pos, code):
+    begin = (pos[0] * 8 + pos[1]) * 8
+    row = lax.broadcasted_iota(jnp.int32, (8, MEM), 0)
+    word = jnp.zeros((8, MEM), jnp.int32)
+    for k in range(8):
+        word = jnp.where(row == k, code[begin + k], word)
+    return word & 15, (word >> 8) & 31, word >> 16
+
+
+def corner_kernel(pos, code, base_north, base_south, from_west, from_east, to_north, to_south):
+    row = lax.broadcasted_iota(jnp.int32, (8, MEM), 0)
+    for shift, base, target, first in ((1, base_north, to_north, 32), (-1, base_south, to_south, 40)):
+        tile_y = jnp.clip(pos[1] + shift, 0, 7)
+        begin = (pos[0] * 8 + tile_y) * 8
+        x = jnp.zeros((8, MEM), jnp.int32)
+        for k in range(8):
+            x = jnp.where(row == k, code[begin + k] & 15, x)
+        target[...] = base[...]
+        target[0:8, :] = jnp.where(x == 0, from_west[first : first + 8, :], base[0:8, :])
+        target[16:24, :] = jnp.where(x == CX - 1, from_east[first : first + 8, :], base[16:24, :])
+
+
+def prior_kernel(
+    pos, code, own, own_coef, from_west, from_east, from_south, from_north, held, out, scratch
+):
+    x, y, comp = obs_columns(pos, code)
+    level = comp >> 1
+    west = x == 0
+    east = x == CX - 1
+    begin = (pos[0] * 8 + pos[1]) * 8
+    for k in range(8):
+        word = code[begin + k]
+        here_l = word >> 17
+        for c in range(3):
+            at = c * 8 + k
+            scratch[at : at + 1, :] = from_west[pl.ds(48 + c * 4 + here_l, 1), :]
+            scratch[24 + at : 25 + at, :] = from_east[pl.ds(48 + c * 4 + here_l, 1), :]
+        scratch[48 + k : 49 + k, :] = from_south[pl.ds(32 + (word & 15), 1), :]
+        scratch[56 + k : 57 + k, :] = from_north[pl.ds(32 + (word & 15), 1), :]
+
+    state = {}
+    for index, (step_x, step_y) in enumerate(OFFSETS):
+        value = own[index * 8 : index * 8 + 8, :]
+        if step_x < 0:
+            group = 3 if step_x == -2 else step_y + 1
+            value = jnp.where(x + step_x < 0, from_west[group * 8 : group * 8 + 8, :], value)
+        if step_x > 0:
+            group = 3 if step_x == 2 else step_y + 1
+            value = jnp.where(x + step_x >= CX, from_east[group * 8 : group * 8 + 8, :], value)
+        if step_y < 0:
+            group = 3 if step_y == -2 else step_x + 1
+            value = jnp.where(y + step_y < 0, from_south[group * 8 : group * 8 + 8, :], value)
+        if step_y > 0:
+            group = 3 if step_y == 2 else step_x + 1
+            value = jnp.where(y + step_y >= CY, from_north[group * 8 : group * 8 + 8, :], value)
+        state[(step_x, step_y)] = value
+
+    lanes = lax.broadcasted_iota(jnp.int32, (8, MEM), 1)
+    at_y = lanes[:, :CY] - y[:, :CY]
+
+    def pick(values, mask):
+        return jnp.sum(jnp.where(mask, values, 0.0), axis=1, keepdims=True)
+
+    def rows_of(c, step_x):
+        at = (c * 3 + step_x + 1) * 8
+        return own_coef[at : at + 8, 0:CY]
+
+    def coefs_at(step_x, step_y):
+        found = []
+        for c in range(3):
+            value = pick(rows_of(c, step_x), at_y == step_y)
+            if step_x == -1:
+                value = jnp.where(west[:, :1], pick(scratch[c * 8 : c * 8 + 8, 0:CY], at_y == 0), value)
+            if step_x == 1:
+                value = jnp.where(east[:, :1], pick(scratch[24 + c * 8 : 32 + c * 8, 0:CY], at_y == 0), value)
+            mine = lanes == c * 4 + level
+            if step_y == -1:
+                value = jnp.where(y[:, :1] == 0, pick(scratch[48:56, :], mine), value)
+            if step_y == 1:
+                value = jnp.where(y[:, :1] == CY - 1, pick(scratch[56:64, :], mine), value)
+            found.append(value)
+        return found
+
+    def advance(field, step_x, step_y):
+        u, v, nu = coefs_at(step_x, step_y)
+        mid = field[(step_x, step_y)]
+        e = field[(step_x + 1, step_y)]
+        w = field[(step_x - 1, step_y)]
+        n = field[(step_x, step_y + 1)]
+        s = field[(step_x, step_y - 1)]
+        return mid + nu * (e + w + n + s - 4.0 * mid) - 0.5 * (u * (e - w) + v * (n - s))
+
+    after = {key: advance(state, *key) for key in OFFSETS[:5]}
+    out[0:8, :] = advance(after, 0, 0)
+    out[8:9, :] = held[...]
+
+
+def stencil(mid, e, w, n, s, u, v, nu):
+    return mid + nu * (e + w + n + s - 4.0 * mid) - 0.5 * (u * (e - w) + v * (n - s))
+
+
+def forecast_kernel(
+    cells, east, north, diff, halo_w, halo_e, halo_s, halo_n, edge_w, edge_e, edge_s, edge_n,
+    out, table, before, after,
+):
+    coefs = (east, north, diff)
+    pad = jnp.zeros((128 - CX, CY), F32)
+    fill = jnp.zeros((128, 128 - CY), F32)
+    for c in range(3):
+        for level in range(4):
+            tile = coefs[c][level * CX : (level + 1) * CX, :]
+            ends = jnp.concatenate(
+                [
+                    tile,
+                    edge_w[48 + c * 4 + level : 49 + c * 4 + level, 0:CY],
+                    edge_e[48 + c * 4 + level : 49 + c * 4 + level, 0:CY],
+                    pad[: 128 - CX - 2],
+                ],
+                axis=0,
+            )
+            turned = jnp.transpose(jnp.concatenate([ends, fill], axis=1))
+            table[level, c] = turned[0:CY, :]
+
+    mid_rows = slice(8, 8 + CY)
+    for level in range(4):
+        for which in range(2):
+            comp = level * 2 + which
+            before[which, 2 : 2 + CX, mid_rows, :] = cells[comp]
+            before[which, 0:2, mid_rows, :] = halo_w[comp]
+            before[which, 2 + CX : 4 + CX, mid_rows, :] = halo_e[comp]
+            before[which, 1 : 3 + CX, 7, :] = halo_s[comp, :, 1, :]
+            before[which, 1 : 3 + CX, 8 + CY, :] = halo_n[comp, :, 0, :]
+        for col in range(-1, CX + 1):
+            lane = CX if col < 0 else (CX + 1 if col == CX else col)
+            u, v, nu = (
+                jnp.broadcast_to(table[level, c, :, lane : lane + 1], (CY, MEM)) for c in range(3)
+            )
+            at = col + 2
+            for which in range(2):
+                after[which, at, mid_rows, :] = stencil(
+                    before[which, at, mid_rows, :],
+                    before[which, at + 1, mid_rows, :],
+                    before[which, at - 1, mid_rows, :],
+                    before[which, at, 9 : 9 + CY, :],
+                    before[which, at, 7 : 7 + CY, :],
+                    u, v, nu,
+                )
+        for rim, edge, inner, outer, inside, target in (
+            (halo_s, edge_s, 1, 0, 0, 7),
+            (halo_n, edge_n, 0, 1, CY - 1, 8 + CY),
+        ):
+            u, v, nu = (
+                jnp.broadcast_to(edge[32:48, c * 4 + level : c * 4 + level + 1], (CX, MEM))
+                for c in range(3)
+            )
+            for which in range(2):
+                comp = level * 2 + which
+                mid = rim[comp, 1 : 1 + CX, inner, :]
+                e = rim[comp, 2 : 2 + CX, inner, :]
+                w = rim[comp, 0:CX, inner, :]
+                far = rim[comp, 1 : 1 + CX, outer, :]
+                close = cells[comp, :, inside, :]
+                n, s = (close, far) if target == 7 else (far, close)
+                after[which, 2 : 2 + CX, target, :] = stencil(mid, e, w, n, s, u, v, nu)
+        for col in range(CX):
+            u, v, nu = (
+                jnp.broadcast_to(table[level, c, :, col : col + 1], (CY, MEM)) for c in range(3)
+            )
+            at = col + 2
+            for which in range(2):
+                out[level * 2 + which, col] = stencil(
+                    after[which, at, mid_rows, :],
+                    after[which, at + 1, mid_rows, :],
+                    after[which, at - 1, mid_rows, :],
+                    after[which, at, 9 : 9 + CY, :],
+                    after[which, at, 7 : 7 + CY, :],
+                    u, v, nu,
+                )
+
+
 def vmem():
     return pl.BlockSpec(memory_space=pltpu.VMEM)
 
@@ -301,35 +532,72 @@
     )
     perm, obs_weight, select, slots, source, place, counts = plan(pos, table)
 
-    east_vel = jnp.repeat(east_speed, per_level, axis=0)[..., None]
-    north_vel = jnp.repeat(north_speed, per_level, axis=0)[..., None]
-    diff_coef = jnp.repeat(diffusion, per_level, axis=0)[..., None]
+    def rows(count, width=MEM):
+        return jax.ShapeDtypeStruct((count, width), F32)
+
+    def along_x(value, step):
+        return lax.ppermute(value, "gx", [(i, (i + step) % 16) for i in range(16)])
+
+    def along_y(value, step):
+        return lax.ppermute(value, "gy", [(i, i + step) for i in range(8) if 0 <= i + step < 8])
+
+    code = obs_column[:, 0] + obs_column[:, 1] * 256 + obs_comp * 65536
     cells = prior_member_matrix
-    for substep in range(FSTEPS):
-        rim_wide = with_halo(cells, (("gx", 1),), 1, True)
-        rim_tall = with_halo(cells, (("gy", 2),), 1, False)
-        east_side = rim_wide[:, 2:]
-        west_side = rim_wide[:, :-2]
-        north_side = rim_tall[:, :, 2:]
-        south_side = rim_tall[:, :, :-2]
-        spread_term = diff_coef * (east_side + west_side + north_side + south_side - 4.0 * cells)
-        carry_term = 0.5 * (
-            east_vel * (east_side - west_side) + north_vel * (north_side - south_side)
-        )
-        cells = cells + spread_term - carry_term
-    state = cells.reshape(comps * zonal_extent * width_y, members)
-
-    begin = (here_x * lax.axis_size("gy") + here_y) * 8
-    mine = lax.dynamic_slice(obs_column, (begin, 0), (8, 2))
-    mine_comp = lax.dynamic_slice(obs_comp, (begin,), (8,))
-    element = (mine_comp * zonal_extent + mine[:, 0] - here_x * zonal_extent) * width_y + (
-        mine[:, 1] - here_y * width_y
-    )
+    flat = cells.reshape(-1, members)
+    speeds = [field.reshape(-1, width_y) for field in (east_speed, north_speed, diffusion)]
+    own, own_coef, to_east, to_west, base_north, base_south = pl.pallas_call(
+        edge_kernel,
+        out_shape=(rows(104), rows(72), rows(64), rows(64), rows(48), rows(48)),
+        in_specs=[smem(), smem()] + [vmem()] * 4,
+        out_specs=[vmem()] * 6,
+        name="edges",
+    )(pos, code, flat, *speeds)
+    from_west = along_x(to_east, 1)
+    from_east = along_x(to_west, -1)
+    to_north, to_south = pl.pallas_call(
+        corner_kernel,
+        out_shape=(rows(48), rows(48)),
+        in_specs=[smem(), smem()] + [vmem()] * 4,
+        out_specs=[vmem()] * 2,
+        name="corners",
+    )(pos, code, base_north, base_south, from_west, from_east)
+    from_south = along_y(to_north, 1)
+    from_north = along_y(to_south, -1)
     held = jnp.concatenate([obs_value.reshape(1, -1), obs_error.reshape(1, -1)], axis=1)
     held = jnp.pad(held, ((0, 0), (0, members - held.shape[1])))
-    bundle = jnp.concatenate([state[element], held], axis=0)
+    bundle = pl.pallas_call(
+        prior_kernel,
+        out_shape=rows(9),
+        in_specs=[smem(), smem()] + [vmem()] * 7,
+        out_specs=vmem(),
+        scratch_shapes=[pltpu.VMEM((64, MEM), F32)],
+        name="priors",
+    )(pos, code, own, own_coef, from_west, from_east, from_south, from_north, held)
+
+    bundle, late = lax.optimization_barrier((bundle, cells))
     bundle = jnp.broadcast_to(bundle.reshape(1, 9, 1, members), (128, 9, 1, members))
     arrived = lax.all_to_all(bundle, ("gx", "gy"), 0, 0, tiled=True)
+
+    halo_w = along_x(late[:, CX - 2 :], 1)
+    halo_e = along_x(late[:, :2], -1)
+    wide = jnp.concatenate([halo_w[:, 1:], late, halo_e[:, :1]], axis=1)
+    halo_s = along_y(wide[:, :, CY - 2 :], 1)
+    halo_n = along_y(wide[:, :, :2], -1)
+    state = pl.pallas_call(
+        forecast_kernel,
+        out_shape=jax.ShapeDtypeStruct(cells.shape, F32),
+        in_specs=[vmem()] * 12,
+        out_specs=vmem(),
+        scratch_shapes=[
+            pltpu.VMEM((4, 3, CY, 128), F32),
+            pltpu.VMEM((2, CX + 4, CY + 16, MEM), F32),
+            pltpu.VMEM((2, CX + 4, CY + 16, MEM), F32),
+        ],
+        compiler_params=pltpu.CompilerParams(vmem_limit_bytes=32 << 20),
+        name="forecast",
+    )(late, *speeds, halo_w, halo_e, halo_s, halo_n, from_west, from_east, from_south, from_north)
+    state = state.reshape(-1, members)
+
     priors = arrived[:, :8].reshape(NOBS, members)
     given = arrived[:, 8].reshape(128, members)
     result = analyse(

time: 93.7 us -> 106 us (1.13)
  Pallas kernels: 26.2 us -> 36.8 us
  other arithmetic: 11.2 us -> 4.18 us
  waiting for transfers between devices: 10.2 us -> 15.3 us
  starting transfers between devices: 30.5 us -> 34.1 us
    ppermute x8, waiting for transfers between devices: 2.53 us -> 15.3 us  [the longest x4 12.5 us: along_x(): return lax.ppermute(value, 'gx', [(i, (i + step) % 16) for i in range(16)])]
    pallas_call x0 -> x4, Pallas kernels: none -> 10.7 us  [the longest x1 4.6 us: shards(): pl.pallas_call(forecast_kernel, out_shape=jax.ShapeDtypeStruct(cells.shap...]
    sub x2 -> x0, other arithmetic: 9.67 us -> none  [shards(): cells = cells + spread_term - carry_term]
    all_to_all x1, waiting for transfers between devices: 7.71 us -> 0.01 us  [shards(): arrived = lax.all_to_all(bundle, ('gx', 'gy'), 0, 0, tiled=True)]
    unnamed x28 -> x52, local copies, waits for them, and re-layouts: 6.57 us -> 9.67 us
    slice x4 -> x3, local copies, waits for them, and re-layouts: 2.41 us -> 0.06 us  [the longest x1 0.04 us: shards(): halo_e = along_x(late[:, :2], -1)]
    all_to_all x1, starting transfers between devices: 7.43 us -> 9.75 us  [shards(): arrived = lax.all_to_all(bundle, ('gx', 'gy'), 0, 0, tiled=True)]
    broadcast_in_dim x3 -> x0, local copies, waits for them, and re-layouts: 2.29 us -> none  [the longest x1 0.76 us: shards(): east_vel = jnp.repeat(east_speed, per_level, axis=0)[..., None]]
  transfers between devices with their start and end apart: 9 -> 9, of which waited for: 3 -> 4; matrix products, arithmetic and copies ran while one was open for 4% -> 2% of each run, Pallas kernels for 6% -> 9%
where the time goes in v2:
time: 106 us; the launch traced here: 105 us
  Pallas kernels  36.8 us (35%)
  starting transfers between devices  34.1 us (32%)
  waiting for transfers between devices  15.3 us (14%)
  local copies, waits for them, and re-layouts  14.1 us (13%)
  other arithmetic  4.18 us (4%)
    pallas_call x1, Pallas kernels, analyse(): pl.pallas_call(analysis_kernel, out_shape=jax.ShapeDtypeStruct(state.shap...  21 us
    ppermute x4, starting transfers between devices, along_y(): lax.ppermute(value, 'gy', [(i, i + step) for i in range(8) if 0 <= i + st...  13.6 us
    ppermute x4, waiting for transfers between devices, along_x(): return lax.ppermute(value, 'gx', [(i, (i + step) % 16) for i in range(16)])  12.5 us
    ppermute x4, starting transfers between devices, along_x(): return lax.ppermute(value, 'gx', [(i, (i + step) % 16) for i in range(16)])  10.7 us
    all_to_all x1, starting transfers between devices, shards(): arrived = lax.all_to_all(bundle, ('gx', 'gy'), 0, 0, tiled=True)  9.75 us
    unnamed x52, local copies, waits for them, and re-layouts  9.67 us
    pallas_call x1, Pallas kernels, plan(): pl.pallas_call(plan_kernel, out_shape=shapes, in_specs=[smem(), vmem()],...  5.11 us
    pallas_call x1, Pallas kernels, shards(): pl.pallas_call(forecast_kernel, out_shape=jax.ShapeDtypeStruct(cells.shap...  4.6 us
  transfers between devices with their start and end apart: 9, of which 4 were waited for; matrix products, arithmetic and copies ran while one was open for 2% of the time, Pallas kernels for 9%

profile of v2, /device:TPU:1, one launch (start us, length us, event | category | flops | bytes accessed | tf_op | source)
XLA Modules:
  0.0 104.8 jit_solution(8751789219041197433)
XLA Ops:
  0.0 0.8 multiply_add_fusion.1
  1.4 1.3 %multiply_add_fusion = (s32[1024]{0:T(1024)}, s32[1024]{0:T(1024)S(1)}) fusion(s32[1024]{0:T(1024)S(1)} %bitcast.36, s32[1024]{0:T(1024)} %param.16), kind=kLoop, calls=%fused_computation.8 | loop fusion | flops 17408 | bytes 16384 | tf_op jit(solution)/shard_map/add | solution.py:544
  2.7 2.9 %edges.1 = (f32[104,128]{1,0:T(8,128)}, f32[72,128]{1,0:T(8,128)}, f32[64,128]{1,0:T(8,128)}, f32[64,128]{1,0:T(8,128)}, f32[48,128]{1,0:T(8,128)}, /*index=5*/f32[48,128]{1,0:T(8,128)}) custom-call(s32[2]{0:T(128)} %pad_add_fusion.pos, s32[1024]{0:T(1024)} %get-tuple-element.46.code, f32[4096,128]{1,0:T(8,128)} %bitcast.25, f32[64,32]{1,0:T(8,128)} %bitcast.29, ...), custom_call_target="tpu_custom_call" | custom-call | tf_op jit(solution)/shard_map/edges/pallas_call | solution.py:548
  5.7 2.0 %collective-permute-start = (f32[64,128]{1,0:T(8,128)}, f32[64,128]{1,0:T(8,128)S(1)}, u32[]{:S(2)}, u32[]{:S(2)}) collective-permute-start(f32[64,128]{1,0:T(8,128)} %get-tuple-element.25), channel_id=1, source_target_pairs={{0,8},{8,16},{16,24},{24,32},{32,40},{40,48},{48,56},{56,64},{64,7... | collective-permute-start | bytes 98312 | tf_op jit(solution)/shard_map/ppermute | solution.py:539
  7.7 3.8 %collective-permute-start.1 = (f32[64,128]{1,0:T(8,128)}, f32[64,128]{1,0:T(8,128)S(1)}, u32[]{:S(2)}, u32[]{:S(2)}) collective-permute-start(f32[64,128]{1,0:T(8,128)} %get-tuple-element.26), channel_id=1, source_target_pairs={{0,120},{8,0},{16,8},{24,16},{32,24},{40,32},{48,40},{56,48},{64,5... | collective-permute-start | bytes 98312 | tf_op jit(solution)/shard_map/ppermute | solution.py:539
  11.5 1.5 %collective-permute-done.from_west.edge_w = f32[64,128]{1,0:T(8,128)S(1)} collective-permute-done((f32[64,128]{1,0:T(8,128)}, f32[64,128]{1,0:T(8,128)S(1)}, u32[]{:S(2)}, u32[]{:S(2)}) %collective-permute-start) | collective-permute-done | bytes 32800 | tf_op jit(solution)/shard_map/ppermute | solution.py:539
  13.6 1.5 %corners.1 = (f32[48,128]{1,0:T(8,128)}, f32[48,128]{1,0:T(8,128)}) custom-call(s32[2]{0:T(128)} %pad_add_fusion.pos, s32[1024]{0:T(1024)} %get-tuple-element.46.code, f32[48,128]{1,0:T(8,128)} %get-tuple-element.27.base_north, f32[48,128]{1,0:T(8,128)} %get-tuple-element.28.base_south, f32[64,128]{1,0:T(8,128)} %copy-done.6, f32[64,128]{1,0:T(8,128)} %copy-done.8), custom_call_target="tpu_custom_call" | custom-call | tf_op jit(solution)/shard_map/corners/pallas_call | solution.py:557
  15.1 5.1 %collective-permute-start.2 = (f32[48,128]{1,0:T(8,128)}, f32[48,128]{1,0:T(8,128)S(1)}, u32[]{:S(2)}, u32[]{:S(2)}) collective-permute-start(f32[48,128]{1,0:T(8,128)} %get-tuple-element.29), channel_id=1, source_target_pairs={{0,1},{1,2},{2,3},{3,4},{4,5},{5,6},{6,7},{8,9},{9,10},{10,11},{11... | collective-permute-start | bytes 73736 | tf_op jit(solution)/shard_map/ppermute | solution.py:542
  20.2 1.9 %collective-permute-start.3 = (f32[48,128]{1,0:T(8,128)}, f32[48,128]{1,0:T(8,128)S(1)}, u32[]{:S(2)}, u32[]{:S(2)}) collective-permute-start(f32[48,128]{1,0:T(8,128)} %get-tuple-element.30), channel_id=1, source_target_pairs={{1,0},{2,1},{3,2},{4,3},{5,4},{6,5},{7,6},{9,8},{10,9},{11,10},{12... | collective-permute-start | bytes 73736 | tf_op jit(solution)/shard_map/ppermute | solution.py:542
  22.8 2.7 %collective-permute-done.3.from_north.edge_n = f32[48,128]{1,0:T(8,128)S(1)} collective-permute-done((f32[48,128]{1,0:T(8,128)}, f32[48,128]{1,0:T(8,128)S(1)}, u32[]{:S(2)}, u32[]{:S(2)}) %collective-permute-start.3) | collective-permute-done | bytes 24608 | tf_op jit(solution)/shard_map/ppermute | solution.py:542
  26.1 1.6 %priors.1 = f32[9,128]{1,0:T(8,128)} custom-call(s32[2]{0:T(128)} %pad_add_fusion.pos, s32[1024]{0:T(1024)} %get-tuple-element.46.code, f32[104,128]{1,0:T(8,128)} %get-tuple-element.23.own, f32[72,128]{1,0:T(8,128)} %get-tuple-element.24.own_coef, f32[64,128]{1,0:T(8,128)} %copy-done.6, f32[64,128]{1,0:T(8,128)} %copy-done.8, f32[48,128]{1,0:T(8,128)} %copy-done.14, ...), custom_call_target="tpu_custom_call" | custom-call | tf_op jit(solution)/shard_map/priors/pallas_call | solution.py:568
  27.8 1.8 %broadcast_in_dim.2 = f32[128,9,1,128]{3,2,1,0:T(1,128)} broadcast(f32[9,128]{1,0:T(8,128)} %priors.1), dimensions={1,3} | broadcast | bytes 594432 | tf_op jit(solution)/shard_map/broadcast_in_dim | solution.py:578
  29.6 9.8 %all-to-all-start = ((f32[128,9,1,128]{3,2,1,0:T(1,128)}), f32[128,9,1,128]{3,2,1,0:T(1,128)}, u32[]{:S(2)}, u32[]{:S(2)}) async-start(f32[128,9,1,128]{3,2,1,0:T(1,128)} %broadcast_in_dim.2), calls=%async_computation | async-start | bytes 1179648 | tf_op jit(solution)/shard_map/all_to_all | solution.py:579
  39.5 4.9 %collective-permute-start.5 = (f32[8,2,32,128]{3,2,1,0:T(8,128)S(1)}, f32[8,2,32,128]{3,2,1,0:T(8,128)S(1)}, u32[]{:S(2)}, u32[]{:S(2)}) collective-permute-start(f32[8,2,32,128]{3,2,1,0:T(8,128)S(1)} %get-tuple-element.41), channel_id=1, source_target_pairs={{0,120},{8,0},{16,8},{24,16},{32,24},{40,32},{48,40},{56,48},{64,5... | collective-permute-start | bytes 786440 | tf_op jit(solution)/shard_map/ppermute | solution.py:539
  44.4 8.1 %collective-permute-done.5.halo_e = f32[8,2,32,128]{3,2,1,0:T(8,128)S(1)} collective-permute-done((f32[8,2,32,128]{3,2,1,0:T(8,128)S(1)}, f32[8,2,32,128]{3,2,1,0:T(8,128)S(1)}, u32[]{:S(2)}, u32[]{:S(2)}) %collective-permute-start.5) | collective-permute-done | bytes 262176 | tf_op jit(solution)/shard_map/ppermute | solution.py:539
  52.5 2.9 %collective-permute-done.4.halo_w = f32[8,2,32,128]{3,2,1,0:T(8,128)S(1)} collective-permute-done((f32[8,2,32,128]{3,2,1,0:T(8,128)S(1)}, f32[8,2,32,128]{3,2,1,0:T(8,128)S(1)}, u32[]{:S(2)}, u32[]{:S(2)}) %collective-permute-start.4) | collective-permute-done | bytes 262176 | tf_op jit(solution)/shard_map/ppermute | solution.py:539
  55.4 0.8 pad_maximum_fusion
  56.2 3.1 %collective-permute-start.7 = (f32[8,18,2,128]{3,2,1,0:T(2,128)}, f32[8,18,2,128]{3,2,1,0:T(2,128)}, u32[]{:S(2)}, u32[]{:S(2)}) collective-permute-start(f32[8,18,2,128]{3,2,1,0:T(2,128)} %get-tuple-element.39), channel_id=1, source_target_pairs={{1,0},{2,1},{3,2},{4,3},{5,4},{6,5},{7,6},{9,8},{10,9},{11,10},{12... | collective-permute-start | bytes 442376 | tf_op jit(solution)/shard_map/ppermute | solution.py:542
  59.4 3.5 %collective-permute-start.6 = (f32[8,18,2,128]{3,2,1,0:T(2,128)}, f32[8,18,2,128]{3,2,1,0:T(2,128)}, u32[]{:S(2)}, u32[]{:S(2)}) collective-permute-start(f32[8,18,2,128]{3,2,1,0:T(2,128)} %get-tuple-element.40), channel_id=1, source_target_pairs={{0,1},{1,2},{2,3},{3,4},{4,5},{5,6},{6,7},{8,9},{9,10},{10,11},{11... | collective-permute-start | bytes 442376 | tf_op jit(solution)/shard_map/ppermute | solution.py:542
  63.6 5.1 %plan.1 = (bf16[1024,1024]{1,0:T(8,128)(2,1)}, f32[1536,256]{1,0:T(8,128)}, bf16[4,256,256]{2,1,0:T(8,128)(2,1)}, f32[4,8,256]{2,1,0:T(8,128)}, bf16[1024,128]{1...) custom-call(s32[2]{0:T(128)} %pad_add_fusion.pos, s32[8,1024]{1,0:T(8,128)} %stack.35.table), custom_call_target="tpu_custom_call" | custom-call | tf_op jit(solution)/shard_map/plan/pallas_call | solution.py:476
  68.8 0.8 copy-done.13
  69.6 0.7 copy-done.15
  70.3 0.7 copy-done.17
  71.1 4.6 %forecast.1 = f32[8,16,32,128]{3,2,1,0:T(8,128)S(1)} custom-call(f32[8,16,32,128]{3,2,1,0:T(8,128)S(1)} %copy-done, f32[64,32]{1,0:T(8,128)S(1)} %bitcast.30, f32[64,32]{1,0:T(8,128)S(1)} %bitcast.32, f32[64,32]{1,0:T(8,128)S(1)} %bitcast.34, f32[8,2,32,128]{3,2,1,0:T(8,128)S(1)} %collective-permute-done.4.halo_w, ...), custom_call_target="tpu_custom_call" | custom-call | tf_op jit(solution)/shard_map/forecast/pallas_call | solution.py:586
  75.7 1.3 %copy-done.1 = f32[8,16,32,128]{3,2,1,0:T(8,128)} copy-done((f32[8,16,32,128]{3,2,1,0:T(8,128)}, f32[8,16,32,128]{3,2,1,0:T(8,128)S(1)}, u32[]{:S(2)}) %copy-start.1) | copy-done | bytes 2097176
  77.0 0.8 slice.43
  77.8 1.1 %slice.42 = f32[128,8,1,128]{3,2,1,0:T(1,128)S(1)} slice(f32[128,9,1,128]{3,2,1,0:T(1,128)} %all-to-all-done), slice={[0:128], [0:8], [0:1], [0:128]} | slice | bytes 1048576 | tf_op jit(solution)/shard_map/slice | solution.py:601
  79.0 1.6 %copy-done.2 = f32[8,16,32,128]{3,2,1,0:T(8,128)S(1)} copy-done((f32[8,16,32,128]{3,2,1,0:T(8,128)S(1)}, f32[8,16,32,128]{3,2,1,0:T(8,128)}, u32[]{:S(2)}) %copy-start.2) | copy-done | bytes 2097176
  80.5 1.4 %copy-done.3 = f32[1536,256]{1,0:T(8,128)S(1)} copy-done((f32[1536,256]{1,0:T(8,128)S(1)}, f32[1536,256]{1,0:T(8,128)}, u32[]{:S(2)}) %copy-start.3) | copy-done | bytes 1572888
  82.0 1.0 copy-done.5
  83.0 0.8 copy-done.18
  83.8 21.0 %analyse.1 = f32[4096,128]{1,0:T(8,128)} custom-call(s32[2]{0:T(128)S(1)} %copy-done.19, s32[4]{0:T(128)S(1)} %copy-done.20, f32[1024,128]{1,0:T(8,128)S(1)} %bitcast.27, f32[128,128]{1,0:T(8,128)S(1)} %bitcast.28, f32[4096,128]{1,0:T(8,128)S(1)} %bitcast.26, bf16[1024,1024]{1,0:T(8,128)(2,1)} %get-tuple-element.33.perm, f32[1536,256]{1,0:T(8,128)S(1)} %copy-done.3, ...), custom_call_target="tpu_custom_call" | custom-call | tf_op jit(solution)/shard_map/analyse/pallas_call | solution.py:486
  (57 shorter events, 3.3 us)
Async XLA Ops:
  0.0 22.1 %copy-start.24 = (f32[1,1,32]{2,1,0:T(1,128)S(1)}, f32[1,1,32]{2,1,0:T(1,128)}, u32[]{:S(2)}) copy-start(f32[1,1,32]{2,1,0:T(1,128)} %param.21) | copy-start | bytes 388
  0.0 22.1 %copy-start.25 = (f32[1,1,32]{2,1,0:T(1,128)S(1)}, f32[1,1,32]{2,1,0:T(1,128)}, u32[]{:S(2)}) copy-start(f32[1,1,32]{2,1,0:T(1,128)} %param.20) | copy-start | bytes 388
  2.7 36.6 %copy-start = (f32[8,16,32,128]{3,2,1,0:T(8,128)S(1)}, f32[8,16,32,128]{3,2,1,0:T(8,128)}, u32[]{:S(2)}) copy-start(f32[8,16,32,128]{3,2,1,0:T(8,128)} %cells) | copy-start | bytes 6291460
  5.7 7.3 %collective-permute-start = (f32[64,128]{1,0:T(8,128)}, f32[64,128]{1,0:T(8,128)S(1)}, u32[]{:S(2)}, u32[]{:S(2)}) collective-permute-start(f32[64,128]{1,0:T(8,128)} %get-tuple-element.25), channel_id=1, source_target_pairs={{0,8},{8,16},{16,24},{24,32},{32,40},{40,48},{48,56},{56,64},{64,7... | collective-permute-start | bytes 98312 | tf_op jit(solution)/shard_map/ppermute | solution.py:539
  7.7 5.2 %collective-permute-start.1 = (f32[64,128]{1,0:T(8,128)}, f32[64,128]{1,0:T(8,128)S(1)}, u32[]{:S(2)}, u32[]{:S(2)}) collective-permute-start(f32[64,128]{1,0:T(8,128)} %get-tuple-element.26), channel_id=1, source_target_pairs={{0,120},{8,0},{16,8},{24,16},{32,24},{40,32},{48,40},{56,48},{64,5... | collective-permute-start | bytes 98312 | tf_op jit(solution)/shard_map/ppermute | solution.py:539
  15.1 7.7 %collective-permute-start.2 = (f32[48,128]{1,0:T(8,128)}, f32[48,128]{1,0:T(8,128)S(1)}, u32[]{:S(2)}, u32[]{:S(2)}) collective-permute-start(f32[48,128]{1,0:T(8,128)} %get-tuple-element.29), channel_id=1, source_target_pairs={{0,1},{1,2},{2,3},{3,4},{4,5},{5,6},{6,7},{8,9},{9,10},{10,11},{11... | collective-permute-start | bytes 73736 | tf_op jit(solution)/shard_map/ppermute | solution.py:542
  20.2 5.4 %collective-permute-start.3 = (f32[48,128]{1,0:T(8,128)}, f32[48,128]{1,0:T(8,128)S(1)}, u32[]{:S(2)}, u32[]{:S(2)}) collective-permute-start(f32[48,128]{1,0:T(8,128)} %get-tuple-element.30), channel_id=1, source_target_pairs={{1,0},{2,1},{3,2},{4,3},{5,4},{6,5},{7,6},{9,8},{10,9},{11,10},{12... | collective-permute-start | bytes 73736 | tf_op jit(solution)/shard_map/ppermute | solution.py:542
  22.8 2.8 %copy-start.14 = (f32[48,128]{1,0:T(8,128)}, f32[48,128]{1,0:T(8,128)S(1)}, u32[]{:S(2)}) copy-start(f32[48,128]{1,0:T(8,128)S(1)} %collective-permute-done.2.from_south.edge_s) | copy-start | bytes 73732
  29.6 47.4 %all-to-all-start = ((f32[128,9,1,128]{3,2,1,0:T(1,128)}), f32[128,9,1,128]{3,2,1,0:T(1,128)}, u32[]{:S(2)}, u32[]{:S(2)}) async-start(f32[128,9,1,128]{3,2,1,0:T(1,128)} %broadcast_in_dim.2), calls=%async_computation | async-start | bytes 1179648 | tf_op jit(solution)/shard_map/all_to_all | solution.py:579
  39.3 23.5 %copy-start.21 = (s32[1024]{0:T(1024)S(1)}, s32[1024]{0:T(1024)}, u32[]{:S(2)}) copy-start(s32[1024]{0:T(1024)} %param.17) | copy-start | bytes 12292
  39.4 23.5 %copy-start.22 = (s32[1024]{0:T(1024)S(1)}, s32[1024]{0:T(1024)}, u32[]{:S(2)}) copy-start(s32[1024]{0:T(1024)} %param.18) | copy-start | bytes 12292
  39.4 23.5 %copy-start.23 = (s32[1024]{0:T(1024)S(1)}, s32[1024]{0:T(1024)}, u32[]{:S(2)}) copy-start(s32[1024]{0:T(1024)} %param.19) | copy-start | bytes 12292
  39.4 29.3 %copy-start.7 = (f32[64,128]{1,0:T(8,128)S(1)}, f32[64,128]{1,0:T(8,128)}, u32[]{:S(2)}) copy-start(f32[64,128]{1,0:T(8,128)} %copy-done.6) | copy-start | bytes 98308
  39.4 29.3 %copy-start.9 = (f32[64,128]{1,0:T(8,128)S(1)}, f32[64,128]{1,0:T(8,128)}, u32[]{:S(2)}) copy-start(f32[64,128]{1,0:T(8,128)} %copy-done.8) | copy-start | bytes 98308
  39.4 29.3 %copy-start.11 = (f32[4,16,32]{2,1,0:T(8,128)S(1)}, f32[4,16,32]{2,1,0:T(8,128)}, u32[]{:S(2)}) copy-start(f32[4,16,32]{2,1,0:T(8,128)} %param.12) | copy-start | bytes 24580
  39.4 29.3 %copy-start.12 = (f32[4,16,32]{2,1,0:T(8,128)S(1)}, f32[4,16,32]{2,1,0:T(8,128)}, u32[]{:S(2)}) copy-start(f32[4,16,32]{2,1,0:T(8,128)} %param.13) | copy-start | bytes 24580
  39.5 13.0 %collective-permute-start.5 = (f32[8,2,32,128]{3,2,1,0:T(8,128)S(1)}, f32[8,2,32,128]{3,2,1,0:T(8,128)S(1)}, u32[]{:S(2)}, u32[]{:S(2)}) collective-permute-start(f32[8,2,32,128]{3,2,1,0:T(8,128)S(1)} %get-tuple-element.41), channel_id=1, source_target_pairs={{0,120},{8,0},{16,8},{24,16},{32,24},{40,32},{48,40},{56,48},{64,5... | collective-permute-start | bytes 786440 | tf_op jit(solution)/shard_map/ppermute | solution.py:539
  44.4 11.1 %collective-permute-start.4 = (f32[8,2,32,128]{3,2,1,0:T(8,128)S(1)}, f32[8,2,32,128]{3,2,1,0:T(8,128)S(1)}, u32[]{:S(2)}, u32[]{:S(2)}) collective-permute-start(f32[8,2,32,128]{3,2,1,0:T(8,128)S(1)} %get-tuple-element.42), channel_id=1, source_target_pairs={{0,8},{8,16},{16,24},{24,32},{32,40},{40,48},{48,56},{56,64},{64,7... | collective-permute-start | bytes 786440 | tf_op jit(solution)/shard_map/ppermute | solution.py:539
  56.2 12.5 %collective-permute-start.7 = (f32[8,18,2,128]{3,2,1,0:T(2,128)}, f32[8,18,2,128]{3,2,1,0:T(2,128)}, u32[]{:S(2)}, u32[]{:S(2)}) collective-permute-start(f32[8,18,2,128]{3,2,1,0:T(2,128)} %get-tuple-element.39), channel_id=1, source_target_pairs={{1,0},{2,1},{3,2},{4,3},{5,4},{6,5},{7,6},{9,8},{10,9},{11,10},{12... | collective-permute-start | bytes 442376 | tf_op jit(solution)/shard_map/ppermute | solution.py:542
  59.4 9.3 %collective-permute-start.6 = (f32[8,18,2,128]{3,2,1,0:T(2,128)}, f32[8,18,2,128]{3,2,1,0:T(2,128)}, u32[]{:S(2)}, u32[]{:S(2)}) collective-permute-start(f32[8,18,2,128]{3,2,1,0:T(2,128)} %get-tuple-element.40), channel_id=1, source_target_pairs={{0,1},{1,2},{2,3},{3,4},{4,5},{5,6},{6,7},{8,9},{9,10},{10,11},{11... | collective-permute-start | bytes 442376 | tf_op jit(solution)/shard_map/ppermute | solution.py:542
  63.6 15.4 %copy-start.19 = (s32[2]{0:T(128)S(1)}, s32[2]{0:T(128)}, u32[]{:S(2)}) copy-start(s32[2]{0:T(128)} %pad_add_fusion.pos) | copy-start | bytes 28
  68.7 10.2 %copy-start.4 = (bf16[4,256,256]{2,1,0:T(8,128)(2,1)S(1)}, bf16[4,256,256]{2,1,0:T(8,128)(2,1)}, u32[]{:S(2)}) copy-start(bf16[4,256,256]{2,1,0:T(8,128)(2,1)} %get-tuple-element.35.select) | copy-start | bytes 1572868
  68.7 10.2 %copy-start.10 = (bf16[1024,128]{1,0:T(8,128)(2,1)S(1)}, bf16[1024,128]{1,0:T(8,128)(2,1)}, u32[]{:S(2)}) copy-start(bf16[1024,128]{1,0:T(8,128)(2,1)} %get-tuple-element.37.source) | copy-start | bytes 786436
  68.8 0.8 copy-start.13
  69.6 0.7 copy-start.15
  70.3 0.7 copy-start.17
  71.1 7.9 %copy-start.20 = (s32[4]{0:T(128)S(1)}, s32[4]{0:T(128)}, u32[]{:S(2)}) copy-start(s32[4]{0:T(128)} %get-tuple-element.22.counts) | copy-start | bytes 52
  75.7 1.3 %copy-start.1 = (f32[8,16,32,128]{3,2,1,0:T(8,128)}, f32[8,16,32,128]{3,2,1,0:T(8,128)S(1)}, u32[]{:S(2)}) copy-start(f32[8,16,32,128]{3,2,1,0:T(8,128)S(1)} %forecast.1) | copy-start | bytes 6291460
  79.0 1.6 %copy-start.2 = (f32[8,16,32,128]{3,2,1,0:T(8,128)S(1)}, f32[8,16,32,128]{3,2,1,0:T(8,128)}, u32[]{:S(2)}) copy-start(f32[8,16,32,128]{3,2,1,0:T(8,128)} %copy-done.1) | copy-start | bytes 6291460
  80.5 1.4 %copy-start.3 = (f32[1536,256]{1,0:T(8,128)S(1)}, f32[1536,256]{1,0:T(8,128)}, u32[]{:S(2)}) copy-start(f32[1536,256]{1,0:T(8,128)} %get-tuple-element.34.obs_weight) | copy-start | bytes 4718596
  82.0 1.0 copy-start.5
  83.0 0.8 copy-start.18
  (3 other events, 1.8 us)

commit v3 on v2

--- a/solution.py
+++ b/solution.py
@@ -105,24 +105,45 @@
 
 
 def analysis_kernel(
-    pos, counts, priors, given, state, perm, obs_weight, select, slots, source, place,
-    out, rows, near, left, right,
+    pos, counts, arrived, slots, perm_far, source_far, place_far, weight_far, select_far, state_far,
+    out, rows, near, left, right, perm, source, place, obs_weight, select, state, arrivals,
 ):
     here_x = pos[0]
     here_y = pos[1]
-    high, low = halves(priors[...])
+    copies = [
+        pltpu.make_async_copy(far, close, arrivals.at[index])
+        for index, (far, close) in enumerate(
+            (
+                (perm_far, perm),
+                (source_far, source),
+                (place_far, place),
+                (weight_far, obs_weight),
+                (select_far, select),
+                (state_far, state),
+            )
+        )
+    ]
+    for copy in copies:
+        copy.start()
+    for k in range(8):
+        rows[pl.ds(k, 128, stride=8), :] = arrived[pl.ds(k, 128, stride=9), :]
+    given = arrived[pl.ds(8, 128, stride=9), :]
+    high, low = halves(rows[...])
     both = jnp.concatenate([high, low], axis=1)
+    copies[0].wait()
     for panel in range(PANELS):
         span = slice(panel * PANEL, (panel + 1) * PANEL)
         moved = dot(perm[span, :], both)
         rows[span, :] = moved[:, :MEM] + moved[:, MEM:]
-    v_high = given[...].astype(BF16)
-    rest = given[...] - v_high.astype(F32)
+    v_high = given.astype(BF16)
+    rest = given - v_high.astype(F32)
     v_mid = rest.astype(BF16)
     v_low = (rest - v_mid.astype(F32)).astype(BF16)
     v_all = jnp.concatenate([v_high, v_mid, v_low], axis=1)
     lanes = lax.broadcasted_iota(jnp.int32, (PANEL, 128), 1).astype(F32)
 
+    copies[1].wait()
+    copies[2].wait()
     first = 0
     for panel in range(PANELS):
         span = slice(panel * PANEL, (panel + 1) * PANEL)
@@ -150,12 +171,16 @@
                 [jnp.concatenate([q_high, q_high], axis=1), jnp.concatenate([q_low, q_low], axis=1)], axis=0
             )
             cov = dot(jnp.concatenate([l_high, l_low], axis=1), q_both, NT)
+            if panel == 0:
+                copies[3].wait()
             local = (cov[:, :PANEL] + cov[:, PANEL:]) * obs_weight[first : first + count, :]
             g_high, g_low = halves(local)
             h_both = jnp.concatenate([h_high, h_low], axis=1)
             step = dot(g_high, h_both) + dot(g_low, h_both)
             rows[begin:, :] = later + (step[:, :MEM] + step[:, MEM:])
             first += count
+        if panel == 0:
+            copies[4].wait()
         packed = dot(select[panel], jnp.concatenate([q_high, q_low, h_high, h_low], axis=1)).astype(BF16)
         for part in range(2):
             half = packed[part * 128 : (part + 1) * 128]
@@ -176,6 +201,8 @@
         for col in range(CX):
             close = jnp.maximum(0.0, part_x[col : col + 1] - part_y)
             near[panel, col * CY : (col + 1) * CY, :] = close * close * (1.0 / (MEM - 1))
+
+    copies[5].wait()
 
     @pl.loop(0, COMP)
     def _(comp):
@@ -261,6 +288,9 @@
             target[24 + k : 25 + k, :] = cell(comp, x, clip_y(y + shift * (CY - 2)))
     for target, edge in ((to_east, CX - 1), (to_west, 0)):
         target[48:64, :] = jnp.zeros((16, MEM), F32)
+        for comp in range(COMP):
+            target[64 + comp : 65 + comp, :] = cell(comp, edge, CY - 1)
+            target[72 + comp : 73 + comp, :] = cell(comp, edge, 0)
         for c in range(3):
             for level in range(4):
                 at = 48 + c * 4 + level
@@ -292,7 +322,10 @@
         x = jnp.zeros((8, MEM), jnp.int32)
         for k in range(8):
             x = jnp.where(row == k, code[begin + k] & 15, x)
-        target[...] = base[...]
+        target[0:48, :] = base[...]
+        corners = 64 if shift == 1 else 72
+        target[48:56, :] = from_west[corners : corners + 8, :]
+        target[56:64, :] = from_east[corners : corners + 8, :]
         target[0:8, :] = jnp.where(x == 0, from_west[first : first + 8, :], base[0:8, :])
         target[16:24, :] = jnp.where(x == CX - 1, from_east[first : first + 8, :], base[16:24, :])
 
@@ -405,8 +438,10 @@
             before[which, 2 : 2 + CX, mid_rows, :] = cells[comp]
             before[which, 0:2, mid_rows, :] = halo_w[comp]
             before[which, 2 + CX : 4 + CX, mid_rows, :] = halo_e[comp]
-            before[which, 1 : 3 + CX, 7, :] = halo_s[comp, :, 1, :]
-            before[which, 1 : 3 + CX, 8 + CY, :] = halo_n[comp, :, 0, :]
+            for rim, edge, inner, target in ((halo_s, edge_s, 1, 7), (halo_n, edge_n, 0, 8 + CY)):
+                before[which, 2 : 2 + CX, target, :] = rim[comp, :, inner, :]
+                before[which, 1, target : target + 1, :] = edge[48 + comp : 49 + comp, :]
+                before[which, 2 + CX, target : target + 1, :] = edge[56 + comp : 57 + comp, :]
         for col in range(-1, CX + 1):
             lane = CX if col < 0 else (CX + 1 if col == CX else col)
             u, v, nu = (
@@ -422,9 +457,9 @@
                     before[which, at, 7 : 7 + CY, :],
                     u, v, nu,
                 )
-        for rim, edge, inner, outer, inside, target in (
-            (halo_s, edge_s, 1, 0, 0, 7),
-            (halo_n, edge_n, 0, 1, CY - 1, 8 + CY),
+        for rim, edge, outer, inside, target in (
+            (halo_s, edge_s, 0, 0, 7),
+            (halo_n, edge_n, 1, CY - 1, 8 + CY),
         ):
             u, v, nu = (
                 jnp.broadcast_to(edge[32:48, c * 4 + level : c * 4 + level + 1], (CX, MEM))
@@ -432,10 +467,10 @@
             )
             for which in range(2):
                 comp = level * 2 + which
-                mid = rim[comp, 1 : 1 + CX, inner, :]
-                e = rim[comp, 2 : 2 + CX, inner, :]
-                w = rim[comp, 0:CX, inner, :]
-                far = rim[comp, 1 : 1 + CX, outer, :]
+                mid = before[which, 2 : 2 + CX, target, :]
+                e = before[which, 3 : 3 + CX, target, :]
+                w = before[which, 1 : 1 + CX, target, :]
+                far = rim[comp, :, outer, :]
                 close = cells[comp, :, inside, :]
                 n, s = (close, far) if target == 7 else (far, close)
                 after[which, 2 : 2 + CX, target, :] = stencil(mid, e, w, n, s, u, v, nu)
@@ -482,21 +517,23 @@
     )(pos, table)
 
 
-def analyse(pos, counts, priors, given, state, *planned):
+def analyse(pos, counts, arrived, slots, *far):
     return pl.pallas_call(
         analysis_kernel,
-        out_shape=jax.ShapeDtypeStruct(state.shape, F32),
-        in_specs=[smem(), smem()] + [vmem()] * (3 + len(planned)),
+        out_shape=jax.ShapeDtypeStruct(far[-1].shape, F32),
+        in_specs=[smem(), smem(), vmem(), vmem()] + [pl.BlockSpec(memory_space=pl.ANY)] * len(far),
         out_specs=vmem(),
         scratch_shapes=[
             pltpu.VMEM((NOBS, MEM), F32),
             pltpu.VMEM((PANELS, BLOCK, PANEL), F32),
             pltpu.VMEM((PANELS, 2, PANEL, PANEL), BF16),
             pltpu.VMEM((PANELS, 2, PANEL, PANEL), BF16),
-        ],
-        compiler_params=pltpu.CompilerParams(vmem_limit_bytes=48 << 20),
+        ]
+        + [pltpu.VMEM(array.shape, array.dtype) for array in far]
+        + [pltpu.SemaphoreType.DMA((len(far),))],
+        compiler_params=pltpu.CompilerParams(vmem_limit_bytes=40 << 20),
         name="analyse",
-    )(pos, counts, priors, given, state, *planned)
+    )(pos, counts, arrived, slots, *far)
 
 
 def shards(
@@ -547,16 +584,21 @@
     speeds = [field.reshape(-1, width_y) for field in (east_speed, north_speed, diffusion)]
     own, own_coef, to_east, to_west, base_north, base_south = pl.pallas_call(
         edge_kernel,
-        out_shape=(rows(104), rows(72), rows(64), rows(64), rows(48), rows(48)),
+        out_shape=(rows(104), rows(72), rows(80), rows(80), rows(48), rows(48)),
         in_specs=[smem(), smem()] + [vmem()] * 4,
         out_specs=[vmem()] * 6,
         name="edges",
     )(pos, code, flat, *speeds)
     from_west = along_x(to_east, 1)
     from_east = along_x(to_west, -1)
+    from_west, from_east, late = lax.optimization_barrier((from_west, from_east, cells))
+    halo_w = along_x(late[:, CX - 2 :], 1)
+    halo_e = along_x(late[:, :2], -1)
+    halo_s = along_y(late[:, :, CY - 2 :], 1)
+    halo_n = along_y(late[:, :, :2], -1)
     to_north, to_south = pl.pallas_call(
         corner_kernel,
-        out_shape=(rows(48), rows(48)),
+        out_shape=(rows(64), rows(64)),
         in_specs=[smem(), smem()] + [vmem()] * 4,
         out_specs=[vmem()] * 2,
         name="corners",
@@ -574,15 +616,9 @@
         name="priors",
     )(pos, code, own, own_coef, from_west, from_east, from_south, from_north, held)
 
-    bundle, late = lax.optimization_barrier((bundle, cells))
     bundle = jnp.broadcast_to(bundle.reshape(1, 9, 1, members), (128, 9, 1, members))
     arrived = lax.all_to_all(bundle, ("gx", "gy"), 0, 0, tiled=True)
 
-    halo_w = along_x(late[:, CX - 2 :], 1)
-    halo_e = along_x(late[:, :2], -1)
-    wide = jnp.concatenate([halo_w[:, 1:], late, halo_e[:, :1]], axis=1)
-    halo_s = along_y(wide[:, :, CY - 2 :], 1)
-    halo_n = along_y(wide[:, :, :2], -1)
     state = pl.pallas_call(
         forecast_kernel,
         out_shape=jax.ShapeDtypeStruct(cells.shape, F32),
@@ -595,13 +631,11 @@
         ],
         compiler_params=pltpu.CompilerParams(vmem_limit_bytes=32 << 20),
         name="forecast",
-    )(late, *speeds, halo_w, halo_e, halo_s, halo_n, from_west, from_east, from_south, from_north)
+    )(cells, *speeds, halo_w, halo_e, halo_s, halo_n, from_west, from_east, from_south, from_north)
     state = state.reshape(-1, members)
 
-    priors = arrived[:, :8].reshape(NOBS, members)
-    given = arrived[:, 8].reshape(128, members)
     result = analyse(
-        pos, counts, priors, given, state, perm, obs_weight, select, slots, source, place
+        pos, counts, arrived.reshape(-1, members), slots, perm, source, place, obs_weight, select, state
     )
     return result.reshape(comps, zonal_extent, width_y, members)
 

time: 106 us -> 98.9 us (0.933)
  waiting for transfers between devices: 15.3 us -> 4.38 us
  local copies, waits for them, and re-layouts: 14.1 us -> 19.2 us
  starting transfers between devices: 34.1 us -> 33 us
    ppermute x4, waiting for transfers between devices: 12.5 us -> 1.53 us  [along_x(): return lax.ppermute(value, 'gx', [(i, (i + step) % 16) for i in range(16)])]
    unnamed x52 -> x54, local copies, waits for them, and re-layouts: 9.67 us -> 15.1 us
    slice x4 -> x1, local copies, waits for them, and re-layouts: 1.94 us -> 0.82 us  [shards(): halo_n = along_y(late[:, :, :2], -1)]
  transfers between devices with their start and end apart: 9 -> 9, of which waited for: 4 -> 2; matrix products, arithmetic and copies ran while one was open for 2% -> 3% of each run, Pallas kernels for 9% -> 10%
where the time goes in v3:
time: 98.9 us; the launch traced here: 97.8 us
  Pallas kernels  37.4 us (38%)
  starting transfers between devices  33 us (33%)
  local copies, waits for them, and re-layouts  19.2 us (19%)
  waiting for transfers between devices  4.38 us (4%)
  other arithmetic  3.36 us (3%)
    pallas_call x1, Pallas kernels, analyse(): pl.pallas_call(analysis_kernel, out_shape=jax.ShapeDtypeStruct(far[-1].sh...  21.5 us
    unnamed x54, local copies, waits for them, and re-layouts  15.1 us
    ppermute x4, starting transfers between devices, along_y(): lax.ppermute(value, 'gy', [(i, i + step) for i in range(8) if 0 <= i + st...  12.9 us
    ppermute x4, starting transfers between devices, along_x(): return lax.ppermute(value, 'gx', [(i, (i + step) % 16) for i in range(16)])  10.7 us
    all_to_all x1, starting transfers between devices, shards(): arrived = lax.all_to_all(bundle, ('gx', 'gy'), 0, 0, tiled=True)  9.36 us
    pallas_call x1, Pallas kernels, plan(): pl.pallas_call(plan_kernel, out_shape=shapes, in_specs=[smem(), vmem()],...  5.16 us
    pallas_call x1, Pallas kernels, shards(): pl.pallas_call(forecast_kernel, out_shape=jax.ShapeDtypeStruct(cells.shap...  4.69 us
    pallas_call x1, Pallas kernels, shards(): pl.pallas_call(edge_kernel, out_shape=(rows(104), rows(72), rows(80), row...  2.94 us
  transfers between devices with their start and end apart: 9, of which 2 were waited for; matrix products, arithmetic and copies ran while one was open for 3% of the time, Pallas kernels for 10%

profile of v3, /device:TPU:1, one launch (start us, length us, event | category | flops | bytes accessed | tf_op | source)
XLA Modules:
  0.0 97.8 jit_solution(4164709358150326542)
XLA Ops:
  0.0 0.8 multiply_add_fusion.1
  1.4 1.3 %multiply_add_fusion = (s32[1024]{0:T(1024)}, s32[1024]{0:T(1024)S(1)}) fusion(s32[1024]{0:T(1024)S(1)} %bitcast.30, s32[1024]{0:T(1024)} %param.16), kind=kLoop, calls=%fused_computation.5 | loop fusion | flops 17408 | bytes 16384 | tf_op jit(solution)/shard_map/add | solution.py:581
  2.7 2.9 %edges.1 = (f32[104,128]{1,0:T(8,128)}, f32[72,128]{1,0:T(8,128)}, f32[80,128]{1,0:T(8,128)}, f32[80,128]{1,0:T(8,128)}, f32[48,128]{1,0:T(8,128)}, /*index=5*/f32[48,128]{1,0:T(8,128)}) custom-call(s32[2]{0:T(128)} %pad_add_fusion.pos, s32[1024]{0:T(1024)} %get-tuple-element.48.code, f32[4096,128]{1,0:T(8,128)} %bitcast.20, f32[64,32]{1,0:T(8,128)} %bitcast.23, ...), custom_call_target="tpu_custom_call" | custom-call | tf_op jit(solution)/shard_map/edges/pallas_call | solution.py:585
  5.7 2.1 %collective-permute-start = (f32[80,128]{1,0:T(8,128)}, f32[80,128]{1,0:T(8,128)S(1)}, u32[]{:S(2)}, u32[]{:S(2)}) collective-permute-start(f32[80,128]{1,0:T(8,128)} %get-tuple-element.26), channel_id=1, source_target_pairs={{0,8},{8,16},{16,24},{24,32},{32,40},{40,48},{48,56},{56,64},{64,7... | collective-permute-start | bytes 122888 | tf_op jit(solution)/shard_map/ppermute | solution.py:576
  7.8 3.8 %collective-permute-start.1 = (f32[80,128]{1,0:T(8,128)}, f32[80,128]{1,0:T(8,128)S(1)}, u32[]{:S(2)}, u32[]{:S(2)}) collective-permute-start(f32[80,128]{1,0:T(8,128)} %get-tuple-element.27), channel_id=1, source_target_pairs={{0,120},{8,0},{16,8},{24,16},{32,24},{40,32},{48,40},{56,48},{64,5... | collective-permute-start | bytes 122888 | tf_op jit(solution)/shard_map/ppermute | solution.py:576
  11.6 1.5 %collective-permute-done.from_west.edge_w = f32[80,128]{1,0:T(8,128)S(1)} collective-permute-done((f32[80,128]{1,0:T(8,128)}, f32[80,128]{1,0:T(8,128)S(1)}, u32[]{:S(2)}, u32[]{:S(2)}) %collective-permute-start) | collective-permute-done | bytes 40992 | tf_op jit(solution)/shard_map/ppermute | solution.py:576
  13.7 1.5 %corners.1 = (f32[64,128]{1,0:T(8,128)}, f32[64,128]{1,0:T(8,128)}) custom-call(s32[2]{0:T(128)} %pad_add_fusion.pos, s32[1024]{0:T(1024)} %get-tuple-element.48.code, f32[48,128]{1,0:T(8,128)} %get-tuple-element.30.base_north, f32[48,128]{1,0:T(8,128)} %get-tuple-element.31.base_south, f32[80,128]{1,0:T(8,128)} %copy-done.7, f32[80,128]{1,0:T(8,128)} %copy-done.9), custom_call_target="tpu_custom_call" | custom-call | tf_op jit(solution)/shard_map/corners/pallas_call | solution.py:599
  15.2 5.2 %collective-permute-start.2 = (f32[64,128]{1,0:T(8,128)}, f32[64,128]{1,0:T(8,128)S(1)}, u32[]{:S(2)}, u32[]{:S(2)}) collective-permute-start(f32[64,128]{1,0:T(8,128)} %get-tuple-element.32), channel_id=1, source_target_pairs={{0,1},{1,2},{2,3},{3,4},{4,5},{5,6},{6,7},{8,9},{9,10},{10,11},{11... | collective-permute-start | bytes 98312 | tf_op jit(solution)/shard_map/ppermute | solution.py:579
  20.5 1.9 %collective-permute-start.3 = (f32[64,128]{1,0:T(8,128)}, f32[64,128]{1,0:T(8,128)S(1)}, u32[]{:S(2)}, u32[]{:S(2)}) collective-permute-start(f32[64,128]{1,0:T(8,128)} %get-tuple-element.33), channel_id=1, source_target_pairs={{1,0},{2,1},{3,2},{4,3},{5,4},{6,5},{7,6},{9,8},{10,9},{11,10},{12... | collective-permute-start | bytes 98312 | tf_op jit(solution)/shard_map/ppermute | solution.py:579
  23.1 2.8 %collective-permute-done.3.from_north.edge_n = f32[64,128]{1,0:T(8,128)S(1)} collective-permute-done((f32[64,128]{1,0:T(8,128)}, f32[64,128]{1,0:T(8,128)S(1)}, u32[]{:S(2)}, u32[]{:S(2)}) %collective-permute-start.3) | collective-permute-done | bytes 32800 | tf_op jit(solution)/shard_map/ppermute | solution.py:579
  26.5 1.6 %priors.1 = f32[9,128]{1,0:T(8,128)} custom-call(s32[2]{0:T(128)} %pad_add_fusion.pos, s32[1024]{0:T(1024)} %get-tuple-element.48.code, f32[104,128]{1,0:T(8,128)} %get-tuple-element.24.own, f32[72,128]{1,0:T(8,128)} %get-tuple-element.25.own_coef, f32[80,128]{1,0:T(8,128)} %copy-done.7, f32[80,128]{1,0:T(8,128)} %copy-done.9, f32[64,128]{1,0:T(8,128)} %copy-done.15, ...), custom_call_target="tpu_custom_call" | custom-call | tf_op jit(solution)/shard_map/priors/pallas_call | solution.py:610
  28.2 1.8 %broadcast_in_dim.2 = f32[128,9,1,128]{3,2,1,0:T(1,128)} broadcast(f32[9,128]{1,0:T(8,128)} %priors.1), dimensions={1,3} | broadcast | bytes 594432 | tf_op jit(solution)/shard_map/broadcast_in_dim | solution.py:619
  30.0 9.4 %all-to-all-start = ((f32[128,9,1,128]{3,2,1,0:T(1,128)}), f32[128,9,1,128]{3,2,1,0:T(1,128)S(1)}, u32[]{:S(2)}, u32[]{:S(2)}) async-start(f32[128,9,1,128]{3,2,1,0:T(1,128)} %broadcast_in_dim.2), calls=%async_computation | async-start | bytes 1179648 | tf_op jit(solution)/shard_map/all_to_all | solution.py:620
  39.4 0.9 fusion.4
  40.2 4.8 %collective-permute-start.5 = (f32[8,2,32,128]{3,2,1,0:T(8,128)}, f32[8,2,32,128]{3,2,1,0:T(8,128)S(1)}, u32[]{:S(2)}, u32[]{:S(2)}) collective-permute-start(f32[8,2,32,128]{3,2,1,0:T(8,128)} %get-tuple-element.43), channel_id=1, source_target_pairs={{0,120},{8,0},{16,8},{24,16},{32,24},{40,32},{48,40},{56,48},{64,5... | collective-permute-start | bytes 786440 | tf_op jit(solution)/shard_map/ppermute | solution.py:576
  45.0 0.8 fusion.3
  45.8 2.5 %collective-permute-start.7 = (f32[8,16,2,128]{3,2,1,0:T(2,128)}, f32[8,16,2,128]{3,2,1,0:T(2,128)}, u32[]{:S(2)}, u32[]{:S(2)}) collective-permute-start(f32[8,16,2,128]{3,2,1,0:T(2,128)} %get-tuple-element.41), channel_id=1, source_target_pairs={{1,0},{2,1},{3,2},{4,3},{5,4},{6,5},{7,6},{9,8},{10,9},{11,10},{12... | collective-permute-start | bytes 393224 | tf_op jit(solution)/shard_map/ppermute | solution.py:579
  48.4 3.3 %collective-permute-start.6 = (f32[8,16,2,128]{3,2,1,0:T(2,128)}, f32[8,16,2,128]{3,2,1,0:T(2,128)}, u32[]{:S(2)}, u32[]{:S(2)}) collective-permute-start(f32[8,16,2,128]{3,2,1,0:T(2,128)} %get-tuple-element.42), channel_id=1, source_target_pairs={{0,1},{1,2},{2,3},{3,4},{4,5},{5,6},{6,7},{8,9},{9,10},{10,11},{11... | collective-permute-start | bytes 393224 | tf_op jit(solution)/shard_map/ppermute | solution.py:579
  52.3 5.2 %plan.1 = (bf16[1024,1024]{1,0:T(8,128)(2,1)}, f32[1536,256]{1,0:T(8,128)}, bf16[4,256,256]{2,1,0:T(8,128)(2,1)}, f32[4,8,256]{2,1,0:T(8,128)}, bf16[1024,128]{1...) custom-call(s32[2]{0:T(128)} %pad_add_fusion.pos, s32[8,1024]{1,0:T(8,128)} %stack.35.table), custom_call_target="tpu_custom_call" | custom-call | tf_op jit(solution)/shard_map/plan/pallas_call | solution.py:511
  57.6 0.8 copy-done.12
  58.4 0.8 copy-done.13
  59.2 0.8 copy-done.14
  59.9 0.8 copy-done.16
  60.7 0.8 copy-done.18
  61.4 4.7 %forecast.1 = f32[8,16,32,128]{3,2,1,0:T(8,128)S(1)} custom-call(f32[8,16,32,128]{3,2,1,0:T(8,128)S(1)} %copy-done, f32[64,32]{1,0:T(8,128)S(1)} %bitcast.24, f32[64,32]{1,0:T(8,128)S(1)} %bitcast.26, f32[64,32]{1,0:T(8,128)S(1)} %bitcast.28, f32[8,2,32,128]{3,2,1,0:T(8,128)} %collective-permute-done.4.halo_w, ...), custom_call_target="tpu_custom_call" | custom-call | tf_op jit(solution)/shard_map/forecast/pallas_call | solution.py:622
  66.1 1.4 %copy-done.1 = f32[8,16,32,128]{3,2,1,0:T(8,128)} copy-done((f32[8,16,32,128]{3,2,1,0:T(8,128)}, f32[8,16,32,128]{3,2,1,0:T(8,128)S(1)}, u32[]{:S(2)}) %copy-start.1) | copy-done | bytes 2097176
  67.5 1.6 %copy-done.2 = f32[8,16,32,128]{3,2,1,0:T(8,128)S(1)} copy-done((f32[8,16,32,128]{3,2,1,0:T(8,128)S(1)}, f32[8,16,32,128]{3,2,1,0:T(8,128)}, u32[]{:S(2)}) %copy-start.2) | copy-done | bytes 2097176
  69.1 1.6 %copy-done.3 = bf16[1024,1024]{1,0:T(8,128)(2,1)S(1)} copy-done((bf16[1024,1024]{1,0:T(8,128)(2,1)S(1)}, bf16[1024,1024]{1,0:T(8,128)(2,1)}, u32[]{:S(2)}) %copy-start.3) | copy-done | bytes 2097176
  70.7 1.4 %copy-done.4 = f32[1536,256]{1,0:T(8,128)S(1)} copy-done((f32[1536,256]{1,0:T(8,128)S(1)}, f32[1536,256]{1,0:T(8,128)}, u32[]{:S(2)}) %copy-start.4) | copy-done | bytes 1572888
  72.1 1.0 %copy-done.6 = f32[1024,128]{1,0:T(8,128)S(1)} copy-done((f32[1024,128]{1,0:T(8,128)S(1)}, f32[1024,128]{1,0:T(8,128)}, u32[]{:S(2)}) %copy-start.6) | copy-done | bytes 524312
  73.1 0.9 copy-done.11
  76.1 21.5 %analyse.1 = f32[4096,128]{1,0:T(8,128)} custom-call(s32[2]{0:T(128)S(1)} %copy-done.20, s32[4]{0:T(128)S(1)} %copy-done.21, f32[1152,128]{1,0:T(8,128)S(1)} %bitcast.22, f32[4,8,256]{2,1,0:T(8,128)S(1)} %copy-done.19, bf16[1024,1024]{1,0:T(8,128)(2,1)S(1)} %copy-done.3, bf16[1024,128]{1,0:T(8,128)(2,1)S(1)} %copy-done.11, f32[1024,128]{1,0:T(8,128)S(1)} %copy-done.6, ...), custom_call_target="tpu_custom_call" | custom-call | tf_op jit(solution)/shard_map/analyse/pallas_call | solution.py:521
  (55 shorter events, 5.3 us)
Async XLA Ops:
  0.0 22.4 %copy-start.25 = (f32[1,1,32]{2,1,0:T(1,128)S(1)}, f32[1,1,32]{2,1,0:T(1,128)}, u32[]{:S(2)}) copy-start(f32[1,1,32]{2,1,0:T(1,128)} %param.21) | copy-start | bytes 388
  0.0 22.4 %copy-start.26 = (f32[1,1,32]{2,1,0:T(1,128)S(1)}, f32[1,1,32]{2,1,0:T(1,128)}, u32[]{:S(2)}) copy-start(f32[1,1,32]{2,1,0:T(1,128)} %param.20) | copy-start | bytes 388
  2.7 36.6 %copy-start = (f32[8,16,32,128]{3,2,1,0:T(8,128)S(1)}, f32[8,16,32,128]{3,2,1,0:T(8,128)}, u32[]{:S(2)}) copy-start(f32[8,16,32,128]{3,2,1,0:T(8,128)} %cells.1) | copy-start | bytes 6291460
  5.7 46.0 %copy-start.22 = (s32[1024]{0:T(1024)S(1)}, s32[1024]{0:T(1024)}, u32[]{:S(2)}) copy-start(s32[1024]{0:T(1024)} %param.17) | copy-start | bytes 12292
  5.7 46.0 %copy-start.23 = (s32[1024]{0:T(1024)S(1)}, s32[1024]{0:T(1024)}, u32[]{:S(2)}) copy-start(s32[1024]{0:T(1024)} %param.18) | copy-start | bytes 12292
  5.7 46.0 %copy-start.24 = (s32[1024]{0:T(1024)S(1)}, s32[1024]{0:T(1024)}, u32[]{:S(2)}) copy-start(s32[1024]{0:T(1024)} %param.19) | copy-start | bytes 12292
  5.7 7.4 %collective-permute-start = (f32[80,128]{1,0:T(8,128)}, f32[80,128]{1,0:T(8,128)S(1)}, u32[]{:S(2)}, u32[]{:S(2)}) collective-permute-start(f32[80,128]{1,0:T(8,128)} %get-tuple-element.26), channel_id=1, source_target_pairs={{0,8},{8,16},{16,24},{24,32},{32,40},{40,48},{48,56},{56,64},{64,7... | collective-permute-start | bytes 122888 | tf_op jit(solution)/shard_map/ppermute | solution.py:576
  7.8 5.3 %collective-permute-start.1 = (f32[80,128]{1,0:T(8,128)}, f32[80,128]{1,0:T(8,128)S(1)}, u32[]{:S(2)}, u32[]{:S(2)}) collective-permute-start(f32[80,128]{1,0:T(8,128)} %get-tuple-element.27), channel_id=1, source_target_pairs={{0,120},{8,0},{16,8},{24,16},{32,24},{40,32},{48,40},{56,48},{64,5... | collective-permute-start | bytes 122888 | tf_op jit(solution)/shard_map/ppermute | solution.py:576
  15.2 42.3 %copy-start.8 = (f32[80,128]{1,0:T(8,128)S(1)}, f32[80,128]{1,0:T(8,128)}, u32[]{:S(2)}) copy-start(f32[80,128]{1,0:T(8,128)} %copy-done.7) | copy-start | bytes 122884
  15.2 42.3 %copy-start.10 = (f32[80,128]{1,0:T(8,128)S(1)}, f32[80,128]{1,0:T(8,128)}, u32[]{:S(2)}) copy-start(f32[80,128]{1,0:T(8,128)} %copy-done.9) | copy-start | bytes 122884
  15.2 7.8 %collective-permute-start.2 = (f32[64,128]{1,0:T(8,128)}, f32[64,128]{1,0:T(8,128)S(1)}, u32[]{:S(2)}, u32[]{:S(2)}) collective-permute-start(f32[64,128]{1,0:T(8,128)} %get-tuple-element.32), channel_id=1, source_target_pairs={{0,1},{1,2},{2,3},{3,4},{4,5},{5,6},{6,7},{8,9},{9,10},{10,11},{11... | collective-permute-start | bytes 98312 | tf_op jit(solution)/shard_map/ppermute | solution.py:579
  20.5 5.4 %collective-permute-start.3 = (f32[64,128]{1,0:T(8,128)}, f32[64,128]{1,0:T(8,128)S(1)}, u32[]{:S(2)}, u32[]{:S(2)}) collective-permute-start(f32[64,128]{1,0:T(8,128)} %get-tuple-element.33), channel_id=1, source_target_pairs={{1,0},{2,1},{3,2},{4,3},{5,4},{6,5},{7,6},{9,8},{10,9},{11,10},{12... | collective-permute-start | bytes 98312 | tf_op jit(solution)/shard_map/ppermute | solution.py:579
  23.1 2.8 %copy-start.15 = (f32[64,128]{1,0:T(8,128)}, f32[64,128]{1,0:T(8,128)S(1)}, u32[]{:S(2)}) copy-start(f32[64,128]{1,0:T(8,128)S(1)} %collective-permute-done.2.from_south.edge_s) | copy-start | bytes 98308
  30.0 37.5 %all-to-all-start = ((f32[128,9,1,128]{3,2,1,0:T(1,128)}), f32[128,9,1,128]{3,2,1,0:T(1,128)S(1)}, u32[]{:S(2)}, u32[]{:S(2)}) async-start(f32[128,9,1,128]{3,2,1,0:T(1,128)} %broadcast_in_dim.2), calls=%async_computation | async-start | bytes 1179648 | tf_op jit(solution)/shard_map/all_to_all | solution.py:620
  40.2 17.3 %collective-permute-start.5 = (f32[8,2,32,128]{3,2,1,0:T(8,128)}, f32[8,2,32,128]{3,2,1,0:T(8,128)S(1)}, u32[]{:S(2)}, u32[]{:S(2)}) collective-permute-start(f32[8,2,32,128]{3,2,1,0:T(8,128)} %get-tuple-element.43), channel_id=1, source_target_pairs={{0,120},{8,0},{16,8},{24,16},{32,24},{40,32},{48,40},{56,48},{64,5... | collective-permute-start | bytes 786440 | tf_op jit(solution)/shard_map/ppermute | solution.py:576
  45.0 12.5 %collective-permute-start.4 = (f32[8,2,32,128]{3,2,1,0:T(8,128)}, f32[8,2,32,128]{3,2,1,0:T(8,128)}, u32[]{:S(2)}, u32[]{:S(2)}) collective-permute-start(f32[8,2,32,128]{3,2,1,0:T(8,128)} %get-tuple-element.44), channel_id=1, source_target_pairs={{0,8},{8,16},{16,24},{24,32},{32,40},{40,48},{48,56},{56,64},{64,7... | collective-permute-start | bytes 786440 | tf_op jit(solution)/shard_map/ppermute | solution.py:576
  45.8 11.7 %collective-permute-start.7 = (f32[8,16,2,128]{3,2,1,0:T(2,128)}, f32[8,16,2,128]{3,2,1,0:T(2,128)}, u32[]{:S(2)}, u32[]{:S(2)}) collective-permute-start(f32[8,16,2,128]{3,2,1,0:T(2,128)} %get-tuple-element.41), channel_id=1, source_target_pairs={{1,0},{2,1},{3,2},{4,3},{5,4},{6,5},{7,6},{9,8},{10,9},{11,10},{12... | collective-permute-start | bytes 393224 | tf_op jit(solution)/shard_map/ppermute | solution.py:579
  48.4 9.1 %collective-permute-start.6 = (f32[8,16,2,128]{3,2,1,0:T(2,128)}, f32[8,16,2,128]{3,2,1,0:T(2,128)}, u32[]{:S(2)}, u32[]{:S(2)}) collective-permute-start(f32[8,16,2,128]{3,2,1,0:T(2,128)} %get-tuple-element.42), channel_id=1, source_target_pairs={{0,1},{1,2},{2,3},{3,4},{4,5},{5,6},{6,7},{8,9},{9,10},{10,11},{11... | collective-permute-start | bytes 393224 | tf_op jit(solution)/shard_map/ppermute | solution.py:579
  57.5 10.0 %copy-start.5 = (bf16[4,256,256]{2,1,0:T(8,128)(2,1)S(1)}, bf16[4,256,256]{2,1,0:T(8,128)(2,1)}, u32[]{:S(2)}) copy-start(bf16[4,256,256]{2,1,0:T(8,128)(2,1)} %get-tuple-element.39.select_far) | copy-start | bytes 1572868
  57.6 0.8 copy-start.12
  58.4 0.8 copy-start.13
  59.1 0.8 copy-start.14
  59.9 0.8 copy-start.16
  60.7 0.8 copy-start.18
  66.1 1.4 %copy-start.1 = (f32[8,16,32,128]{3,2,1,0:T(8,128)}, f32[8,16,32,128]{3,2,1,0:T(8,128)S(1)}, u32[]{:S(2)}) copy-start(f32[8,16,32,128]{3,2,1,0:T(8,128)S(1)} %forecast.1) | copy-start | bytes 6291460
  67.5 1.6 %copy-start.2 = (f32[8,16,32,128]{3,2,1,0:T(8,128)S(1)}, f32[8,16,32,128]{3,2,1,0:T(8,128)}, u32[]{:S(2)}) copy-start(f32[8,16,32,128]{3,2,1,0:T(8,128)} %copy-done.1) | copy-start | bytes 6291460
  69.1 1.6 %copy-start.3 = (bf16[1024,1024]{1,0:T(8,128)(2,1)S(1)}, bf16[1024,1024]{1,0:T(8,128)(2,1)}, u32[]{:S(2)}) copy-start(bf16[1024,1024]{1,0:T(8,128)(2,1)} %get-tuple-element.35.perm_far) | copy-start | bytes 6291460
  70.7 1.4 %copy-start.4 = (f32[1536,256]{1,0:T(8,128)S(1)}, f32[1536,256]{1,0:T(8,128)}, u32[]{:S(2)}) copy-start(f32[1536,256]{1,0:T(8,128)} %get-tuple-element.38.weight_far) | copy-start | bytes 4718596
  72.1 1.0 %copy-start.6 = (f32[1024,128]{1,0:T(8,128)S(1)}, f32[1024,128]{1,0:T(8,128)}, u32[]{:S(2)}) copy-start(f32[1024,128]{1,0:T(8,128)} %get-tuple-element.37.place_far) | copy-start | bytes 1572868
  73.1 0.9 copy-start.11
  74.1 0.8 copy-start.19
  74.8 0.7 copy-start.20
  (4 other events, 2.5 us)

commit v4 on v3

--- a/solution.py
+++ b/solution.py
@@ -411,8 +411,20 @@
 
 def forecast_kernel(
     cells, east, north, diff, halo_w, halo_e, halo_s, halo_n, edge_w, edge_e, edge_s, edge_n,
-    out, table, before, after,
+    out, table, before, after, arrivals,
 ):
+    rows = pl.ds(8, CY)
+    copies = []
+    for level in range(4):
+        pair = pl.ds(level * 2, 2)
+        copies.append(
+            [
+                pltpu.make_async_copy(far.at[pair], before.at[pair, cols, rows, :], arrivals.at[level])
+                for far, cols in ((cells, pl.ds(2, CX)), (halo_w, pl.ds(0, 2)), (halo_e, pl.ds(2 + CX, 2)))
+            ]
+        )
+        for copy in copies[level]:
+            copy.start()
     coefs = (east, north, diff)
     pad = jnp.zeros((128 - CX, CY), F32)
     fill = jnp.zeros((128, 128 - CY), F32)
@@ -433,15 +445,14 @@
 
     mid_rows = slice(8, 8 + CY)
     for level in range(4):
+        for copy in copies[level]:
+            copy.wait()
         for which in range(2):
             comp = level * 2 + which
-            before[which, 2 : 2 + CX, mid_rows, :] = cells[comp]
-            before[which, 0:2, mid_rows, :] = halo_w[comp]
-            before[which, 2 + CX : 4 + CX, mid_rows, :] = halo_e[comp]
             for rim, edge, inner, target in ((halo_s, edge_s, 1, 7), (halo_n, edge_n, 0, 8 + CY)):
-                before[which, 2 : 2 + CX, target, :] = rim[comp, :, inner, :]
-                before[which, 1, target : target + 1, :] = edge[48 + comp : 49 + comp, :]
-                before[which, 2 + CX, target : target + 1, :] = edge[56 + comp : 57 + comp, :]
+                before[level * 2 + which, 2 : 2 + CX, target, :] = rim[comp, :, inner, :]
+                before[level * 2 + which, 1, target : target + 1, :] = edge[48 + comp : 49 + comp, :]
+                before[level * 2 + which, 2 + CX, target : target + 1, :] = edge[56 + comp : 57 + comp, :]
         for col in range(-1, CX + 1):
             lane = CX if col < 0 else (CX + 1 if col == CX else col)
             u, v, nu = (
@@ -450,11 +461,11 @@
             at = col + 2
             for which in range(2):
                 after[which, at, mid_rows, :] = stencil(
-                    before[which, at, mid_rows, :],
-                    before[which, at + 1, mid_rows, :],
-                    before[which, at - 1, mid_rows, :],
-                    before[which, at, 9 : 9 + CY, :],
-                    before[which, at, 7 : 7 + CY, :],
+                    before[level * 2 + which, at, mid_rows, :],
+                    before[level * 2 + which, at + 1, mid_rows, :],
+                    before[level * 2 + which, at - 1, mid_rows, :],
+                    before[level * 2 + which, at, 9 : 9 + CY, :],
+                    before[level * 2 + which, at, 7 : 7 + CY, :],
                     u, v, nu,
                 )
         for rim, edge, outer, inside, target in (
@@ -467,11 +478,11 @@
             )
             for which in range(2):
                 comp = level * 2 + which
-                mid = before[which, 2 : 2 + CX, target, :]
-                e = before[which, 3 : 3 + CX, target, :]
-                w = before[which, 1 : 1 + CX, target, :]
+                mid = before[level * 2 + which, 2 : 2 + CX, target, :]
+                e = before[level * 2 + which, 3 : 3 + CX, target, :]
+                w = before[level * 2 + which, 1 : 1 + CX, target, :]
                 far = rim[comp, :, outer, :]
-                close = cells[comp, :, inside, :]
+                close = before[comp, 2 : 2 + CX, 8 + inside, :]
                 n, s = (close, far) if target == 7 else (far, close)
                 after[which, 2 : 2 + CX, target, :] = stencil(mid, e, w, n, s, u, v, nu)
         for col in range(CX):
@@ -492,6 +503,10 @@
 
 def vmem():
     return pl.BlockSpec(memory_space=pltpu.VMEM)
+
+
+def hbm():
+    return pl.BlockSpec(memory_space=pltpu.HBM)
 
 
 def smem():
@@ -521,7 +536,7 @@
     return pl.pallas_call(
         analysis_kernel,
         out_shape=jax.ShapeDtypeStruct(far[-1].shape, F32),
-        in_specs=[smem(), smem(), vmem(), vmem()] + [pl.BlockSpec(memory_space=pl.ANY)] * len(far),
+        in_specs=[smem(), smem(), vmem(), vmem()] + [hbm()] * len(far),
         out_specs=vmem(),
         scratch_shapes=[
             pltpu.VMEM((NOBS, MEM), F32),
@@ -567,7 +582,6 @@
             zero,
         ]
     )
-    perm, obs_weight, select, slots, source, place, counts = plan(pos, table)
 
     def rows(count, width=MEM):
         return jax.ShapeDtypeStruct((count, width), F32)
@@ -616,18 +630,23 @@
         name="priors",
     )(pos, code, own, own_coef, from_west, from_east, from_south, from_north, held)
 
+    bundle, table, halo_w, halo_e, halo_s, halo_n = lax.optimization_barrier(
+        (bundle, table, halo_w, halo_e, halo_s, halo_n)
+    )
+    perm, obs_weight, select, slots, source, place, counts = plan(pos, table)
     bundle = jnp.broadcast_to(bundle.reshape(1, 9, 1, members), (128, 9, 1, members))
     arrived = lax.all_to_all(bundle, ("gx", "gy"), 0, 0, tiled=True)
 
     state = pl.pallas_call(
         forecast_kernel,
         out_shape=jax.ShapeDtypeStruct(cells.shape, F32),
-        in_specs=[vmem()] * 12,
+        in_specs=[hbm()] + [vmem()] * 3 + [hbm()] * 2 + [vmem()] * 6,
         out_specs=vmem(),
         scratch_shapes=[
             pltpu.VMEM((4, 3, CY, 128), F32),
+            pltpu.VMEM((COMP, CX + 4, CY + 16, MEM), F32),
             pltpu.VMEM((2, CX + 4, CY + 16, MEM), F32),
-            pltpu.VMEM((2, CX + 4, CY + 16, MEM), F32),
+            pltpu.SemaphoreType.DMA((4,)),
         ],
         compiler_params=pltpu.CompilerParams(vmem_limit_bytes=32 << 20),
         name="forecast",

time: 98.9 us -> 100 us (1.011)
  local copies, waits for them, and re-layouts: 19.2 us -> 22.4 us
  waiting for transfers between devices: 4.38 us -> 1.73 us
  other arithmetic: 3.36 us -> 4.69 us
  Pallas kernels: 37.4 us -> 36.4 us
    ppermute x4, waiting for transfers between devices: 2.85 us -> 0.17 us  [along_y(): lax.ppermute(value, 'gy', [(i, i + step) for i in range(8) if 0 <= i + st...]
    unnamed x54 -> x56, local copies, waits for them, and re-layouts: 15.1 us -> 17.7 us
    add x2 -> x0, other arithmetic: 2.05 us -> none  [shards(): code = obs_column[:, 0] + obs_column[:, 1] * 256 + obs_comp * 65536]
    another operation x0 -> x1, other arithmetic: none -> 1.46 us  [shards(): jnp.stack([obs_column[:, 0], obs_column[:, 1], obs_comp // per_level, obs...]
    another operation x2, local copies, waits for them, and re-layouts: 0.65 us -> 2.02 us  [shards(): jnp.stack([obs_column[:, 0], obs_column[:, 1], obs_comp // per_level, obs...]
    select_n x0 -> x1, other arithmetic: none -> 1.29 us  [shards(): obs_comp // per_level]
  transfers between devices with their start and end apart: 9 -> 9, of which waited for: 2 -> 2; matrix products, arithmetic and copies ran while one was open for 3% -> 4% of each run, Pallas kernels for 10% -> 11%
where the time goes in v4:
time: 100 us; the launch traced here: 98.7 us
  Pallas kernels  36.4 us (36%)
  starting transfers between devices  33.1 us (33%)
  local copies, waits for them, and re-layouts  22.4 us (22%)
  other arithmetic  4.69 us (5%)
  waiting for transfers between devices  1.73 us (2%)
    pallas_call x1, Pallas kernels, analyse(): pl.pallas_call(analysis_kernel, out_shape=jax.ShapeDtypeStruct(far[-1].sh...  21.5 us
    unnamed x56, local copies, waits for them, and re-layouts  17.7 us
    ppermute x4, starting transfers between devices, along_y(): lax.ppermute(value, 'gy', [(i, i + step) for i in range(8) if 0 <= i + st...  12.7 us
    ppermute x4, starting transfers between devices, along_x(): return lax.ppermute(value, 'gx', [(i, (i + step) % 16) for i in range(16)])  10.9 us
    all_to_all x1, starting transfers between devices, shards(): arrived = lax.all_to_all(bundle, ('gx', 'gy'), 0, 0, tiled=True)  9.47 us
    pallas_call x1, Pallas kernels, plan(): pl.pallas_call(plan_kernel, out_shape=shapes, in_specs=[smem(), vmem()],...  5.18 us
    pallas_call x1, Pallas kernels, shards(): pl.pallas_call(forecast_kernel, out_shape=jax.ShapeDtypeStruct(cells.shap...  3.75 us
    pallas_call x1, Pallas kernels, shards(): pl.pallas_call(edge_kernel, out_shape=(rows(104), rows(72), rows(80), row...  2.78 us
  transfers between devices with their start and end apart: 9, of which 2 were waited for; matrix products, arithmetic and copies ran while one was open for 4% of the time, Pallas kernels for 11%

profile of v4, /device:TPU:1, one launch (start us, length us, event | category | flops | bytes accessed | tf_op | source)
XLA Modules:
  0.0 98.7 jit_solution(14200340625985575834)
XLA Ops:
  0.0 1.5 %slice_bitcast_fusion = (s32[1,1024]{1,0:T(1,128)}, s32[1024,1]{0,1:T(1,128)S(1)}, s32[1,1024]{1,0:T(1,128)}) fusion(s32[1024,2]{0,1:T(2,128)} %param.15), kind=kLoop, calls=%fused_computation.9 | loop fusion | flops 2048 | bytes 20480 | tf_op jit(solution)/shard_map/stack;squeeze | solution.py:573
  2.1 1.3 %add_select_fusion = (s32[1024]{0:T(1024)}, s32[1024]{0:T(1024)}) fusion(s32[1024]{0:T(1024)} %param.16, s32[1024]{0:T(1024)S(1)} %bitcast.30), kind=kLoop, calls=%fused_computation | loop fusion | flops 17408 | bytes 16384 | tf_op jit(solution)/shard_map/jit(floor_divide)/jit(_where)/select_n | solution.py:577
  3.4 2.8 %edges.1 = (f32[104,128]{1,0:T(8,128)}, f32[72,128]{1,0:T(8,128)}, f32[80,128]{1,0:T(8,128)}, f32[80,128]{1,0:T(8,128)}, f32[48,128]{1,0:T(8,128)}, /*index=5*/f32[48,128]{1,0:T(8,128)}) custom-call(s32[2]{0:T(128)} %pad_add_fusion.pos, s32[1024]{0:T(1024)} %get-tuple-element.61.code, f32[4096,128]{1,0:T(8,128)} %bitcast.20, f32[64,32]{1,0:T(8,128)} %bitcast.23, ...), custom_call_target="tpu_custom_call" | custom-call | tf_op jit(solution)/shard_map/edges/pallas_call | solution.py:599
  6.1 2.0 %collective-permute-start = (f32[80,128]{1,0:T(8,128)}, f32[80,128]{1,0:T(8,128)S(1)}, u32[]{:S(2)}, u32[]{:S(2)}) collective-permute-start(f32[80,128]{1,0:T(8,128)} %get-tuple-element.31), channel_id=1, source_target_pairs={{0,8},{8,16},{16,24},{24,32},{32,40},{40,48},{48,56},{56,64},{64,7... | collective-permute-start | bytes 122888 | tf_op jit(solution)/shard_map/ppermute | solution.py:590
  8.2 3.8 %collective-permute-start.1 = (f32[80,128]{1,0:T(8,128)}, f32[80,128]{1,0:T(8,128)S(1)}, u32[]{:S(2)}, u32[]{:S(2)}) collective-permute-start(f32[80,128]{1,0:T(8,128)} %get-tuple-element.32), channel_id=1, source_target_pairs={{0,120},{8,0},{16,8},{24,16},{32,24},{40,32},{48,40},{56,48},{64,5... | collective-permute-start | bytes 122888 | tf_op jit(solution)/shard_map/ppermute | solution.py:590
  11.9 1.5 %collective-permute-done.from_west.edge_w = f32[80,128]{1,0:T(8,128)S(1)} collective-permute-done((f32[80,128]{1,0:T(8,128)}, f32[80,128]{1,0:T(8,128)S(1)}, u32[]{:S(2)}, u32[]{:S(2)}) %collective-permute-start) | collective-permute-done | bytes 40992 | tf_op jit(solution)/shard_map/ppermute | solution.py:590
  14.1 1.5 %corners.1 = (f32[64,128]{1,0:T(8,128)}, f32[64,128]{1,0:T(8,128)}) custom-call(s32[2]{0:T(128)} %pad_add_fusion.pos, s32[1024]{0:T(1024)} %get-tuple-element.61.code, f32[48,128]{1,0:T(8,128)} %get-tuple-element.35.base_north, f32[48,128]{1,0:T(8,128)} %get-tuple-element.36.base_south, f32[80,128]{1,0:T(8,128)} %copy-done.7, f32[80,128]{1,0:T(8,128)} %copy-done.9), custom_call_target="tpu_custom_call" | custom-call | tf_op jit(solution)/shard_map/corners/pallas_call | solution.py:613
  15.7 5.2 %collective-permute-start.2 = (f32[64,128]{1,0:T(8,128)}, f32[64,128]{1,0:T(8,128)S(1)}, u32[]{:S(2)}, u32[]{:S(2)}) collective-permute-start(f32[64,128]{1,0:T(8,128)} %get-tuple-element.37), channel_id=1, source_target_pairs={{0,1},{1,2},{2,3},{3,4},{4,5},{5,6},{6,7},{8,9},{9,10},{10,11},{11... | collective-permute-start | bytes 98312 | tf_op jit(solution)/shard_map/ppermute | solution.py:593
  21.0 5.1 %collective-permute-start.5 = (f32[8,2,32,128]{3,2,1,0:T(8,128)S(1)}, f32[8,2,32,128]{3,2,1,0:T(8,128)S(1)}, u32[]{:S(2)}, u32[]{:S(2)}) collective-permute-start(f32[8,2,32,128]{3,2,1,0:T(8,128)S(1)} %get-tuple-element.55), channel_id=1, source_target_pairs={{0,120},{8,0},{16,8},{24,16},{32,24},{40,32},{48,40},{56,48},{64,5... | collective-permute-start | bytes 786440 | tf_op jit(solution)/shard_map/ppermute | solution.py:590
  26.1 0.8 fusion.3
  26.9 1.9 %collective-permute-start.7 = (f32[8,16,2,128]{3,2,1,0:T(2,128)}, f32[8,16,2,128]{3,2,1,0:T(2,128)S(1)}, u32[]{:S(2)}, u32[]{:S(2)}) collective-permute-start(f32[8,16,2,128]{3,2,1,0:T(2,128)} %get-tuple-element.53), channel_id=1, source_target_pairs={{1,0},{2,1},{3,2},{4,3},{5,4},{6,5},{7,6},{9,8},{10,9},{11,10},{12... | collective-permute-start | bytes 393224 | tf_op jit(solution)/shard_map/ppermute | solution.py:593
  28.8 3.6 %collective-permute-start.6 = (f32[8,16,2,128]{3,2,1,0:T(2,128)}, f32[8,16,2,128]{3,2,1,0:T(2,128)S(1)}, u32[]{:S(2)}, u32[]{:S(2)}) collective-permute-start(f32[8,16,2,128]{3,2,1,0:T(2,128)} %get-tuple-element.54), channel_id=1, source_target_pairs={{0,1},{1,2},{2,3},{3,4},{4,5},{5,6},{6,7},{8,9},{9,10},{10,11},{11... | collective-permute-start | bytes 393224 | tf_op jit(solution)/shard_map/ppermute | solution.py:593
  32.5 1.9 %collective-permute-start.3 = (f32[64,128]{1,0:T(8,128)}, f32[64,128]{1,0:T(8,128)S(1)}, u32[]{:S(2)}, u32[]{:S(2)}) collective-permute-start(f32[64,128]{1,0:T(8,128)} %get-tuple-element.38), channel_id=1, source_target_pairs={{1,0},{2,1},{3,2},{4,3},{5,4},{6,5},{7,6},{9,8},{10,9},{11,10},{12... | collective-permute-start | bytes 98312 | tf_op jit(solution)/shard_map/ppermute | solution.py:593
  34.4 1.3 %fusion.2.held = f32[1,128]{1,0:T(1,128)} fusion(f32[1,32]{1,0:T(1,128)} %bitcast.34, f32[1,32]{1,0:T(1,128)} %bitcast.35), kind=kLoop, calls=%fused_computation.13 | loop fusion | flops 512 | bytes 768 | tf_op jit(solution)/shard_map/concatenate | solution.py:622
  36.3 1.4 %stack.35.table = s32[8,1024]{1,0:T(8,128)} concatenate(s32[1,1024]{1,0:T(1,128)} %get-tuple-element.59, s32[1,1024]{1,0:T(1,128)} %get-tuple-element.57, s32[1,1024]{1,0:T(1,128)} %bitcast.29, s32[1,1024]{1,0:T(1,128)} %bitcast.31, s32[1,1024]{1,0:T(1,128)} %bitcast.32, s32[1,1024]{1,0:T(1,128)} %bitcast.33, s32[2,1024]{1,0:T(2,128)} %stack.34), dimensions={0} | concatenate | bytes 65536 | tf_op jit(solution)/shard_map/stack | solution.py:573
  38.5 1.6 %priors.1 = f32[9,128]{1,0:T(8,128)} custom-call(s32[2]{0:T(128)} %pad_add_fusion.pos, s32[1024]{0:T(1024)} %get-tuple-element.61.code, f32[104,128]{1,0:T(8,128)} %get-tuple-element.29.own, f32[72,128]{1,0:T(8,128)} %get-tuple-element.30.own_coef, f32[80,128]{1,0:T(8,128)} %copy-done.7, f32[80,128]{1,0:T(8,128)} %copy-done.9, f32[64,128]{1,0:T(8,128)} %copy-done.17, ...), custom_call_target="tpu_custom_call" | custom-call | tf_op jit(solution)/shard_map/priors/pallas_call | solution.py:624
  40.2 1.9 %broadcast_in_dim.2 = f32[128,9,1,128]{3,2,1,0:T(1,128)} broadcast(f32[9,128]{1,0:T(8,128)} %priors.1), dimensions={1,3} | broadcast | bytes 594432 | tf_op jit(solution)/shard_map/broadcast_in_dim | solution.py:637
  42.1 9.5 %all-to-all-start = ((f32[128,9,1,128]{3,2,1,0:T(1,128)}), f32[128,9,1,128]{3,2,1,0:T(1,128)S(1)}, u32[]{:S(2)}, u32[]{:S(2)}) async-start(f32[128,9,1,128]{3,2,1,0:T(1,128)} %broadcast_in_dim.2), calls=%async_computation | async-start | bytes 1179648 | tf_op jit(solution)/shard_map/all_to_all | solution.py:638
  51.6 5.2 %plan.1 = (bf16[1024,1024]{1,0:T(8,128)(2,1)}, f32[1536,256]{1,0:T(8,128)}, bf16[4,256,256]{2,1,0:T(8,128)(2,1)}, f32[4,8,256]{2,1,0:T(8,128)}, bf16[1024,128]{1...) custom-call(s32[2]{0:T(128)} %pad_add_fusion.pos, s32[8,1024]{1,0:T(8,128)} %stack.35.table), custom_call_target="tpu_custom_call" | custom-call | tf_op jit(solution)/shard_map/plan/pallas_call | solution.py:526
  56.8 0.9 copy-done.12
  57.7 0.8 copy-done.14
  58.5 0.8 copy-done.15
  61.5 0.9 copy-done.22
  62.4 0.9 copy-done.24
  63.3 3.8 %forecast.1 = f32[8,16,32,128]{3,2,1,0:T(8,128)S(1)} custom-call(f32[8,16,32,128]{3,2,1,0:T(8,128)S(1)} %copy-done, f32[64,32]{1,0:T(8,128)S(1)} %bitcast.24, f32[64,32]{1,0:T(8,128)S(1)} %bitcast.26, f32[64,32]{1,0:T(8,128)S(1)} %bitcast.28, f32[8,2,32,128]{3,2,1,0:T(8,128)S(1)} %copy-done.12, f32[8,2,32,128]{3,2,1,0:T(8,128)S(1)} %collective-permute-done.5.halo_e, ...), custom_call_target="tpu_custom_call" | custom-call | tf_op jit(solution)/shard_map/forecast/pallas_call | solution.py:640
  67.1 1.3 %copy-done.1 = f32[8,16,32,128]{3,2,1,0:T(8,128)} copy-done((f32[8,16,32,128]{3,2,1,0:T(8,128)}, f32[8,16,32,128]{3,2,1,0:T(8,128)S(1)}, u32[]{:S(2)}) %copy-start.1) | copy-done | bytes 2097176
  68.4 1.6 %copy-done.2 = f32[8,16,32,128]{3,2,1,0:T(8,128)S(1)} copy-done((f32[8,16,32,128]{3,2,1,0:T(8,128)S(1)}, f32[8,16,32,128]{3,2,1,0:T(8,128)}, u32[]{:S(2)}) %copy-start.2) | copy-done | bytes 2097176
  70.0 1.6 %copy-done.3 = bf16[1024,1024]{1,0:T(8,128)(2,1)S(1)} copy-done((bf16[1024,1024]{1,0:T(8,128)(2,1)S(1)}, bf16[1024,1024]{1,0:T(8,128)(2,1)}, u32[]{:S(2)}) %copy-start.3) | copy-done | bytes 2097176
  71.6 1.4 %copy-done.4 = f32[1536,256]{1,0:T(8,128)S(1)} copy-done((f32[1536,256]{1,0:T(8,128)S(1)}, f32[1536,256]{1,0:T(8,128)}, u32[]{:S(2)}) %copy-start.4) | copy-done | bytes 1572888
  73.0 1.0 %copy-done.6 = f32[1024,128]{1,0:T(8,128)S(1)} copy-done((f32[1024,128]{1,0:T(8,128)S(1)}, f32[1024,128]{1,0:T(8,128)}, u32[]{:S(2)}) %copy-start.6) | copy-done | bytes 524312
  74.1 0.9 copy-done.13
  77.0 21.5 %analyse.1 = f32[4096,128]{1,0:T(8,128)} custom-call(s32[2]{0:T(128)S(1)} %copy-done.26, s32[4]{0:T(128)S(1)} %copy-done.27, f32[1152,128]{1,0:T(8,128)S(1)} %bitcast.22, f32[4,8,256]{2,1,0:T(8,128)S(1)} %copy-done.25, bf16[1024,1024]{1,0:T(8,128)(2,1)S(1)} %copy-done.3, bf16[1024,128]{1,0:T(8,128)(2,1)S(1)} %copy-done.13, f32[1024,128]{1,0:T(8,128)S(1)} %copy-done.6, ...), custom_call_target="tpu_custom_call" | custom-call | tf_op jit(solution)/shard_map/analyse/pallas_call | solution.py:536
  (57 shorter events, 7.0 us)
Async XLA Ops:
  0.0 20.9 %copy-start = (f32[8,16,32,128]{3,2,1,0:T(8,128)S(1)}, f32[8,16,32,128]{3,2,1,0:T(8,128)}, u32[]{:S(2)}) copy-start(f32[8,16,32,128]{3,2,1,0:T(8,128)} %cells.1) | copy-start | bytes 6291460
  6.1 7.4 %collective-permute-start = (f32[80,128]{1,0:T(8,128)}, f32[80,128]{1,0:T(8,128)S(1)}, u32[]{:S(2)}, u32[]{:S(2)}) collective-permute-start(f32[80,128]{1,0:T(8,128)} %get-tuple-element.31), channel_id=1, source_target_pairs={{0,8},{8,16},{16,24},{24,32},{32,40},{40,48},{48,56},{56,64},{64,7... | collective-permute-start | bytes 122888 | tf_op jit(solution)/shard_map/ppermute | solution.py:590
  8.2 5.3 %collective-permute-start.1 = (f32[80,128]{1,0:T(8,128)}, f32[80,128]{1,0:T(8,128)S(1)}, u32[]{:S(2)}, u32[]{:S(2)}) collective-permute-start(f32[80,128]{1,0:T(8,128)} %get-tuple-element.32), channel_id=1, source_target_pairs={{0,120},{8,0},{16,8},{24,16},{32,24},{40,32},{48,40},{56,48},{64,5... | collective-permute-start | bytes 122888 | tf_op jit(solution)/shard_map/ppermute | solution.py:590
  15.7 41.1 %copy-start.8 = (f32[80,128]{1,0:T(8,128)S(1)}, f32[80,128]{1,0:T(8,128)}, u32[]{:S(2)}) copy-start(f32[80,128]{1,0:T(8,128)} %copy-done.7) | copy-start | bytes 122884
  15.7 41.1 %copy-start.10 = (f32[80,128]{1,0:T(8,128)S(1)}, f32[80,128]{1,0:T(8,128)}, u32[]{:S(2)}) copy-start(f32[80,128]{1,0:T(8,128)} %copy-done.9) | copy-start | bytes 122884
  15.7 16.8 %collective-permute-start.2 = (f32[64,128]{1,0:T(8,128)}, f32[64,128]{1,0:T(8,128)S(1)}, u32[]{:S(2)}, u32[]{:S(2)}) collective-permute-start(f32[64,128]{1,0:T(8,128)} %get-tuple-element.37), channel_id=1, source_target_pairs={{0,1},{1,2},{2,3},{3,4},{4,5},{5,6},{6,7},{8,9},{9,10},{10,11},{11... | collective-permute-start | bytes 98312 | tf_op jit(solution)/shard_map/ppermute | solution.py:593
  21.0 19.2 %collective-permute-start.5 = (f32[8,2,32,128]{3,2,1,0:T(8,128)S(1)}, f32[8,2,32,128]{3,2,1,0:T(8,128)S(1)}, u32[]{:S(2)}, u32[]{:S(2)}) collective-permute-start(f32[8,2,32,128]{3,2,1,0:T(8,128)S(1)} %get-tuple-element.55), channel_id=1, source_target_pairs={{0,120},{8,0},{16,8},{24,16},{32,24},{40,32},{48,40},{56,48},{64,5... | collective-permute-start | bytes 786440 | tf_op jit(solution)/shard_map/ppermute | solution.py:590
  26.1 14.1 %collective-permute-start.4 = (f32[8,2,32,128]{3,2,1,0:T(8,128)S(1)}, f32[8,2,32,128]{3,2,1,0:T(8,128)S(1)}, u32[]{:S(2)}, u32[]{:S(2)}) collective-permute-start(f32[8,2,32,128]{3,2,1,0:T(8,128)S(1)} %get-tuple-element.56), channel_id=1, source_target_pairs={{0,8},{8,16},{16,24},{24,32},{32,40},{40,48},{48,56},{56,64},{64,7... | collective-permute-start | bytes 786440 | tf_op jit(solution)/shard_map/ppermute | solution.py:590
  26.9 13.3 %collective-permute-start.7 = (f32[8,16,2,128]{3,2,1,0:T(2,128)}, f32[8,16,2,128]{3,2,1,0:T(2,128)S(1)}, u32[]{:S(2)}, u32[]{:S(2)}) collective-permute-start(f32[8,16,2,128]{3,2,1,0:T(2,128)} %get-tuple-element.53), channel_id=1, source_target_pairs={{1,0},{2,1},{3,2},{4,3},{5,4},{6,5},{7,6},{9,8},{10,9},{11,10},{12... | collective-permute-start | bytes 393224 | tf_op jit(solution)/shard_map/ppermute | solution.py:593
  28.8 11.4 %collective-permute-start.6 = (f32[8,16,2,128]{3,2,1,0:T(2,128)}, f32[8,16,2,128]{3,2,1,0:T(2,128)S(1)}, u32[]{:S(2)}, u32[]{:S(2)}) collective-permute-start(f32[8,16,2,128]{3,2,1,0:T(2,128)} %get-tuple-element.54), channel_id=1, source_target_pairs={{0,1},{1,2},{2,3},{3,4},{4,5},{5,6},{6,7},{8,9},{9,10},{10,11},{11... | collective-permute-start | bytes 393224 | tf_op jit(solution)/shard_map/ppermute | solution.py:593
  32.5 5.5 %copy-start.17 = (f32[64,128]{1,0:T(8,128)}, f32[64,128]{1,0:T(8,128)S(1)}, u32[]{:S(2)}) copy-start(f32[64,128]{1,0:T(8,128)S(1)} %collective-permute-done.2.from_south.edge_s) | copy-start | bytes 98308
  32.5 5.4 %collective-permute-start.3 = (f32[64,128]{1,0:T(8,128)}, f32[64,128]{1,0:T(8,128)S(1)}, u32[]{:S(2)}, u32[]{:S(2)}) collective-permute-start(f32[64,128]{1,0:T(8,128)} %get-tuple-element.38), channel_id=1, source_target_pairs={{1,0},{2,1},{3,2},{4,3},{5,4},{6,5},{7,6},{9,8},{10,9},{11,10},{12... | collective-permute-start | bytes 98312 | tf_op jit(solution)/shard_map/ppermute | solution.py:593
  40.2 1.9 %copy-start.21 = (f32[8,16,2,128]{3,2,1,0:T(2,128)}, f32[8,16,2,128]{3,2,1,0:T(2,128)S(1)}, u32[]{:S(2)}) copy-start(f32[8,16,2,128]{3,2,1,0:T(2,128)S(1)} %collective-permute-done.7.halo_n) | copy-start | bytes 393220
  40.2 1.9 %copy-start.23 = (f32[8,16,2,128]{3,2,1,0:T(2,128)}, f32[8,16,2,128]{3,2,1,0:T(2,128)S(1)}, u32[]{:S(2)}) copy-start(f32[8,16,2,128]{3,2,1,0:T(2,128)S(1)} %collective-permute-done.6.halo_s) | copy-start | bytes 393220
  40.2 1.9 %copy-start.11 = (f32[8,2,32,128]{3,2,1,0:T(8,128)}, f32[8,2,32,128]{3,2,1,0:T(8,128)S(1)}, u32[]{:S(2)}) copy-start(f32[8,2,32,128]{3,2,1,0:T(8,128)S(1)} %collective-permute-done.4.halo_w) | copy-start | bytes 786436
  42.1 26.4 %all-to-all-start = ((f32[128,9,1,128]{3,2,1,0:T(1,128)}), f32[128,9,1,128]{3,2,1,0:T(1,128)S(1)}, u32[]{:S(2)}, u32[]{:S(2)}) async-start(f32[128,9,1,128]{3,2,1,0:T(1,128)} %broadcast_in_dim.2), calls=%async_computation | async-start | bytes 1179648 | tf_op jit(solution)/shard_map/all_to_all | solution.py:638
  56.8 1.0 copy-start.12
  57.7 0.8 copy-start.14
  58.5 0.8 copy-start.15
  59.2 0.8 copy-start.16
  60.0 0.8 copy-start.18
  60.7 0.8 copy-start.20
  61.5 0.9 copy-start.22
  62.4 0.9 copy-start.24
  63.3 5.1 %copy-start.5 = (bf16[4,256,256]{2,1,0:T(8,128)(2,1)S(1)}, bf16[4,256,256]{2,1,0:T(8,128)(2,1)}, u32[]{:S(2)}) copy-start(bf16[4,256,256]{2,1,0:T(8,128)(2,1)} %get-tuple-element.48.select_far) | copy-start | bytes 1572868
  67.1 1.4 %copy-start.1 = (f32[8,16,32,128]{3,2,1,0:T(8,128)}, f32[8,16,32,128]{3,2,1,0:T(8,128)S(1)}, u32[]{:S(2)}) copy-start(f32[8,16,32,128]{3,2,1,0:T(8,128)S(1)} %forecast.1) | copy-start | bytes 6291460
  68.4 1.6 %copy-start.2 = (f32[8,16,32,128]{3,2,1,0:T(8,128)S(1)}, f32[8,16,32,128]{3,2,1,0:T(8,128)}, u32[]{:S(2)}) copy-start(f32[8,16,32,128]{3,2,1,0:T(8,128)} %copy-done.1) | copy-start | bytes 6291460
  70.0 1.6 %copy-start.3 = (bf16[1024,1024]{1,0:T(8,128)(2,1)S(1)}, bf16[1024,1024]{1,0:T(8,128)(2,1)}, u32[]{:S(2)}) copy-start(bf16[1024,1024]{1,0:T(8,128)(2,1)} %get-tuple-element.44.perm_far) | copy-start | bytes 6291460
  71.6 1.4 %copy-start.4 = (f32[1536,256]{1,0:T(8,128)S(1)}, f32[1536,256]{1,0:T(8,128)}, u32[]{:S(2)}) copy-start(f32[1536,256]{1,0:T(8,128)} %get-tuple-element.47.weight_far) | copy-start | bytes 4718596
  73.0 1.0 %copy-start.6 = (f32[1024,128]{1,0:T(8,128)S(1)}, f32[1024,128]{1,0:T(8,128)}, u32[]{:S(2)}) copy-start(f32[1024,128]{1,0:T(8,128)} %get-tuple-element.46.place_far) | copy-start | bytes 1572868
  74.1 0.9 copy-start.13
  75.0 0.8 copy-start.25
  (5 other events, 3.1 us)

commit v5 on v4

--- a/solution.py
+++ b/solution.py
@@ -546,7 +546,7 @@
         ]
         + [pltpu.VMEM(array.shape, array.dtype) for array in far]
         + [pltpu.SemaphoreType.DMA((len(far),))],
-        compiler_params=pltpu.CompilerParams(vmem_limit_bytes=40 << 20),
+        compiler_params=pltpu.CompilerParams(vmem_limit_bytes=62 << 20),
         name="analyse",
     )(pos, counts, arrived, slots, *far)
 
@@ -630,9 +630,7 @@
         name="priors",
     )(pos, code, own, own_coef, from_west, from_east, from_south, from_north, held)
 
-    bundle, table, halo_w, halo_e, halo_s, halo_n = lax.optimization_barrier(
-        (bundle, table, halo_w, halo_e, halo_s, halo_n)
-    )
+    bundle, table = lax.optimization_barrier((bundle, table))
     perm, obs_weight, select, slots, source, place, counts = plan(pos, table)
     bundle = jnp.broadcast_to(bundle.reshape(1, 9, 1, members), (128, 9, 1, members))
     arrived = lax.all_to_all(bundle, ("gx", "gy"), 0, 0, tiled=True)
@@ -648,7 +646,7 @@
             pltpu.VMEM((2, CX + 4, CY + 16, MEM), F32),
             pltpu.SemaphoreType.DMA((4,)),
         ],
-        compiler_params=pltpu.CompilerParams(vmem_limit_bytes=32 << 20),
+        compiler_params=pltpu.CompilerParams(vmem_limit_bytes=62 << 20),
         name="forecast",
     )(cells, *speeds, halo_w, halo_e, halo_s, halo_n, from_west, from_east, from_south, from_north)
     state = state.reshape(-1, members)

time: 100 us -> 90.2 us (0.902)
  local copies, waits for them, and re-layouts: 22.4 us -> 8.46 us
  Pallas kernels: 36.4 us -> 40.6 us
  waiting for transfers between devices: 1.73 us -> 3.73 us
  other arithmetic: 4.69 us -> 3.32 us
    unnamed x56 -> x28, local copies, waits for them, and re-layouts: 17.7 us -> 3.61 us
    pallas_call x1, Pallas kernels: 3.75 us -> 6.78 us  [shards(): pl.pallas_call(forecast_kernel, out_shape=jax.ShapeDtypeStruct(cells.shap...]
    ppermute x4, waiting for transfers between devices: 0.17 us -> 2.17 us  [along_y(): lax.ppermute(value, 'gy', [(i, i + step) for i in range(8) if 0 <= i + st...]
    another operation x2, local copies, waits for them, and re-layouts: 2.02 us -> 0.67 us  [shards(): jnp.stack([obs_column[:, 0], obs_column[:, 1], obs_comp // per_level, obs...]
    pallas_call x1, Pallas kernels: 21.5 us -> 22.7 us  [analyse(): pl.pallas_call(analysis_kernel, out_shape=jax.ShapeDtypeStruct(far[-1].sh...]
    slice x1, local copies, waits for them, and re-layouts: 0.04 us -> 1.07 us  [shards(): halo_e = along_x(late[:, :2], -1)]
  transfers between devices with their start and end apart: 9 -> 9, of which waited for: 2 -> 2; matrix products, arithmetic and copies ran while one was open for 4% -> 4% of each run, Pallas kernels for 11% -> 13%
where the time goes in v5:
time: 90.2 us; the launch traced here: 89.5 us
  Pallas kernels  40.6 us (45%)
  starting transfers between devices  33 us (37%)
  local copies, waits for them, and re-layouts  8.46 us (9%)
  waiting for transfers between devices  3.73 us (4%)
  other arithmetic  3.32 us (4%)
    pallas_call x1, Pallas kernels, analyse(): pl.pallas_call(analysis_kernel, out_shape=jax.ShapeDtypeStruct(far[-1].sh...  22.7 us
    ppermute x4, starting transfers between devices, along_y(): lax.ppermute(value, 'gy', [(i, i + step) for i in range(8) if 0 <= i + st...  13 us
    ppermute x4, starting transfers between devices, along_x(): return lax.ppermute(value, 'gx', [(i, (i + step) % 16) for i in range(16)])  10.7 us
    all_to_all x1, starting transfers between devices, shards(): arrived = lax.all_to_all(bundle, ('gx', 'gy'), 0, 0, tiled=True)  9.35 us
    pallas_call x1, Pallas kernels, shards(): pl.pallas_call(forecast_kernel, out_shape=jax.ShapeDtypeStruct(cells.shap...  6.78 us
    pallas_call x1, Pallas kernels, plan(): pl.pallas_call(plan_kernel, out_shape=shapes, in_specs=[smem(), vmem()],...  5.14 us
    unnamed x28, local copies, waits for them, and re-layouts  3.61 us
    pallas_call x1, Pallas kernels, shards(): pl.pallas_call(edge_kernel, out_shape=(rows(104), rows(72), rows(80), row...  2.78 us
  transfers between devices with their start and end apart: 9, of which 2 were waited for; matrix products, arithmetic and copies ran while one was open for 4% of the time, Pallas kernels for 13%

profile of v5, /device:TPU:1, one launch (start us, length us, event | category | flops | bytes accessed | tf_op | source)
XLA Modules:
  0.0 89.5 jit_solution(12885263156814786325)
XLA Ops:
  0.0 0.8 slice_bitcast_fusion
  0.8 0.6 pad_add_fusion.pos
  1.4 1.3 %add_select_fusion = (s32[1024]{0:T(1024)S(1)}, s32[1024]{0:T(1024)}) fusion(s32[1024]{0:T(1024)} %param.16, s32[1024]{0:T(1024)S(1)} %bitcast.30), kind=kLoop, calls=%fused_computation | loop fusion | flops 17408 | bytes 16384 | tf_op jit(solution)/shard_map/jit(floor_divide)/jit(_where)/select_n | solution.py:577
  2.7 2.8 %edges.1 = (f32[104,128]{1,0:T(8,128)}, f32[72,128]{1,0:T(8,128)}, f32[80,128]{1,0:T(8,128)}, f32[80,128]{1,0:T(8,128)}, f32[48,128]{1,0:T(8,128)}, /*index=5*/f32[48,128]{1,0:T(8,128)}) custom-call(s32[2]{0:T(128)} %pad_add_fusion.pos, s32[1024]{0:T(1024)} %get-tuple-element.53.code, f32[4096,128]{1,0:T(8,128)} %bitcast.20, f32[64,32]{1,0:T(8,128)} %bitcast.23, ...), custom_call_target="tpu_custom_call" | custom-call | tf_op jit(solution)/shard_map/edges/pallas_call | solution.py:599
  5.5 2.0 %collective-permute-start = (f32[80,128]{1,0:T(8,128)}, f32[80,128]{1,0:T(8,128)S(1)}, u32[]{:S(2)}, u32[]{:S(2)}) collective-permute-start(f32[80,128]{1,0:T(8,128)} %get-tuple-element.27), channel_id=1, source_target_pairs={{0,8},{8,16},{16,24},{24,32},{32,40},{40,48},{48,56},{56,64},{64,7... | collective-permute-start | bytes 122888 | tf_op jit(solution)/shard_map/ppermute | solution.py:590
  7.5 3.8 %collective-permute-start.1 = (f32[80,128]{1,0:T(8,128)}, f32[80,128]{1,0:T(8,128)S(1)}, u32[]{:S(2)}, u32[]{:S(2)}) collective-permute-start(f32[80,128]{1,0:T(8,128)} %get-tuple-element.28), channel_id=1, source_target_pairs={{0,120},{8,0},{16,8},{24,16},{32,24},{40,32},{48,40},{56,48},{64,5... | collective-permute-start | bytes 122888 | tf_op jit(solution)/shard_map/ppermute | solution.py:590
  11.3 1.6 %collective-permute-done.from_west.edge_w = f32[80,128]{1,0:T(8,128)S(1)} collective-permute-done((f32[80,128]{1,0:T(8,128)}, f32[80,128]{1,0:T(8,128)S(1)}, u32[]{:S(2)}, u32[]{:S(2)}) %collective-permute-start) | collective-permute-done | bytes 40992 | tf_op jit(solution)/shard_map/ppermute | solution.py:590
  12.9 0.6 copy-done.1
  13.5 0.0 copy-done.2
  13.5 1.5 %corners.1 = (f32[64,128]{1,0:T(8,128)}, f32[64,128]{1,0:T(8,128)}) custom-call(s32[2]{0:T(128)} %pad_add_fusion.pos, s32[1024]{0:T(1024)} %get-tuple-element.53.code, f32[48,128]{1,0:T(8,128)} %get-tuple-element.31.base_north, f32[48,128]{1,0:T(8,128)} %get-tuple-element.32.base_south, f32[80,128]{1,0:T(8,128)} %copy-done.1, f32[80,128]{1,0:T(8,128)} %copy-done.2), custom_call_target="tpu_custom_call" | custom-call | tf_op jit(solution)/shard_map/corners/pallas_call | solution.py:613
  15.0 5.1 %collective-permute-start.2 = (f32[64,128]{1,0:T(8,128)}, f32[64,128]{1,0:T(8,128)S(1)}, u32[]{:S(2)}, u32[]{:S(2)}) collective-permute-start(f32[64,128]{1,0:T(8,128)} %get-tuple-element.33), channel_id=1, source_target_pairs={{0,1},{1,2},{2,3},{3,4},{4,5},{5,6},{6,7},{8,9},{9,10},{10,11},{11... | collective-permute-start | bytes 98312 | tf_op jit(solution)/shard_map/ppermute | solution.py:593
  20.1 1.9 %collective-permute-start.3 = (f32[64,128]{1,0:T(8,128)}, f32[64,128]{1,0:T(8,128)S(1)}, u32[]{:S(2)}, u32[]{:S(2)}) collective-permute-start(f32[64,128]{1,0:T(8,128)} %get-tuple-element.34), channel_id=1, source_target_pairs={{1,0},{2,1},{3,2},{4,3},{5,4},{6,5},{7,6},{9,8},{10,9},{11,10},{12... | collective-permute-start | bytes 98312 | tf_op jit(solution)/shard_map/ppermute | solution.py:593
  22.1 0.6 fusion.2.held
  22.7 0.7 stack.35.table
  23.4 2.2 %collective-permute-done.3.from_north.edge_n = f32[64,128]{1,0:T(8,128)S(1)} collective-permute-done((f32[64,128]{1,0:T(8,128)}, f32[64,128]{1,0:T(8,128)S(1)}, u32[]{:S(2)}, u32[]{:S(2)}) %collective-permute-start.3) | collective-permute-done | bytes 32800 | tf_op jit(solution)/shard_map/ppermute | solution.py:593
  25.6 0.6 copy-done.6
  26.2 1.6 %priors.1 = f32[9,128]{1,0:T(8,128)} custom-call(s32[2]{0:T(128)} %pad_add_fusion.pos, s32[1024]{0:T(1024)} %get-tuple-element.53.code, f32[104,128]{1,0:T(8,128)} %get-tuple-element.25.own, f32[72,128]{1,0:T(8,128)} %get-tuple-element.26.own_coef, f32[80,128]{1,0:T(8,128)} %copy-done.1, f32[80,128]{1,0:T(8,128)} %copy-done.2, f32[64,128]{1,0:T(8,128)} %copy-done.5, ...), custom_call_target="tpu_custom_call" | custom-call | tf_op jit(solution)/shard_map/priors/pallas_call | solution.py:624
  27.8 1.8 %broadcast_in_dim.2 = f32[128,9,1,128]{3,2,1,0:T(1,128)} broadcast(f32[9,128]{1,0:T(8,128)} %priors.1), dimensions={1,3} | broadcast | bytes 594432 | tf_op jit(solution)/shard_map/broadcast_in_dim | solution.py:635
  29.6 9.4 %all-to-all-start = ((f32[128,9,1,128]{3,2,1,0:T(1,128)}), f32[128,9,1,128]{3,2,1,0:T(1,128)S(1)}, u32[]{:S(2)}, u32[]{:S(2)}) async-start(f32[128,9,1,128]{3,2,1,0:T(1,128)} %broadcast_in_dim.2), calls=%async_computation | async-start | bytes 1179648 | tf_op jit(solution)/shard_map/all_to_all | solution.py:636
  39.0 1.1 %fusion.4 = (f32[8,2,32,128]{3,2,1,0:T(8,128)S(1)}, f32[8,2,32,128]{3,2,1,0:T(8,128)S(1)}) fusion(f32[8,16,32,128]{3,2,1,0:T(8,128)} %cells.1), kind=kLoop, calls=%fused_computation.16 | loop fusion | bytes 1048576 | tf_op jit(solution)/shard_map/slice | solution.py:610
  40.1 4.9 %collective-permute-start.5 = (f32[8,2,32,128]{3,2,1,0:T(8,128)S(1)}, f32[8,2,32,128]{3,2,1,0:T(8,128)S(1)}, u32[]{:S(2)}, u32[]{:S(2)}) collective-permute-start(f32[8,2,32,128]{3,2,1,0:T(8,128)S(1)} %get-tuple-element.47), channel_id=1, source_target_pairs={{0,120},{8,0},{16,8},{24,16},{32,24},{40,32},{48,40},{56,48},{64,5... | collective-permute-start | bytes 786440 | tf_op jit(solution)/shard_map/ppermute | solution.py:590
  45.0 1.3 %fusion.3 = (f32[8,16,2,128]{3,2,1,0:T(2,128)S(1)}, f32[8,16,2,128]{3,2,1,0:T(2,128)S(1)}) fusion(f32[8,16,32,128]{3,2,1,0:T(8,128)} %cells.1), kind=kLoop, calls=%fused_computation.15 | loop fusion | bytes 524288 | tf_op jit(solution)/shard_map/slice | solution.py:612
  46.3 2.5 %collective-permute-start.7 = (f32[8,16,2,128]{3,2,1,0:T(2,128)S(1)}, f32[8,16,2,128]{3,2,1,0:T(2,128)S(1)}, u32[]{:S(2)}, u32[]{:S(2)}) collective-permute-start(f32[8,16,2,128]{3,2,1,0:T(2,128)S(1)} %get-tuple-element.45), channel_id=1, source_target_pairs={{1,0},{2,1},{3,2},{4,3},{5,4},{6,5},{7,6},{9,8},{10,9},{11,10},{12... | collective-permute-start | bytes 393224 | tf_op jit(solution)/shard_map/ppermute | solution.py:593
  48.8 3.4 %collective-permute-start.6 = (f32[8,16,2,128]{3,2,1,0:T(2,128)S(1)}, f32[8,16,2,128]{3,2,1,0:T(2,128)S(1)}, u32[]{:S(2)}, u32[]{:S(2)}) collective-permute-start(f32[8,16,2,128]{3,2,1,0:T(2,128)S(1)} %get-tuple-element.46), channel_id=1, source_target_pairs={{0,1},{1,2},{2,3},{3,4},{4,5},{5,6},{6,7},{8,9},{9,10},{10,11},{11... | collective-permute-start | bytes 393224 | tf_op jit(solution)/shard_map/ppermute | solution.py:593
  52.3 5.1 %plan.1 = (bf16[1024,1024]{1,0:T(8,128)(2,1)}, f32[1536,256]{1,0:T(8,128)}, bf16[4,256,256]{2,1,0:T(8,128)(2,1)}, f32[4,8,256]{2,1,0:T(8,128)}, bf16[1024,128]{1...) custom-call(s32[2]{0:T(128)} %pad_add_fusion.pos, s32[8,1024]{1,0:T(8,128)} %stack.35.table), custom_call_target="tpu_custom_call" | custom-call | tf_op jit(solution)/shard_map/plan/pallas_call | solution.py:526
  57.5 0.6 copy-done.7
  58.1 0.1 copy-done.8
  58.2 0.1 copy-done.3
  58.3 0.7 copy-done.4
  59.0 6.8 %forecast.1 = f32[8,16,32,128]{3,2,1,0:T(8,128)} custom-call(f32[8,16,32,128]{3,2,1,0:T(8,128)} %cells.1, f32[64,32]{1,0:T(8,128)} %bitcast.24, f32[64,32]{1,0:T(8,128)} %bitcast.26, f32[64,32]{1,0:T(8,128)} %bitcast.28, f32[8,2,32,128]{3,2,1,0:T(8,128)} %copy-done.4, f32[8,2,32,128]{3,2,1,0:T(8,128)} %copy-done.3, f32[8,16,2,128]{3,2,1,0:T(2,128)} %copy-done.8, ...), custom_call_target="tpu_custom_call" | custom-call | tf_op jit(solution)/shard_map/forecast/pallas_call | solution.py:638
  65.8 0.8 copy-done
  66.6 22.7 %analyse.1 = f32[4096,128]{1,0:T(8,128)} custom-call(s32[2]{0:T(128)} %pad_add_fusion.pos, s32[4]{0:T(128)} %get-tuple-element.36.counts, f32[1152,128]{1,0:T(8,128)} %bitcast.22, f32[4,8,256]{2,1,0:T(8,128)} %get-tuple-element.38.slots, bf16[1024,1024]{1,0:T(8,128)(2,1)} %get-tuple-element.39.perm_far, bf16[1024,128]{1,0:T(8,128)(2,1)} %get-tuple-element.40.source_far, ...), custom_call_target="tpu_custom_call" | custom-call | tf_op jit(solution)/shard_map/analyse/pallas_call | solution.py:536
  (29 shorter events, 0.1 us)
Async XLA Ops:
  0.0 22.1 %copy-start.12 = (f32[1,1,32]{2,1,0:T(1,128)S(1)}, f32[1,1,32]{2,1,0:T(1,128)}, u32[]{:S(2)}) copy-start(f32[1,1,32]{2,1,0:T(1,128)} %param.21) | copy-start | bytes 388
  0.0 22.1 %copy-start.13 = (f32[1,1,32]{2,1,0:T(1,128)S(1)}, f32[1,1,32]{2,1,0:T(1,128)}, u32[]{:S(2)}) copy-start(f32[1,1,32]{2,1,0:T(1,128)} %param.20) | copy-start | bytes 388
  0.0 22.7 %copy-start.11 = (s32[1024]{0:T(1024)S(1)}, s32[1024]{0:T(1024)}, u32[]{:S(2)}) copy-start(s32[1024]{0:T(1024)} %param.19) | copy-start | bytes 12292
  0.0 22.7 %copy-start.10 = (s32[1024]{0:T(1024)S(1)}, s32[1024]{0:T(1024)}, u32[]{:S(2)}) copy-start(s32[1024]{0:T(1024)} %param.18) | copy-start | bytes 12292
  0.0 22.7 %copy-start.9 = (s32[1024]{0:T(1024)S(1)}, s32[1024]{0:T(1024)}, u32[]{:S(2)}) copy-start(s32[1024]{0:T(1024)} %param.17) | copy-start | bytes 12292
  5.5 7.4 %collective-permute-start = (f32[80,128]{1,0:T(8,128)}, f32[80,128]{1,0:T(8,128)S(1)}, u32[]{:S(2)}, u32[]{:S(2)}) collective-permute-start(f32[80,128]{1,0:T(8,128)} %get-tuple-element.27), channel_id=1, source_target_pairs={{0,8},{8,16},{16,24},{24,32},{32,40},{40,48},{48,56},{56,64},{64,7... | collective-permute-start | bytes 122888 | tf_op jit(solution)/shard_map/ppermute | solution.py:590
  7.5 5.3 %collective-permute-start.1 = (f32[80,128]{1,0:T(8,128)}, f32[80,128]{1,0:T(8,128)S(1)}, u32[]{:S(2)}, u32[]{:S(2)}) collective-permute-start(f32[80,128]{1,0:T(8,128)} %get-tuple-element.28), channel_id=1, source_target_pairs={{0,120},{8,0},{16,8},{24,16},{32,24},{40,32},{48,40},{56,48},{64,5... | collective-permute-start | bytes 122888 | tf_op jit(solution)/shard_map/ppermute | solution.py:590
  12.9 0.6 copy-start.1
  12.9 0.6 copy-start.2
  15.0 8.4 %collective-permute-start.2 = (f32[64,128]{1,0:T(8,128)}, f32[64,128]{1,0:T(8,128)S(1)}, u32[]{:S(2)}, u32[]{:S(2)}) collective-permute-start(f32[64,128]{1,0:T(8,128)} %get-tuple-element.33), channel_id=1, source_target_pairs={{0,1},{1,2},{2,3},{3,4},{4,5},{5,6},{6,7},{8,9},{9,10},{10,11},{11... | collective-permute-start | bytes 98312 | tf_op jit(solution)/shard_map/ppermute | solution.py:593
  20.1 5.4 %collective-permute-start.3 = (f32[64,128]{1,0:T(8,128)}, f32[64,128]{1,0:T(8,128)S(1)}, u32[]{:S(2)}, u32[]{:S(2)}) collective-permute-start(f32[64,128]{1,0:T(8,128)} %get-tuple-element.34), channel_id=1, source_target_pairs={{1,0},{2,1},{3,2},{4,3},{5,4},{6,5},{7,6},{9,8},{10,9},{11,10},{12... | collective-permute-start | bytes 98312 | tf_op jit(solution)/shard_map/ppermute | solution.py:593
  23.4 2.2 %copy-start.5 = (f32[64,128]{1,0:T(8,128)}, f32[64,128]{1,0:T(8,128)S(1)}, u32[]{:S(2)}) copy-start(f32[64,128]{1,0:T(8,128)S(1)} %collective-permute-done.2.from_south.edge_s) | copy-start | bytes 98308
  25.6 0.6 copy-start.6
  29.6 36.1 %all-to-all-start = ((f32[128,9,1,128]{3,2,1,0:T(1,128)}), f32[128,9,1,128]{3,2,1,0:T(1,128)S(1)}, u32[]{:S(2)}, u32[]{:S(2)}) async-start(f32[128,9,1,128]{3,2,1,0:T(1,128)} %broadcast_in_dim.2), calls=%async_computation | async-start | bytes 1179648 | tf_op jit(solution)/shard_map/all_to_all | solution.py:636
  40.1 17.4 %collective-permute-start.5 = (f32[8,2,32,128]{3,2,1,0:T(8,128)S(1)}, f32[8,2,32,128]{3,2,1,0:T(8,128)S(1)}, u32[]{:S(2)}, u32[]{:S(2)}) collective-permute-start(f32[8,2,32,128]{3,2,1,0:T(8,128)S(1)} %get-tuple-element.47), channel_id=1, source_target_pairs={{0,120},{8,0},{16,8},{24,16},{32,24},{40,32},{48,40},{56,48},{64,5... | collective-permute-start | bytes 786440 | tf_op jit(solution)/shard_map/ppermute | solution.py:590
  45.0 12.5 %collective-permute-start.4 = (f32[8,2,32,128]{3,2,1,0:T(8,128)S(1)}, f32[8,2,32,128]{3,2,1,0:T(8,128)S(1)}, u32[]{:S(2)}, u32[]{:S(2)}) collective-permute-start(f32[8,2,32,128]{3,2,1,0:T(8,128)S(1)} %get-tuple-element.48), channel_id=1, source_target_pairs={{0,8},{8,16},{16,24},{24,32},{32,40},{40,48},{48,56},{56,64},{64,7... | collective-permute-start | bytes 786440 | tf_op jit(solution)/shard_map/ppermute | solution.py:590
  46.3 11.2 %collective-permute-start.7 = (f32[8,16,2,128]{3,2,1,0:T(2,128)S(1)}, f32[8,16,2,128]{3,2,1,0:T(2,128)S(1)}, u32[]{:S(2)}, u32[]{:S(2)}) collective-permute-start(f32[8,16,2,128]{3,2,1,0:T(2,128)S(1)} %get-tuple-element.45), channel_id=1, source_target_pairs={{1,0},{2,1},{3,2},{4,3},{5,4},{6,5},{7,6},{9,8},{10,9},{11,10},{12... | collective-permute-start | bytes 393224 | tf_op jit(solution)/shard_map/ppermute | solution.py:593
  48.8 8.6 %collective-permute-start.6 = (f32[8,16,2,128]{3,2,1,0:T(2,128)S(1)}, f32[8,16,2,128]{3,2,1,0:T(2,128)S(1)}, u32[]{:S(2)}, u32[]{:S(2)}) collective-permute-start(f32[8,16,2,128]{3,2,1,0:T(2,128)S(1)} %get-tuple-element.46), channel_id=1, source_target_pairs={{0,1},{1,2},{2,3},{3,4},{4,5},{5,6},{6,7},{8,9},{9,10},{10,11},{11... | collective-permute-start | bytes 393224 | tf_op jit(solution)/shard_map/ppermute | solution.py:593
  57.4 0.7 copy-start.7
  57.5 0.7 copy-start.8
  57.5 0.8 copy-start.3
  58.3 0.7 copy-start.4
  65.8 0.8 copy-start
